TPU v7x, 32 devices: a whole 2x2x4 slice. The times are simulated.
32 devices in a mesh: dp: 8 (over z, y), tensor: 4 (over x, core).
Axes of the slice: x: 2, y: 2, z: 4, core: 2. Of those that a mesh axis runs over, the one named last changes fastest.
Arguments:
- inputs: bfloat16 [8192, 2048], P(('dp', 'tensor')), may hold values from -6 to 6
- cotangent: bfloat16 [8192, 2048], P(('dp', 'tensor')), may hold values from -6 to 6
- segment_ids: int32 [8, 1024], P('dp'), may hold values from 0 to 12, never falling along the last dimension, each value on 1 to 256 neighbouring positions
- parent_links: int32 [8, 13], P('dp'), may hold values from 0 to 11, as said below
- adapter_choice: int32 [8], P('dp'), may hold values from 0 to 7
- gain_one: float32 [2048], replicated, may hold values from 0.25 to 1.75
- shift_one: float32 [2048], replicated, may hold values from -1.75 to 1.75
- gain_two: float32 [2048], replicated, may hold values from 0.25 to 1.75
- shift_two: float32 [2048], replicated, may hold values from -1.75 to 1.75
- query_weight: bfloat16 [2048, 2048], P('dp', 'tensor'), may hold values from -0.125 to 0.125
- key_weight: bfloat16 [2048, 2048], P('dp', 'tensor'), may hold values from -0.125 to 0.125
- value_weight: bfloat16 [2048, 2048], P('dp', 'tensor'), may hold values from -0.125 to 0.125
- output_weight: bfloat16 [2048, 2048], P('tensor', 'dp'), may hold values from -0.5 to 0.5
- expand_weight: bfloat16 [2048, 8192], P('dp', 'tensor'), may hold values from -0.125 to 0.125
- shrink_weight: bfloat16 [8192, 2048], P('tensor', 'dp'), may hold values from -0.0625 to 0.0625
- query_bias: float32 [2048], P('tensor'), may hold values from -1.75 to 1.75
- value_bias: float32 [2048], P('tensor'), may hold values from -1.75 to 1.75
- output_bias: float32 [2048], replicated, may hold values from -1.75 to 1.75
- expand_bias: float32 [8192], P('tensor'), may hold values from -1.75 to 1.75
- shrink_bias: float32 [2048], replicated, may hold values from -1.75 to 1.75
- query_down: bfloat16 [8, 16, 2048], replicated, may hold values from -0.125 to 0.125
- query_up: bfloat16 [8, 16, 2048], P(None, None, 'tensor'), may hold values from -0.5 to 0.5
- key_down: bfloat16 [8, 16, 2048], replicated, may hold values from -0.125 to 0.125
- key_up: bfloat16 [8, 16, 2048], P(None, None, 'tensor'), may hold values from -0.5 to 0.5
- value_down: bfloat16 [8, 16, 2048], replicated, may hold values from -0.125 to 0.125
- value_up: bfloat16 [8, 16, 2048], P(None, None, 'tensor'), may hold values from -0.5 to 0.5
- output_down: bfloat16 [8, 16, 2048], P(None, None, 'tensor'), may hold values from -0.5 to 0.5
- output_up: bfloat16 [8, 16, 2048], replicated, may hold values from -0.5 to 0.5
- expand_down: bfloat16 [8, 16, 2048], replicated, may hold values from -0.125 to 0.125
- expand_up: bfloat16 [8, 16, 8192], P(None, None, 'tensor'), may hold values from -0.5 to 0.5
- shrink_down: bfloat16 [8, 16, 8192], P(None, None, 'tensor'), may hold values from -0.125 to 0.125
- shrink_up: bfloat16 [8, 16, 2048], replicated, may hold values from -0.5 to 0.5
Outputs:
- output: bfloat16 [8192, 2048], P(('dp', 'tensor'))
- input_delta: bfloat16 [8192, 2048], P(('dp', 'tensor'))
- query_down_delta: float32 [8, 16, 2048], replicated
- query_up_delta: float32 [8, 16, 2048], P(None, None, 'tensor')
- key_down_delta: float32 [8, 16, 2048], replicated
- key_up_delta: float32 [8, 16, 2048], P(None, None, 'tensor')
- value_down_delta: float32 [8, 16, 2048], replicated
- value_up_delta: float32 [8, 16, 2048], P(None, None, 'tensor')
- output_down_delta: float32 [8, 16, 2048], P(None, None, 'tensor')
- output_up_delta: float32 [8, 16, 2048], replicated
- expand_down_delta: float32 [8, 16, 2048], replicated
- expand_up_delta: float32 [8, 16, 8192], P(None, None, 'tensor')
- shrink_down_delta: float32 [8, 16, 8192], P(None, None, 'tensor')
- shrink_up_delta: float32 [8, 16, 2048], replicated
Inputs may be any that keep to these rules, and one draw needn't show every extreme that they name: `segment_ids`: within a tree the ids never fall, all 13 segments occur, and each holds 1 to a quarter of 1024 tokens. `parent_links`: entry 0 is 0; entry s above 0 names an earlier segment, so that the segments of a tree form a tree rooted at segment 0; the last segment's parent is the segment before it.
All inputs are finite; a program needn't handle non-finite values.
Results may differ from a plain program's by a relative error of at most 0.015.
Values may be sent and summed in bfloat16 or wider, within the bound.
No kernel may reach another device: no remote copies, remote signals or barrier semaphores. Data moves between devices by JAX's collectives and lax.ppermute only.
A program may use at most 192 MiB of HBM per device.

v0:
```python
import jax
import jax.numpy as jnp
from jax import lax
from jax.sharding import PartitionSpec as P

HEAD_DIM = 128
SEGS = 13


def layer_norm(values, gain_vec, shift_vec):
    row_mean = jnp.mean(values, axis=-1, keepdims=True)
    centred = values - row_mean
    row_var = jnp.mean(centred * centred, axis=-1, keepdims=True)
    return centred * lax.rsqrt(row_var + 1e-05) * gain_vec + shift_vec


def ancestry(parents):
    seg_range = jnp.arange(SEGS, dtype=jnp.int32)
    current = seg_range
    ancestors = current[:, None] == seg_range[None, :]
    for hop_index in range(SEGS - 1):
        current = jnp.sum(
            jnp.where(current[:, None] == seg_range[None, :], parents[None, :], 0), axis=1
        )
        ancestors = jnp.logical_or(ancestors, current[:, None] == seg_range[None, :])
    return ancestors


def product(left, right):
    return jnp.dot(left, right, preferred_element_type=jnp.float32)


def product_cols(left, right):
    return lax.dot_general(
        left, right, (((1,), (1,)), ((), ())), preferred_element_type=jnp.float32
    )


def product_rows(left, right):
    return lax.dot_general(
        left, right, (((0,), (0,)), ((), ())), preferred_element_type=jnp.float32
    )


def shards(
    inputs,
    cotangent,
    segment_ids,
    parent_links,
    adapter_choice,
    gain_one,
    shift_one,
    gain_two,
    shift_two,
    query_weight,
    key_weight,
    value_weight,
    output_weight,
    expand_weight,
    shrink_weight,
    query_bias,
    value_bias,
    output_bias,
    expand_bias,
    shrink_bias,
    query_down,
    query_up,
    key_down,
    key_up,
    value_down,
    value_up,
    output_down,
    output_up,
    expand_down,
    expand_up,
    shrink_down,
    shrink_up,
):
    slot_count = query_down.shape[0]
    rank_width = query_down.shape[1]
    select = (jnp.arange(slot_count, dtype=jnp.int32) == adapter_choice[0]).astype(jnp.bfloat16)
    select_wide = select.astype(jnp.float32)

    def adapter_of(adapter_table):
        return jnp.einsum(
            "a,ard->rd", select, adapter_table, preferred_element_type=jnp.float32
        ).astype(jnp.bfloat16)

    def spread(delta):
        return select_wide[:, None, None] * delta[None]

    down_qkv = jnp.concatenate(
        [adapter_of(query_down), adapter_of(key_down), adapter_of(value_down)], axis=0
    )
    lift_query = adapter_of(query_up)
    lift_key = adapter_of(key_up)
    lift_value = adapter_of(value_up)
    down_output = adapter_of(output_down)
    lift_output = adapter_of(output_up)
    down_expand = adapter_of(expand_down)
    lift_expand = adapter_of(expand_up)
    down_shrink = adapter_of(shrink_down)
    lift_shrink = adapter_of(shrink_up)
    query_full, key_full, value_full, output_full = (
        lax.all_gather(query_weight, "dp", axis=0, tiled=True),
        lax.all_gather(key_weight, "dp", axis=0, tiled=True),
        lax.all_gather(value_weight, "dp", axis=0, tiled=True),
        lax.all_gather(output_weight, "dp", axis=1, tiled=True),
    )
    inputs_wide = inputs.astype(jnp.float32)
    normed_one, norm_one_back = jax.vjp(
        lambda rows_in: layer_norm(rows_in, gain_one, shift_one), inputs_wide
    )
    rows_one = normed_one.astype(jnp.bfloat16)
    rank_one = product_cols(rows_one, down_qkv).astype(jnp.bfloat16)
    full_one, rank_full = (
        lax.all_gather(rows_one, "tensor", axis=0, tiled=True),
        lax.all_gather(rank_one, "tensor", axis=0, tiled=True),
    )
    seq_len = full_one.shape[0]
    width_local = query_full.shape[1]
    head_count = width_local // HEAD_DIM
    rank_query = rank_full[:, :rank_width]
    rank_key = rank_full[:, rank_width : 2 * rank_width]
    rank_value = rank_full[:, 2 * rank_width :]
    queries = (product(full_one, query_full) + product(rank_query, lift_query) + query_bias).astype(
        jnp.bfloat16
    )
    keys_low = (product(full_one, key_full) + product(rank_key, lift_key)).astype(jnp.bfloat16)
    values_low = (
        product(full_one, value_full) + product(rank_value, lift_value) + value_bias
    ).astype(jnp.bfloat16)
    seg_range = jnp.arange(SEGS, dtype=jnp.int32)
    seg_hot = (segment_ids[0][:, None] == seg_range[None, :]).astype(jnp.bfloat16)
    path_hot = product(seg_hot, ancestry(parent_links[0]).astype(jnp.bfloat16)).astype(jnp.bfloat16)
    positions = jnp.arange(seq_len, dtype=jnp.int32)
    block_rows = min(512, seq_len)
    block_count = seq_len // block_rows
    score_scale = HEAD_DIM ** (-0.5)
    query_heads = queries.reshape(seq_len, head_count, HEAD_DIM)
    key_heads = keys_low.reshape(seq_len, head_count, HEAD_DIM)
    value_heads = values_low.reshape(seq_len, head_count, HEAD_DIM)

    def block_scores(row_start, key_end):
        same_path = (
            product_cols(path_hot[row_start : row_start + block_rows], seg_hot[:key_end]) > 0.5
        )
        causal = positions[row_start : row_start + block_rows, None] >= positions[None, :key_end]
        raw_scores = (
            jnp.einsum(
                "qhd,khd->hqk",
                query_heads[row_start : row_start + block_rows],
                key_heads[:key_end],
                preferred_element_type=jnp.float32,
            )
            * score_scale
        )
        return jnp.where(jnp.logical_and(same_path, causal)[None], raw_scores, -1e30)

    attended_parts = []
    lse_parts = []
    for block_index in range(block_count):
        row_start = block_index * block_rows
        key_end = row_start + block_rows
        scores = block_scores(row_start, key_end)
        row_top = jnp.max(scores, axis=-1, keepdims=True)
        raised = jnp.exp(scores - row_top)
        row_total = jnp.sum(raised, axis=-1, keepdims=True)
        lse_parts.append(row_top + jnp.log(row_total))
        probs_low = (raised / row_total).astype(jnp.bfloat16)
        attended_parts.append(
            jnp.einsum(
                "hqk,khd->qhd", probs_low, value_heads[:key_end], preferred_element_type=jnp.float32
            )
        )
    attended = (
        jnp.concatenate(attended_parts, axis=0).reshape(seq_len, width_local).astype(jnp.bfloat16)
    )
    main_part = product(attended, output_full)
    rank_part = product_cols(attended, down_output)
    main_rows, rank_rows = (
        lax.psum_scatter(main_part, "tensor", scatter_dimension=0, tiled=True),
        lax.psum_scatter(rank_part, "tensor", scatter_dimension=0, tiled=True),
    )
    rank_out = rank_rows.astype(jnp.bfloat16)
    residual = inputs_wide + main_rows + product(rank_out, lift_output) + output_bias
    normed_two, norm_two_back = jax.vjp(
        lambda rows_in: layer_norm(rows_in, gain_two, shift_two), residual
    )
    rows_two = normed_two.astype(jnp.bfloat16)
    rank_two = product_cols(rows_two, down_expand).astype(jnp.bfloat16)
    full_two, rank_full_two = (
        lax.all_gather(rows_two, "tensor", axis=0, tiled=True),
        lax.all_gather(rank_two, "tensor", axis=0, tiled=True),
    )
    expand_full, shrink_full = (
        lax.all_gather(expand_weight, "dp", axis=0, tiled=True),
        lax.all_gather(shrink_weight, "dp", axis=1, tiled=True),
    )
    pre_act = product(full_two, expand_full) + product(rank_full_two, lift_expand) + expand_bias
    hidden, gelu_back = jax.vjp(lambda pre_in: jax.nn.gelu(pre_in, approximate=False), pre_act)
    hidden_low = hidden.astype(jnp.bfloat16)
    main_part_two = product(hidden_low, shrink_full)
    rank_part_two = product_cols(hidden_low, down_shrink)
    main_rows_two, rank_rows_two = (
        lax.psum_scatter(main_part_two, "tensor", scatter_dimension=0, tiled=True),
        lax.psum_scatter(rank_part_two, "tensor", scatter_dimension=0, tiled=True),
    )
    rank_shrink = rank_rows_two.astype(jnp.bfloat16)
    output = (residual + main_rows_two + product(rank_shrink, lift_shrink) + shrink_bias).astype(
        jnp.bfloat16
    )
    grad_out = cotangent.astype(jnp.float32)
    delta_shrink_up = product_rows(rank_shrink, cotangent)
    rank_grad = product_cols(cotangent, lift_shrink).astype(jnp.bfloat16)
    grad_full, rank_grad_full = (
        lax.all_gather(cotangent, "tensor", axis=0, tiled=True),
        lax.all_gather(rank_grad, "tensor", axis=0, tiled=True),
    )
    expand_back, shrink_back = (
        lax.all_gather(expand_weight, "dp", axis=0, tiled=True),
        lax.all_gather(shrink_weight, "dp", axis=1, tiled=True),
    )
    grad_hidden = product_cols(grad_full, shrink_back) + product(rank_grad_full, down_shrink)
    delta_shrink_down = product_rows(rank_grad_full, hidden_low)
    grad_pre = gelu_back(grad_hidden)[0].astype(jnp.bfloat16)
    delta_expand_up = product_rows(rank_full_two, grad_pre)
    grad_rows_part = product_cols(grad_pre, expand_back)
    grad_rank_part = product_cols(grad_pre, lift_expand)
    grad_norm_two, grad_rank_two = (
        lax.psum_scatter(grad_rows_part, "tensor", scatter_dimension=0, tiled=True),
        lax.psum_scatter(grad_rank_part, "tensor", scatter_dimension=0, tiled=True),
    )
    grad_rank_two_low = grad_rank_two.astype(jnp.bfloat16)
    delta_expand_down = product_rows(grad_rank_two_low, rows_two)
    grad_norm_two = grad_norm_two + product(grad_rank_two_low, down_expand)
    grad_residual = grad_out + norm_two_back(grad_norm_two)[0]
    grad_branch = grad_residual.astype(jnp.bfloat16)
    delta_output_up = product_rows(rank_out, grad_branch)
    rank_grad_out = product_cols(grad_branch, lift_output).astype(jnp.bfloat16)
    branch_full, rank_branch_full = (
        lax.all_gather(grad_branch, "tensor", axis=0, tiled=True),
        lax.all_gather(rank_grad_out, "tensor", axis=0, tiled=True),
    )
    query_back, key_back, value_back, output_back = (
        lax.all_gather(query_weight, "dp", axis=0, tiled=True),
        lax.all_gather(key_weight, "dp", axis=0, tiled=True),
        lax.all_gather(value_weight, "dp", axis=0, tiled=True),
        lax.all_gather(output_weight, "dp", axis=1, tiled=True),
    )
    grad_attended = (
        product_cols(branch_full, output_back) + product(rank_branch_full, down_output)
    ).astype(jnp.bfloat16)
    delta_output_down = product_rows(rank_branch_full, attended)
    grad_heads = grad_attended.reshape(seq_len, head_count, HEAD_DIM)
    grad_query_parts = []
    grad_keys = jnp.zeros((seq_len, head_count, HEAD_DIM), jnp.float32)
    grad_values = jnp.zeros((seq_len, head_count, HEAD_DIM), jnp.float32)
    for block_index in range(block_count):
        row_start = block_index * block_rows
        key_end = row_start + block_rows
        scores = block_scores(row_start, key_end)
        probs = jnp.exp(scores - lse_parts[block_index])
        probs_low = probs.astype(jnp.bfloat16)
        grad_block = grad_heads[row_start:key_end]
        grad_values = grad_values.at[:key_end].add(
            jnp.einsum("hqk,qhd->khd", probs_low, grad_block, preferred_element_type=jnp.float32)
        )
        grad_probs = jnp.einsum(
            "qhd,khd->hqk", grad_block, value_heads[:key_end], preferred_element_type=jnp.float32
        )
        grad_scores = (
            probs * (grad_probs - jnp.sum(grad_probs * probs, axis=-1, keepdims=True))
        ).astype(jnp.bfloat16)
        grad_query_parts.append(
            jnp.einsum(
                "hqk,khd->qhd", grad_scores, key_heads[:key_end], preferred_element_type=jnp.float32
            )
            * score_scale
        )
        grad_keys = grad_keys.at[:key_end].add(
            jnp.einsum(
                "hqk,qhd->khd",
                grad_scores,
                query_heads[row_start:key_end],
                preferred_element_type=jnp.float32,
            )
            * score_scale
        )
    grad_query_low = (
        jnp.concatenate(grad_query_parts, axis=0).reshape(seq_len, width_local).astype(jnp.bfloat16)
    )
    grad_key_low = grad_keys.reshape(seq_len, width_local).astype(jnp.bfloat16)
    grad_value_low = grad_values.reshape(seq_len, width_local).astype(jnp.bfloat16)
    delta_query_up = product_rows(rank_query, grad_query_low)
    delta_key_up = product_rows(rank_key, grad_key_low)
    delta_value_up = product_rows(rank_value, grad_value_low)
    grad_rows_one = (
        product_cols(grad_query_low, query_back)
        + product_cols(grad_key_low, key_back)
        + product_cols(grad_value_low, value_back)
    )
    grad_rank_one = jnp.concatenate(
        [
            product_cols(grad_query_low, lift_query),
            product_cols(grad_key_low, lift_key),
            product_cols(grad_value_low, lift_value),
        ],
        axis=1,
    )
    grad_norm_one, grad_rank_rows = (
        lax.psum_scatter(grad_rows_one, "tensor", scatter_dimension=0, tiled=True),
        lax.psum_scatter(grad_rank_one, "tensor", scatter_dimension=0, tiled=True),
    )
    grad_rank_low = grad_rank_rows.astype(jnp.bfloat16)
    delta_qkv_down = product_rows(grad_rank_low, rows_one)
    grad_norm_one = grad_norm_one + product(grad_rank_low, down_qkv)
    input_delta = (grad_residual + norm_one_back(grad_norm_one)[0]).astype(jnp.bfloat16)
    shared = lax.psum(
        (
            spread(delta_qkv_down[:rank_width]),
            spread(delta_qkv_down[rank_width : 2 * rank_width]),
            spread(delta_qkv_down[2 * rank_width :]),
            spread(delta_output_up),
            spread(delta_expand_down),
            spread(delta_shrink_up),
        ),
        ("dp", "tensor"),
    )
    split = lax.psum(
        (
            spread(delta_query_up),
            spread(delta_key_up),
            spread(delta_value_up),
            spread(delta_output_down),
            spread(delta_expand_up),
            spread(delta_shrink_down),
        ),
        "dp",
    )
    return (
        output,
        input_delta,
        shared[0],
        split[0],
        shared[1],
        split[1],
        shared[2],
        split[2],
        split[3],
        shared[3],
        shared[4],
        split[4],
        split[5],
        shared[5],
    )


def solution(mesh):
    return jax.shard_map(
        shards,
        mesh=mesh,
        in_specs=(
            P(("dp", "tensor"), None),
            P(("dp", "tensor"), None),
            P("dp", None),
            P("dp", None),
            P("dp"),
            P(),
            P(),
            P(),
            P(),
            P("dp", "tensor"),
            P("dp", "tensor"),
            P("dp", "tensor"),
            P("tensor", "dp"),
            P("dp", "tensor"),
            P("tensor", "dp"),
            P("tensor"),
            P("tensor"),
            P(),
            P("tensor"),
            P(),
            P(),
            P(None, None, "tensor"),
            P(),
            P(None, None, "tensor"),
            P(),
            P(None, None, "tensor"),
            P(None, None, "tensor"),
            P(),
            P(),
            P(None, None, "tensor"),
            P(None, None, "tensor"),
            P(),
        ),
        out_specs=(
            P(("dp", "tensor"), None),
            P(("dp", "tensor"), None),
            P(),
            P(None, None, "tensor"),
            P(),
            P(None, None, "tensor"),
            P(),
            P(None, None, "tensor"),
            P(None, None, "tensor"),
            P(),
            P(),
            P(None, None, "tensor"),
            P(None, None, "tensor"),
            P(),
        ),
        check_vma=False,
    )
```

profile of v0, /device:TPU:17, one launch (start us, length us, event | category | flops | bytes accessed | tf_op | source)
XLA Modules:
  0.0 1356.8 jit_solution(10319225183722140593)
XLA Ops:
  11.7 2.8 fusion.26
  22.8 6.0 all_gather.50
  30.6 28.5 %all-gather.15.cloned.1.call-done = bf16[2048,512]{1,0:T(8,128)(2,1)} async-done(((bf16[256,512]{1,0:T(8,128)(2,1)}), bf16[2048,512]{1,0:T(8,128)(2,1)}) %all-gather.15.cloned.1.call-update) | async-done | bytes 2097168 | tf_op jit(solution)/shard_map/all_gather | solution.py:105
  59.1 36.8 %all-gather.11.cloned.1.call-done = bf16[1024,2048]{1,0:T(8,128)(2,1)} async-done(((bf16[256,2048]{1,0:T(8,128)(2,1)}), bf16[1024,2048]{1,0:T(8,128)(2,1)}) %all-gather.11.cloned.1.call-update) | async-done | bytes 4194320 | tf_op jit(solution)/shard_map/all_gather | solution.py:117
  95.9 5.2 fusion.171
  101.8 43.7 %all-gather.17.cloned.1.call-done = bf16[2048,512]{1,0:T(8,128)(2,1)} async-done(((bf16[256,512]{1,0:T(8,128)(2,1)}), bf16[2048,512]{1,0:T(8,128)(2,1)}) %all-gather.17.cloned.1.call-update) | async-done | bytes 2097168 | tf_op jit(solution)/shard_map/all_gather | solution.py:106
  145.5 5.2 fusion.172
  152.1 3.0 fusion.168
  155.2 39.9 %all-gather.13.cloned.1.call-done = bf16[2048,512]{1,0:T(8,128)(2,1)} async-done(((bf16[256,512]{1,0:T(8,128)(2,1)}), bf16[2048,512]{1,0:T(8,128)(2,1)}) %all-gather.13.cloned.1.call-update) | async-done | bytes 2097168 | tf_op jit(solution)/shard_map/all_gather | solution.py:107
  195.1 5.2 fusion.170
  212.7 32.8 %all-gather.19.cloned.1.call-done = bf16[512,2048]{1,0:T(8,128)(2,1)} async-done(((bf16[512,256]{1,0:T(8,128)(2,1)}), bf16[512,2048]{1,0:T(8,128)(2,1)}) %all-gather.19.cloned.1.call-update) | async-done | bytes 2097168 | tf_op jit(solution)/shard_map/all_gather | solution.py:108
  245.6 7.3 fusion.173
  255.5 11.8 reduce-scatter.11.cloned.1.call-done
  267.2 74.4 %reduce-scatter.9.cloned.1.call-done = f32[256,2048]{1,0:T(8,128)} async-done(((f32[1024,2048]{1,0:T(8,128)}), f32[256,2048]{1,0:T(8,128)}) %reduce-scatter.9.cloned.1.call-update) | async-done | bytes 2097168 | tf_op jit(solution)/shard_map/reduce_scatter | solution.py:182
  347.7 6.3 all_gather.59
  359.2 19.1 %all-gather.27.cloned.1.call-done = bf16[1024,2048]{1,0:T(8,128)(2,1)} async-done(((bf16[256,2048]{1,0:T(8,128)(2,1)}), bf16[1024,2048]{1,0:T(8,128)(2,1)}) %all-gather.27.cloned.1.call-update) | async-done | bytes 4194320 | tf_op jit(solution)/shard_map/all_gather | solution.py:217
  378.3 125.0 %all-gather.25.cloned.1.call-done = bf16[2048,2048]{1,0:T(8,128)(2,1)} async-done(((bf16[2048,256]{1,0:T(8,128)(2,1)}), bf16[2048,2048]{1,0:T(8,128)(2,1)}) %all-gather.25.cloned.1.call-update) | async-done | bytes 8388624 | tf_op jit(solution)/shard_map/all_gather | solution.py:198
  503.3 14.7 %fusion.176 = f32[1024,2048]{1,0:T(8,128)} fusion(bf16[1024,2048]{1,0:T(8,128)(2,1)} %all-gather.27.cloned.1.call-done, bf16[2048,2048]{1,0:T(8,128)(2,1)} %all-gather.25.cloned.1.call-done), kind=kOutput, calls=%fused_computation.289 | convolution fusion | flops 8589934592 | bytes 20971520 | tf_op jit(solution)/shard_map/dot_general | solution.py:34
  518.3 7.3 all_gather.56
  525.6 102.3 %all-gather.23.cloned.1.call-done = bf16[2048,2048]{1,0:T(8,128)(2,1)} async-done(((bf16[256,2048]{1,0:T(8,128)(2,1)}), bf16[2048,2048]{1,0:T(8,128)(2,1)}) %all-gather.23.cloned.1.call-update) | async-done | bytes 8388624 | tf_op jit(solution)/shard_map/all_gather | solution.py:197
  627.9 36.8 %all-gather.21.cloned.1.call-done = bf16[1024,2048]{1,0:T(8,128)(2,1)} async-done(((bf16[256,2048]{1,0:T(8,128)(2,1)}), bf16[1024,2048]{1,0:T(8,128)(2,1)}) %all-gather.21.cloned.1.call-update) | async-done | bytes 4194320 | tf_op jit(solution)/shard_map/all_gather | solution.py:193
  664.8 12.6 fusion.174
  677.4 20.9 %multiply_convert_fusion.1 = (bf16[1024,2048]{1,0:T(8,128)(2,1)}, f32[1024,2048]{1,0:T(8,128)S(1)}, f32[1024,2048]{1,0:T(8,128)}) fusion(f32[2048]{0:T(1024)S(1)} %copy-done.109, f32[1024,2048]{1,0:T(8,128)S(1)} %fusion.174, bf16[1024,16]{0,1:T(8,128)(2,1)S(1)} %copy-done.71, bf16[1,16,2048]{2,0,1:T(2,128)(2,1)S(1)} %copy-done.50), kind=kOutput, calls=%fused_computation.7 | convolution fusion | flops 207618048 | bytes 29466624 | tf_op jit(solution)/shard_map/dot_general | solution.py:30
  698.4 7.8 add_convert_fusion
  706.2 4.0 fusion.88
  710.5 14.7 %fusion.177 = f32[1024,2048]{1,0:T(8,128)} fusion(bf16[1024,2048]{1,0:T(8,128)(2,1)} %add_convert_fusion, bf16[2048,2048]{1,0:T(8,128)(2,1)} %all-gather.23.cloned.1.call-done), kind=kOutput, calls=%fused_computation.290 | convolution fusion | flops 8589934592 | bytes 20971520 | tf_op jit(solution)/shard_map/dot_general | solution.py:34
  725.2 3.8 reduce-scatter.19.cloned.1.call-done
  729.0 74.4 %reduce-scatter.17.cloned.1.call-done = f32[256,2048]{1,0:T(8,128)} async-done(((f32[1024,2048]{1,0:T(8,128)}), f32[256,2048]{1,0:T(8,128)}) %reduce-scatter.17.cloned.1.call-update) | async-done | bytes 2097168 | tf_op jit(solution)/shard_map/reduce_scatter | solution.py:231
  803.4 2.3 multiply_reduce_fusion.2
  809.1 4.0 fusion.89
  814.8 6.0 all_gather.61
  820.9 23.3 %all-gather.29.cloned.1.call-done = bf16[1024,2048]{1,0:T(8,128)(2,1)} async-done(((bf16[256,2048]{1,0:T(8,128)(2,1)}), bf16[1024,2048]{1,0:T(8,128)(2,1)}) %all-gather.29.cloned.1.call-update) | async-done | bytes 4194320 | tf_op jit(solution)/shard_map/all_gather | solution.py:242
  844.2 5.2 fusion.178
  857.7 2.6 multiply_reduce_fusion
  870.0 14.6 %fusion.175 = f32[1024,2048]{1,0:T(8,128)} fusion(bf16[1024,2048]{1,0:T(8,128)(2,1)} %get-tuple-element.92, bf16[2048,2048]{1,0:T(8,128)(2,1)} %all-gather.25.cloned.1.call-done), kind=kOutput, calls=%fused_computation.288 | convolution fusion | flops 8589934592 | bytes 20971520 | tf_op jit(solution)/shard_map/dot_general | solution.py:30
  884.6 4.5 fusion.180
  889.2 2.4 fusion.179
  891.6 5.8 add_add_fusion
  898.3 3.8 fusion.182
  914.3 4.6 broadcast_multiply_fusion.1
  919.6 43.3 %reduce-scatter.13.cloned.1.call-done = f32[256,2048]{1,0:T(8,128)} async-done(((f32[1024,2048]{1,0:T(8,128)}), f32[256,2048]{1,0:T(8,128)}) %reduce-scatter.13.cloned.1.call-update) | async-done | bytes 2097168 | tf_op jit(solution)/shard_map/reduce_scatter | solution.py:206
  962.9 3.0 fusion.22
  966.0 70.8 %reduce-scatter.21.cloned.1.call-done = f32[256,2048]{1,0:T(8,128)} async-done(((f32[1024,2048]{1,0:T(8,128)}), f32[256,2048]{1,0:T(8,128)}) %reduce-scatter.21.cloned.1.call-update) | async-done | bytes 2097168 | tf_op jit(solution)/shard_map/reduce_scatter | solution.py:312
  1036.8 2.4 fusion.27
  1042.5 127.9 %all-reduce.9.cloned.1.call-done = (f32[8,16,512]{2,1,0:T(8,128)}, f32[8,16,512]{2,1,0:T(8,128)}, f32[8,16,512]{2,1,0:T(8,128)}, f32[8,16,512]{2,1,0:T(8,128)}, ...) async-done(((f32[8,16,512]{2,1,0:T(8,128)}, f32[8,16,512]{2,1,0:T(8,128)}, f32[8,16,512]{2,1,0:T(8,128)}, f32[8,16,512]{2,1,0:T(8,128)}, f32[8,16,2048]{2,1,0:T(8,128)}, ...) | async-done | bytes 3145744 | tf_op jit(solution)/shard_map/psum | solution.py:330
  1170.4 164.6 %all-reduce.7.cloned.1.call-done = (f32[8,16,2048]{2,1,0:T(8,128)}, f32[8,16,2048]{2,1,0:T(8,128)}, f32[8,16,2048]{2,1,0:T(8,128)}, f32[8,16,2048]{2,1,0:T(8,128...) async-done(((f32[8,16,2048]{2,1,0:T(8,128)}, f32[8,16,2048]{2,1,0:T(8,128)}, f32[8,16,2048]{2,1,0:T(8,128)}, f32[8,16,2048]{2,1,0:T(8,128)}, f32[8,16,2048]{2,1,0:T(8,128)}, ...) | async-done | bytes 6291472 | tf_op jit(solution)/shard_map/psum | solution.py:319
  1335.0 2.4 copy.183
  1339.2 2.3 copy.185
  (383 shorter events, 91.3 us)
Async XLA Ops:
  7.2 51.8 %all-gather.15.cloned.1.call-start = ((), (), s32[]{:S(2)}) async-start(), calls=%async_computation.10 | async-start | bytes 2359296 | tf_op jit(solution)/shard_map/all_gather | solution.py:105
  8.0 87.9 %all-gather.11.cloned.1.call-start = ((), (), s32[]{:S(2)}) async-start(), calls=%async_computation.8 | async-start | bytes 5242880 | tf_op jit(solution)/shard_map/all_gather | solution.py:117
  14.5 131.0 %all-gather.17.cloned.1.call-start = ((), (), s32[]{:S(2)}) async-start(), calls=%async_computation.11 | async-start | bytes 2359296 | tf_op jit(solution)/shard_map/all_gather | solution.py:106
  15.2 179.9 %all-gather.13.cloned.1.call-start = ((), (), s32[]{:S(2)}) async-start(), calls=%async_computation.9 | async-start | bytes 2359296 | tf_op jit(solution)/shard_map/all_gather | solution.py:107
  15.8 229.7 %all-gather.19.cloned.1.call-start = ((), (), s32[]{:S(2)}) async-start(), calls=%async_computation.12 | async-start | bytes 2359296 | tf_op jit(solution)/shard_map/all_gather | solution.py:108
  16.4 250.9 %reduce-scatter.11.cloned.1.call-start = ((), (), s32[]{:S(2)}) async-start(), calls=%async_computation.14 | async-start | bytes 81920 | tf_op jit(solution)/shard_map/reduce_scatter | solution.py:183
  22.3 78.8 %copy-start.53 = (bf16[16,2048]{1,0:T(8,128)(2,1)}, bf16[16,2048]{1,0:T(8,128)(2,1)S(1)}, u32[]{:S(2)}) copy-start(bf16[16,2048]{1,0:T(8,128)(2,1)S(1)} %get-tuple-element.128) | copy-start | bytes 196612
  22.3 78.8 %copy-start.55 = (bf16[16,2048]{1,0:T(8,128)(2,1)}, bf16[16,2048]{1,0:T(8,128)(2,1)S(1)}, u32[]{:S(2)}) copy-start(bf16[16,2048]{1,0:T(8,128)(2,1)S(1)} %get-tuple-element.129) | copy-start | bytes 196612
  28.8 171.6 %copy-start.43 = (bf16[1024,48]{0,1:T(8,128)(2,1)}, bf16[1024,48]{0,1:T(8,128)(2,1)S(1)}, u32[]{:S(2)}) copy-start(bf16[1024,48]{0,1:T(8,128)(2,1)S(1)} %all_gather.50) | copy-start | bytes 294916
  29.9 71.3 %copy-start.61 = (bf16[1,16,512]{2,0,1:T(2,128)(2,1)}, bf16[1,16,512]{2,0,1:T(2,128)(2,1)S(1)}, u32[]{:S(2)}) copy-start(bf16[1,16,512]{2,0,1:T(2,128)(2,1)S(1)} %fusion.75) | copy-start | bytes 49156
  30.1 120.6 %copy-start.63 = (bf16[1,16,512]{2,0,1:T(2,128)(2,1)}, bf16[1,16,512]{2,0,1:T(2,128)(2,1)S(1)}, u32[]{:S(2)}) copy-start(bf16[1,16,512]{2,0,1:T(2,128)(2,1)S(1)} %fusion.73) | copy-start | bytes 49156
  30.3 170.0 %copy-start.65 = (bf16[1,16,512]{2,0,1:T(2,128)(2,1)}, bf16[1,16,512]{2,0,1:T(2,128)(2,1)S(1)}, u32[]{:S(2)}) copy-start(bf16[1,16,512]{2,0,1:T(2,128)(2,1)S(1)} %fusion.77) | copy-start | bytes 49156
  30.6 181.1 %copy-start.67 = (bf16[1,16,512]{2,0,1:T(2,128)(2,1)}, bf16[1,16,512]{2,0,1:T(2,128)(2,1)S(1)}, u32[]{:S(2)}) copy-start(bf16[1,16,512]{2,0,1:T(2,128)(2,1)S(1)} %fusion.71) | copy-start | bytes 49156
  30.6 70.6 %copy-start.106 = (f32[512]{0:T(512)S(1)}, f32[512]{0:T(512)}, u32[]{:S(2)}) copy-start(f32[512]{0:T(512)} %param.59) | copy-start | bytes 6148
  101.8 101.9 %copy-start.28 = (bf16[512,512]{0,1:T(8,128)(2,1)}, bf16[512,512]{0,1:T(8,128)(2,1)S(1)}, u32[]{:S(2)}) copy-start(bf16[512,512]{0,1:T(8,128)(2,1)S(1)} %get-tuple-element.97) | copy-start | bytes 1572868
  151.2 52.5 %copy-start.16 = (bf16[1024,512]{0,1:T(8,128)(2,1)}, bf16[1024,512]{0,1:T(8,128)(2,1)S(1)}, u32[]{:S(2)}) copy-start(bf16[1024,512]{0,1:T(8,128)(2,1)S(1)} %add_convert_fusion.4) | copy-start | bytes 3145732
  155.2 52.6 %copy-start.77 = (f32[4,512]{1,0:T(4,128)}, f32[4,512]{1,0:T(4,128)S(1)}, u32[]{:S(2)}) copy-start(f32[4,512]{1,0:T(4,128)S(1)} %get-tuple-element.115) | copy-start | bytes 24580
  212.7 129.0 %reduce-scatter.9.cloned.1.call-start = ((), (), s32[]{:S(2)}) async-start(), calls=%async_computation.13 | async-start | bytes 10485760 | tf_op jit(solution)/shard_map/reduce_scatter | solution.py:182
  252.8 88.8 %copy-start.5 = (bf16[256,2048]{1,0:T(8,128)(2,1)S(1)}, bf16[256,2048]{1,0:T(8,128)(2,1)}, u32[]{:S(2)}) copy-start(bf16[256,2048]{1,0:T(8,128)(2,1)} %param.44) | copy-start | bytes 3145732
  252.8 88.8 %copy-start.101 = (f32[2048]{0:T(1024)S(1)}, f32[2048]{0:T(1024)}, u32[]{:S(2)}) copy-start(f32[2048]{0:T(1024)} %param.61) | copy-start | bytes 24580
  252.8 125.4 %all-gather.27.cloned.1.call-start = ((), (), s32[]{:S(2)}) async-start(), calls=%async_computation.20 | async-start | bytes 5242880 | tf_op jit(solution)/shard_map/all_gather | solution.py:217
  253.6 249.7 %all-gather.25.cloned.1.call-start = ((), (), s32[]{:S(2)}) async-start(), calls=%async_computation.17 | async-start | bytes 9437184 | tf_op jit(solution)/shard_map/all_gather | solution.py:198
  254.3 373.6 %all-gather.23.cloned.1.call-start = ((), (), s32[]{:S(2)}) async-start(), calls=%async_computation.16 | async-start | bytes 9437184 | tf_op jit(solution)/shard_map/all_gather | solution.py:197
  254.9 89.3 %copy-start.84 = (f32[2048]{0:T(1024)S(1)}, f32[2048]{0:T(1024)}, u32[]{:S(2)}) copy-start(f32[2048]{0:T(1024)} %param.51) | copy-start | bytes 24580
  254.9 89.3 %copy-start.102 = (f32[2048]{0:T(1024)S(1)}, f32[2048]{0:T(1024)}, u32[]{:S(2)}) copy-start(f32[2048]{0:T(1024)} %param.52) | copy-start | bytes 24580
  254.9 409.8 %all-gather.21.cloned.1.call-start = ((), (), s32[]{:S(2)}) async-start(), calls=%async_computation.15 | async-start | bytes 5242880 | tf_op jit(solution)/shard_map/all_gather | solution.py:193
  345.7 383.3 %reduce-scatter.19.cloned.1.call-start = ((), (), s32[]{:S(2)}) async-start(), calls=%async_computation.22 | async-start | bytes 81920 | tf_op jit(solution)/shard_map/reduce_scatter | solution.py:232
  710.2 93.2 %reduce-scatter.17.cloned.1.call-start = ((), (), s32[]{:S(2)}) async-start(), calls=%async_computation.21 | async-start | bytes 10485760 | tf_op jit(solution)/shard_map/reduce_scatter | solution.py:231
  725.2 119.0 %all-gather.29.cloned.1.call-start = ((), (), s32[]{:S(2)}) async-start(), calls=%async_computation.23 | async-start | bytes 5242880 | tf_op jit(solution)/shard_map/all_gather | solution.py:242
  809.0 94.9 %reduce-scatter.15.cloned.1.call-start = ((), (), s32[]{:S(2)}) async-start(), calls=%async_computation.19 | async-start | bytes 81920 | tf_op jit(solution)/shard_map/reduce_scatter | solution.py:207
  813.2 100.0 %reduce-scatter.23.cloned.1.call-start = ((), (), s32[]{:S(2)}) async-start(), calls=%async_computation.25 | async-start | bytes 245760 | tf_op jit(solution)/shard_map/reduce_scatter | solution.py:313
  869.7 93.3 %reduce-scatter.13.cloned.1.call-start = ((), (), s32[]{:S(2)}) async-start(), calls=%async_computation.18 | async-start | bytes 10485760 | tf_op jit(solution)/shard_map/reduce_scatter | solution.py:206
  884.6 152.2 %reduce-scatter.21.cloned.1.call-start = ((), (), s32[]{:S(2)}) async-start(), calls=%async_computation.24 | async-start | bytes 10485760 | tf_op jit(solution)/shard_map/reduce_scatter | solution.py:312
  897.4 273.0 %all-reduce.9.cloned.1.call-start = ((), (), s32[]{:S(2)}) async-start(), calls=%async_computation.27 | async-start | bytes 6291456 | tf_op jit(solution)/shard_map/psum | solution.py:330
  918.9 416.1 %all-reduce.7.cloned.1.call-start = ((), (), s32[]{:S(2)}) async-start(), calls=%async_computation.26 | async-start | bytes 12582912 | tf_op jit(solution)/shard_map/psum | solution.py:319
  919.5 117.3 %copy-start.6 = (bf16[256,2048]{1,0:T(8,128)(2,1)S(1)}, bf16[256,2048]{1,0:T(8,128)(2,1)}, u32[]{:S(2)}) copy-start(bf16[256,2048]{1,0:T(8,128)(2,1)} %param.44) | copy-start | bytes 3145732
  919.5 117.3 %copy-start.52 = (bf16[1,16,2048]{2,1,0:T(8,128)(2,1)S(1)}, bf16[1,16,2048]{2,1,0:T(8,128)(2,1)}, u32[]{:S(2)}) copy-start(bf16[1,16,2048]{2,1,0:T(8,128)(2,1)} %copy-done.51) | copy-start | bytes 196612
  919.5 117.3 %copy-start.54 = (bf16[16,2048]{1,0:T(8,128)(2,1)S(1)}, bf16[16,2048]{1,0:T(8,128)(2,1)}, u32[]{:S(2)}) copy-start(bf16[16,2048]{1,0:T(8,128)(2,1)} %copy-done.53) | copy-start | bytes 196612
  919.5 117.3 %copy-start.56 = (bf16[16,2048]{1,0:T(8,128)(2,1)S(1)}, bf16[16,2048]{1,0:T(8,128)(2,1)}, u32[]{:S(2)}) copy-start(bf16[16,2048]{1,0:T(8,128)(2,1)} %copy-done.55) | copy-start | bytes 196612
  919.6 117.3 %copy-start.60 = (f32[256,48]{0,1:T(8,128)S(1)}, f32[256,48]{0,1:T(8,128)}, u32[]{:S(2)}) copy-start(f32[256,48]{0,1:T(8,128)} %reduce-scatter.23.cloned.1.call-done) | copy-start | bytes 147460
  919.6 117.3 %copy-start.83 = (f32[256]{0:T(256)S(1)}, f32[256]{0:T(256)}, u32[]{:S(2)}) copy-start(f32[256]{0:T(256)} %copy-done.82) | copy-start | bytes 3076
  919.6 117.3 %copy-start.85 = (f32[2048]{0:T(1024)S(1)}, f32[2048]{0:T(1024)}, u32[]{:S(2)}) copy-start(f32[2048]{0:T(1024)} %param.49) | copy-start | bytes 24580
  919.6 120.4 %copy-start.93 = (f32[256]{0:T(256)S(1)}, f32[256]{0:T(256)}, u32[]{:S(2)}) copy-start(f32[256]{0:T(256)} %copy-done.92) | copy-start | bytes 3076
  966.0 74.6 %copy-start.8 = (bf16[256,2048]{1,0:T(8,128)(2,1)S(1)}, bf16[256,2048]{1,0:T(8,128)(2,1)}, u32[]{:S(2)}) copy-start(bf16[256,2048]{1,0:T(8,128)(2,1)} %param.45) | copy-start | bytes 3145732
  966.0 74.6 %copy-start.97 = (f32[256]{0:T(256)S(1)}, f32[256]{0:T(256)}, u32[]{:S(2)}) copy-start(f32[256]{0:T(256)} %copy-done.96) | copy-start | bytes 3076
  1170.4 171.1 %copy-start.59 = (f32[8,16,512]{2,1,0:T(8,128)S(1)}, f32[8,16,512]{2,1,0:T(8,128)}, u32[]{:S(2)}) copy-start(f32[8,16,512]{2,1,0:T(8,128)} %get-tuple-element.135) | copy-start | bytes 786436
  1170.4 172.8 %copy-start.58 = (f32[8,16,512]{2,1,0:T(8,128)S(1)}, f32[8,16,512]{2,1,0:T(8,128)}, u32[]{:S(2)}) copy-start(f32[8,16,512]{2,1,0:T(8,128)} %get-tuple-element.137) | copy-start | bytes 786436
  1170.4 173.5 %copy-start.57 = (f32[8,16,512]{2,1,0:T(8,128)S(1)}, f32[8,16,512]{2,1,0:T(8,128)}, u32[]{:S(2)}) copy-start(f32[8,16,512]{2,1,0:T(8,128)} %get-tuple-element.138) | copy-start | bytes 786436
  (87 other events, 736.5 us)
Sparse Core Ops, SparseCore 0:
  10.1 48.8 all-gather.14
  61.2 34.6 all-gather.10
  98.0 47.4 all-gather.16
  147.5 47.6 all-gather.12
  197.0 48.5 all-gather.18
  248.4 18.8 reduce-scatter.10
  269.8 71.7 reduce-scatter.8
  343.2 35.0 all-gather.26
  380.3 122.9 all-gather.24
  505.2 122.6 all-gather.22
  630.1 34.6 all-gather.20
  710.3 18.6 reduce-scatter.18
  731.6 71.7 reduce-scatter.16
  809.1 35.0 all-gather.28
  847.0 18.6 reduce-scatter.14
  869.8 19.0 reduce-scatter.22
  891.3 71.5 reduce-scatter.12
  965.4 71.3 reduce-scatter.20
  1042.2 128.1 all-reduce.8
  1177.8 157.1 all-reduce.6
where the time goes:
time: 1360 us
  waiting for transfers between devices  1060 us (78%)
  matrix products  194 us (14%)
  other arithmetic  27.6 us (2%)
  local copies, waits for them, and re-layouts  26.3 us (2%)
  blocking collectives  25.6 us (2%)
  between operations  17.1 us (1%)
    psum x1, waiting for transfers between devices, shards(): lax.psum((spread(delta_qkv_down[:rank_width]), spread(delta_qkv_down[rank...  165 us
    psum x1, waiting for transfers between devices, shards(): lax.psum((spread(delta_query_up), spread(delta_key_up), spread(delta_valu...  128 us
    all_gather x1, waiting for transfers between devices, shards(): lax.all_gather(shrink_weight, 'dp', axis=1, tiled=True)  125 us
    all_gather x1, waiting for transfers between devices, shards(): lax.all_gather(expand_weight, 'dp', axis=0, tiled=True)  102 us
    dot_general x17, matrix products, product(): return jnp.dot(left, right, preferred_element_type=jnp.float32)  91.1 us
    reduce_scatter x1, waiting for transfers between devices, shards(): lax.psum_scatter(main_part, 'tensor', scatter_dimension=0, tiled=True)  74.4 us
    reduce_scatter x1, waiting for transfers between devices, shards(): lax.psum_scatter(grad_rows_part, 'tensor', scatter_dimension=0, tiled=True)  74.4 us
    reduce_scatter x1, waiting for transfers between devices, shards(): lax.psum_scatter(grad_rows_one, 'tensor', scatter_dimension=0, tiled=True)  70.8 us
  transfers between devices with their start and end apart: 20, of which 18 were waited for; matrix products, arithmetic and copies ran while one was open for 13% of the time, Pallas kernels for 0%

commit v1 on v0

v1 whole, which is shorter than its diff:
```python
import functools

import jax
import jax.numpy as jnp
from jax import lax
from jax.sharding import PartitionSpec as P

HEAD_DIM = 128
SEGS = 13
BF = jnp.bfloat16
F32 = jnp.float32


def ancestry(parents):
    seg_range = jnp.arange(SEGS, dtype=jnp.int32)
    current = seg_range
    ancestors = current[:, None] == seg_range[None, :]
    for hop_index in range(SEGS - 1):
        current = jnp.sum(
            jnp.where(current[:, None] == seg_range[None, :], parents[None, :], 0), axis=1
        )
        ancestors = jnp.logical_or(ancestors, current[:, None] == seg_range[None, :])
    return ancestors


def product(left, right):
    return jnp.dot(left, right, preferred_element_type=F32)


def product_cols(left, right):
    return lax.dot_general(
        left, right, (((1,), (1,)), ((), ())), preferred_element_type=F32
    )


def product_rows(left, right):
    return lax.dot_general(
        left, right, (((0,), (0,)), ((), ())), preferred_element_type=F32
    )


def shards(
    dp_size,
    inputs,
    cotangent,
    segment_ids,
    parent_links,
    adapter_choice,
    gain_one,
    shift_one,
    gain_two,
    shift_two,
    query_weight,
    key_weight,
    value_weight,
    output_weight,
    expand_weight,
    shrink_weight,
    query_bias,
    value_bias,
    output_bias,
    expand_bias,
    shrink_bias,
    query_down,
    query_up,
    key_down,
    key_up,
    value_down,
    value_up,
    output_down,
    output_up,
    expand_down,
    expand_up,
    shrink_down,
    shrink_up,
):
    slot_count = query_down.shape[0]
    rank_width = query_down.shape[1]
    feats = inputs.shape[1]
    row_count = inputs.shape[0]
    width_local = query_weight.shape[1]
    hidden_local = expand_weight.shape[1]
    pair_count = dp_size // 2
    block = feats // dp_size
    half = feats // 2

    tensor_index = lax.axis_index("tensor")
    core_odd = (tensor_index % 2) == 1
    chip_odd = (tensor_index // 2) == 1
    dp_odd = (lax.axis_index("dp") % 2) == 1

    core_pairs = [(0, 1), (1, 0), (2, 3), (3, 2)]
    chip_pairs = [(0, 2), (2, 0), (1, 3), (3, 1)]
    dp_pairs = [(i, i ^ 1) for i in range(dp_size)]
    line_groups = [list(range(0, dp_size, 2)), list(range(1, dp_size, 2))]

    def to_core(v):
        return lax.ppermute(v, "tensor", core_pairs)

    def to_chip(v):
        return lax.ppermute(v, "tensor", chip_pairs)

    def own_first(v):
        parts = [v[..., b * block : (b + 1) * block] for b in range(dp_size)]
        pairs = [(parts[2 * p], parts[2 * p + 1]) for p in range(pair_count)]
        return jnp.concatenate(
            [jnp.where(dp_odd, odd, even) for even, odd in pairs]
            + [jnp.where(dp_odd, even, odd) for even, odd in pairs],
            axis=-1,
        )

    def natural(v):
        parts = [v[..., b * block : (b + 1) * block] for b in range(dp_size)]
        pairs = [(parts[p], parts[pair_count + p]) for p in range(pair_count)]
        return jnp.concatenate(
            [
                jnp.where(dp_odd, a, b)
                for own, other in pairs
                for a, b in ((other, own), (own, other))
            ],
            axis=-1,
        )

    def after(value, *others):
        return lax.optimization_barrier((value,) + others)[0]

    def swap_blocks(v):
        parts = [v[k * row_count : (k + 1) * row_count] for k in range(4)]
        low = [jnp.where(core_odd, parts[1], parts[0]), jnp.where(core_odd, parts[0], parts[1])]
        high = [jnp.where(core_odd, parts[3], parts[2]), jnp.where(core_odd, parts[2], parts[3])]
        return jnp.concatenate(
            [
                jnp.where(chip_odd, high[0], low[0]),
                jnp.where(chip_odd, high[1], low[1]),
                jnp.where(chip_odd, low[0], high[0]),
                jnp.where(chip_odd, low[1], high[1]),
            ],
            axis=0,
        )

    def gather_rows(rows):
        near = to_core(rows)
        far = to_chip(rows)
        far_near = to_core(far)
        return jnp.concatenate([rows, near, far, far_near], axis=0)

    def reduce_rows(partial):
        parts = [partial[k * row_count : (k + 1) * row_count] for k in range(4)]
        far = parts[2] + to_core(parts[3].astype(BF)).astype(F32)
        far_sum = to_chip(far.astype(BF))
        near = parts[0] + to_core(parts[1].astype(BF)).astype(F32)
        return near + far_sum.astype(F32)

    def fetch(pieces, *held):
        shard = jnp.concatenate(pieces, axis=1)
        if held:
            shard = after(shard, *held)
        own = lax.all_gather(shard, "dp", axis=0, tiled=True, axis_index_groups=line_groups)
        return own, lax.ppermute(own, "dp", dp_pairs), 0

    def fetch_paired(pieces, *held):
        shard = jnp.concatenate(pieces, axis=1)
        shard = jnp.concatenate([shard, lax.ppermute(shard, "dp", dp_pairs)], axis=1)
        if held:
            shard = after(shard, *held)
        both = lax.all_gather(shard, "dp", axis=0, tiled=True, axis_index_groups=line_groups)
        return both, both, shard.shape[1] // 2

    def into(left, weight, first, last):
        own, other, skip = weight
        return product(left[:, :half], own[:, first:last]) + product(
            left[:, half:], other[:, skip + first : skip + last]
        )

    def out_of(left, weight, first, last, base=None):
        own, other, skip = weight
        near = product_cols(left, own[:, first:last])
        far = product_cols(left, other[:, skip + first : skip + last])
        if base is not None:
            near, far = base[0] + near, base[1] + far
        return near, far

    def beside(pair):
        return jnp.concatenate(pair, axis=1)

    chunk_count = 4
    chunk = hidden_local // chunk_count
    output_turned = output_weight.T
    shrink_turned = shrink_weight.T
    weight_qk = fetch([query_weight, key_weight])
    weight_vo = fetch([value_weight, output_turned])
    weight_ffn, held = [], [weight_qk, weight_vo]
    for h in range(chunk_count):
        pieces = [
            expand_weight[:, h * chunk : (h + 1) * chunk],
            shrink_turned[:, h * chunk : (h + 1) * chunk],
        ]
        got = (fetch_paired if h == chunk_count - 1 else fetch)(pieces, held[-2][0])
        held.append(got)
        weight_ffn.append(got)

    select = (jnp.arange(slot_count, dtype=jnp.int32) == adapter_choice[0]).astype(BF)

    def adapter_of(adapter_table):
        return jnp.einsum(
            "a,ard->rd", select, adapter_table, preferred_element_type=F32
        ).astype(BF)

    down_qkv = own_first(
        jnp.concatenate(
            [adapter_of(query_down), adapter_of(key_down), adapter_of(value_down)], axis=0
        )
    )
    lift_query = adapter_of(query_up)
    lift_key = adapter_of(key_up)
    lift_value = adapter_of(value_up)
    down_output = adapter_of(output_down)
    lift_output = own_first(adapter_of(output_up))
    down_expand = own_first(adapter_of(expand_down))
    lift_expand = adapter_of(expand_up)
    down_shrink = adapter_of(shrink_down)
    lift_shrink = own_first(adapter_of(shrink_up))

    gain_a, shift_a = own_first(gain_one), own_first(shift_one)
    gain_b, shift_b = own_first(gain_two), own_first(shift_two)
    out_bias = own_first(output_bias)
    last_bias = own_first(shrink_bias)

    def normalize(values):
        row_mean = jnp.mean(values, axis=-1, keepdims=True)
        centred = values - row_mean
        row_var = jnp.mean(centred * centred, axis=-1, keepdims=True)
        scale = lax.rsqrt(row_var + 1e-05)
        return centred * scale, scale

    def norm_back(grad, gain, unit, scale):
        scaled = grad * gain
        return (
            scaled
            - jnp.mean(scaled, axis=-1, keepdims=True)
            - unit * jnp.mean(scaled * unit, axis=-1, keepdims=True)
        ) * scale

    inputs_wide = own_first(inputs).astype(F32)
    cot = own_first(cotangent)
    unit_one, scale_one = normalize(inputs_wide)
    rows_one = (unit_one * gain_a + shift_a).astype(BF)
    full_one = gather_rows(rows_one)
    full_cot = gather_rows(cot)
    seq_len = full_one.shape[0]
    head_count = width_local // HEAD_DIM

    rank_one = product_cols(full_one, down_qkv).astype(BF)
    rank_query = rank_one[:, :rank_width]
    rank_key = rank_one[:, rank_width : 2 * rank_width]
    rank_value = rank_one[:, 2 * rank_width :]
    query_key = into(after(full_one, weight_vo[0]), weight_qk, 0, 2 * width_local)
    queries = swap_blocks(
        (query_key[:, :width_local] + product(rank_query, lift_query) + query_bias).astype(BF)
    )
    keys_low = swap_blocks((query_key[:, width_local:] + product(rank_key, lift_key)).astype(BF))
    values_low = swap_blocks(
        (
            into(after(full_one, weight_ffn[0][0]), weight_vo, 0, width_local)
            + product(rank_value, lift_value)
            + value_bias
        ).astype(BF)
    )
    seg_range = jnp.arange(SEGS, dtype=jnp.int32)
    seg_hot = (segment_ids[0][:, None] == seg_range[None, :]).astype(BF)
    path_hot = product(seg_hot, ancestry(parent_links[0]).astype(BF)).astype(BF)
    positions = jnp.arange(seq_len, dtype=jnp.int32)
    block_rows = min(512, seq_len)
    block_count = seq_len // block_rows
    score_scale = HEAD_DIM ** (-0.5)
    query_heads = queries.reshape(seq_len, head_count, HEAD_DIM)
    key_heads = keys_low.reshape(seq_len, head_count, HEAD_DIM)
    value_heads = values_low.reshape(seq_len, head_count, HEAD_DIM)

    def block_scores(row_start, key_end):
        same_path = (
            product_cols(path_hot[row_start : row_start + block_rows], seg_hot[:key_end]) > 0.5
        )
        causal = positions[row_start : row_start + block_rows, None] >= positions[None, :key_end]
        raw_scores = (
            jnp.einsum(
                "qhd,khd->hqk",
                query_heads[row_start : row_start + block_rows],
                key_heads[:key_end],
                preferred_element_type=F32,
            )
            * score_scale
        )
        return jnp.where(jnp.logical_and(same_path, causal)[None], raw_scores, -1e30)

    attended_parts = []
    lse_parts = []
    for block_index in range(block_count):
        row_start = block_index * block_rows
        key_end = row_start + block_rows
        scores = block_scores(row_start, key_end)
        row_top = jnp.max(scores, axis=-1, keepdims=True)
        raised = jnp.exp(scores - row_top)
        row_total = jnp.sum(raised, axis=-1, keepdims=True)
        lse_parts.append(row_top + jnp.log(row_total))
        probs_low = (raised / row_total).astype(BF)
        attended_parts.append(
            jnp.einsum(
                "hqk,khd->qhd", probs_low, value_heads[:key_end], preferred_element_type=F32
            )
        )
    attended = swap_blocks(
        jnp.concatenate(attended_parts, axis=0).reshape(seq_len, width_local).astype(BF)
    )
    rank_out = product_cols(attended, down_output).astype(BF)
    main_rows = reduce_rows(
        beside(out_of(attended, weight_vo, width_local, 2 * width_local))
        + product(rank_out, lift_output)
    )
    main_rows = after(main_rows, weight_ffn[1][0])
    residual = inputs_wide + main_rows + out_bias
    unit_two, scale_two = normalize(residual)
    rows_two = (unit_two * gain_b + shift_b).astype(BF)
    full_two = after(gather_rows(rows_two), weight_ffn[2][0])
    rank_two = product_cols(full_two, down_expand).astype(BF)
    rank_grad = product_cols(full_cot, lift_shrink).astype(BF)

    hidden_parts = []
    grad_pre_parts = []
    grad_two, main_two = None, None
    for h in range(chunk_count):
        cols = slice(h * chunk, (h + 1) * chunk)
        weight = weight_ffn[h]
        here_two, here_cot = full_two, full_cot
        if h:
            here_two, here_cot, _ = lax.optimization_barrier(
                (full_two, full_cot, grad_pre_parts[-1])
            )
        pre_act = (
            into(here_two, weight, 0, chunk)
            + product(rank_two, lift_expand[:, cols])
            + expand_bias[cols]
        )
        grad_hidden = into(here_cot, weight, chunk, 2 * chunk) + product(
            rank_grad, down_shrink[:, cols]
        )
        bell = 0.5 * (1.0 + lax.erf(pre_act * (0.5**0.5)))
        slope = bell + pre_act * jnp.exp(-0.5 * pre_act * pre_act) * (0.5 / jnp.pi) ** 0.5
        hidden_parts.append((pre_act * bell).astype(BF))
        grad_pre_parts.append((grad_hidden * slope).astype(BF))
        grad_two = out_of(grad_pre_parts[h], weight, 0, chunk, grad_two)
        main_two = out_of(hidden_parts[h], weight, chunk, 2 * chunk, main_two)

    grad_rank_two = sum(
        product_cols(grad_pre_parts[h], lift_expand[:, h * chunk : (h + 1) * chunk])
        for h in range(chunk_count)
    ).astype(BF)
    grad_norm_two = reduce_rows(beside(grad_two) + product(grad_rank_two, down_expand))
    grad_residual = cot.astype(F32) + norm_back(grad_norm_two, gain_b, unit_two, scale_two)
    grad_branch = grad_residual.astype(BF)
    full_branch = gather_rows(grad_branch)
    rank_grad_out = product_cols(full_branch, lift_output).astype(BF)
    grad_attended = swap_blocks(
        (
            into(full_branch, weight_vo, width_local, 2 * width_local)
            + product(rank_grad_out, down_output)
        ).astype(BF)
    )

    rank_shrink = sum(
        product_cols(hidden_parts[h], down_shrink[:, h * chunk : (h + 1) * chunk])
        for h in range(chunk_count)
    ).astype(BF)
    main_rows_two = reduce_rows(beside(main_two) + product(rank_shrink, lift_shrink))
    output = natural((residual + main_rows_two + last_bias).astype(BF))

    delta_shrink_up = product_rows(rank_shrink, full_cot)
    delta_expand_down = product_rows(grad_rank_two, full_two)
    delta_output_up = product_rows(rank_out, full_branch)
    delta_shrink_down = jnp.concatenate(
        [product_rows(rank_grad, part) for part in hidden_parts], axis=1
    )
    delta_expand_up = jnp.concatenate(
        [product_rows(rank_two, part) for part in grad_pre_parts], axis=1
    )
    delta_output_down = product_rows(rank_grad_out, attended)

    hot_lanes = (
        jnp.arange(128, dtype=jnp.int32)[None, :] == adapter_choice[0]
    ).astype(BF) * jnp.ones((rank_width, 1), BF)

    def by_tensor(parts):
        low = [jnp.where(core_odd, parts[1], parts[0]), jnp.where(core_odd, parts[0], parts[1])]
        high = [jnp.where(core_odd, parts[3], parts[2]), jnp.where(core_odd, parts[2], parts[3])]
        return [jnp.where(chip_odd, b, a) for a, b in zip(low + high, high + low)]

    def settle(wide, slim):
        count = len(wide)
        quarter = feats // 4
        stacked = natural(jnp.concatenate(wide, axis=0).astype(BF))
        parts = by_tensor([stacked[:, t * quarter : (t + 1) * quarter] for t in range(4)])
        got = to_core(jnp.concatenate([parts[1], parts[3]], axis=0)).astype(F32)
        rows = stacked.shape[0]
        far = to_chip((parts[2] + got[rows:]).astype(BF)).astype(F32)
        mine = (parts[0] + got[:rows] + far).astype(BF)
        flat = jnp.concatenate(
            [mine[k * rank_width : (k + 1) * rank_width] for k in range(count)]
            + [d.astype(BF) for d in slim]
            + [hot_lanes],
            axis=1,
        )
        pair = jnp.stack([flat, lax.ppermute(flat, "dp", dp_pairs)])
        trees = [pair] + [
            lax.ppermute(pair, "dp", [(i, (i + 2 * s) % dp_size) for i in range(dp_size)])
            for s in range(1, pair_count)
        ]
        trees = jnp.concatenate(trees, axis=0)
        hot = trees[:, 0, flat.shape[1] - 128 : flat.shape[1] - 128 + slot_count]
        summed = lax.dot_general(
            hot,
            trees[:, :, : flat.shape[1] - 128],
            (((0,), (0,)), ((), ())),
            preferred_element_type=F32,
        )
        own = summed[:, :, : count * quarter].astype(BF)
        near = to_core(own)
        away = to_chip(own)
        across = by_tensor([own, near, away, to_core(away)])
        wide_out = [
            jnp.concatenate(
                [piece[:, :, k * quarter : (k + 1) * quarter] for piece in across], axis=-1
            ).astype(F32)
            for k in range(count)
        ]
        slim_out, at = [], count * quarter
        for d in slim:
            slim_out.append(summed[:, :, at : at + d.shape[1]])
            at += d.shape[1]
        return wide_out, slim_out

    (shrink_up_out, expand_down_out, output_up_out), (
        shrink_down_out,
        expand_up_out,
        output_down_out,
    ) = settle(
        [delta_shrink_up, delta_expand_down, delta_output_up],
        [delta_shrink_down, delta_expand_up, delta_output_down],
    )

    grad_heads = grad_attended.reshape(seq_len, head_count, HEAD_DIM)
    grad_query_parts = []
    grad_keys = jnp.zeros((seq_len, head_count, HEAD_DIM), F32)
    grad_values = jnp.zeros((seq_len, head_count, HEAD_DIM), F32)
    for block_index in range(block_count):
        row_start = block_index * block_rows
        key_end = row_start + block_rows
        scores = block_scores(row_start, key_end)
        probs = jnp.exp(scores - lse_parts[block_index])
        probs_low = probs.astype(BF)
        grad_block = grad_heads[row_start:key_end]
        grad_values = grad_values.at[:key_end].add(
            jnp.einsum("hqk,qhd->khd", probs_low, grad_block, preferred_element_type=F32)
        )
        grad_probs = jnp.einsum(
            "qhd,khd->hqk", grad_block, value_heads[:key_end], preferred_element_type=F32
        )
        grad_scores = (
            probs * (grad_probs - jnp.sum(grad_probs * probs, axis=-1, keepdims=True))
        ).astype(BF)
        grad_query_parts.append(
            jnp.einsum(
                "hqk,khd->qhd", grad_scores, key_heads[:key_end], preferred_element_type=F32
            )
            * score_scale
        )
        grad_keys = grad_keys.at[:key_end].add(
            jnp.einsum(
                "hqk,qhd->khd",
                grad_scores,
                query_heads[row_start:key_end],
                preferred_element_type=F32,
            )
            * score_scale
        )
    grad_query_low = swap_blocks(
        jnp.concatenate(grad_query_parts, axis=0).reshape(seq_len, width_local).astype(BF)
    )
    grad_key_low = swap_blocks(grad_keys.reshape(seq_len, width_local).astype(BF))
    grad_value_low = swap_blocks(grad_values.reshape(seq_len, width_local).astype(BF))
    delta_query_up = product_rows(rank_query, grad_query_low)
    delta_key_up = product_rows(rank_key, grad_key_low)
    delta_value_up = product_rows(rank_value, grad_value_low)
    grad_rank_one = jnp.concatenate(
        [
            product_cols(grad_query_low, lift_query),
            product_cols(grad_key_low, lift_key),
            product_cols(grad_value_low, lift_value),
        ],
        axis=1,
    ).astype(BF)
    grad_rows_one = (
        beside(
            out_of(
                grad_value_low,
                weight_vo,
                0,
                width_local,
                out_of(
                    jnp.concatenate([grad_query_low, grad_key_low], axis=1),
                    weight_qk,
                    0,
                    2 * width_local,
                ),
            )
        )
        + product(grad_rank_one, down_qkv)
    )
    delta_qkv_down = product_rows(grad_rank_one, full_one)
    grad_norm_one = reduce_rows(grad_rows_one)
    input_delta = natural(
        (grad_residual + norm_back(grad_norm_one, gain_a, unit_one, scale_one)).astype(BF)
    )
    (query_down_out, key_down_out, value_down_out), (
        query_up_out,
        key_up_out,
        value_up_out,
    ) = settle(
        [
            delta_qkv_down[:rank_width],
            delta_qkv_down[rank_width : 2 * rank_width],
            delta_qkv_down[2 * rank_width :],
        ],
        [delta_query_up, delta_key_up, delta_value_up],
    )
    return (
        output,
        input_delta,
        query_down_out,
        query_up_out,
        key_down_out,
        key_up_out,
        value_down_out,
        value_up_out,
        output_down_out,
        output_up_out,
        expand_down_out,
        expand_up_out,
        shrink_down_out,
        shrink_up_out,
    )


def solution(mesh):
    rows = P(("dp", "tensor"), None)
    tree = P("dp", None)
    whole = P()
    slim = P(None, None, "tensor")
    inward = P("dp", "tensor")
    outward = P("tensor", "dp")
    return jax.shard_map(
        functools.partial(shards, mesh.shape["dp"]),
        mesh=mesh,
        in_specs=(
            rows,
            rows,
            tree,
            tree,
            P("dp"),
            whole,
            whole,
            whole,
            whole,
            inward,
            inward,
            inward,
            outward,
            inward,
            outward,
            P("tensor"),
            P("tensor"),
            whole,
            P("tensor"),
            whole,
            whole,
            slim,
            whole,
            slim,
            whole,
            slim,
            slim,
            whole,
            whole,
            slim,
            slim,
            whole,
        ),
        out_specs=(
            rows,
            rows,
            whole,
            slim,
            whole,
            slim,
            whole,
            slim,
            slim,
            whole,
            whole,
            slim,
            slim,
            whole,
        ),
        check_vma=False,
    )
```

time: 1360 us -> 690 us (0.51)
  waiting for transfers between devices: 1060 us -> 211 us
  other arithmetic: 27.6 us -> 91.6 us
  local copies, waits for them, and re-layouts: 26.3 us -> 82.6 us
  starting transfers between devices: 1.52 us -> 51 us
  matrix products: 194 us -> 223 us
  blocking collectives: 25.6 us -> 0 us
    all_gather x10 -> x6, waiting for transfers between devices: 488 us -> 55.5 us  [the longest x5 55.5 us: fetch(): lax.all_gather(shard, 'dp', axis=0, tiled=True, axis_index_groups=line_gr...]
    psum x2 -> x0, waiting for transfers between devices: 293 us -> none  [the longest x1 165 us: shards(): lax.psum((spread(delta_qkv_down[:rank_width]), spread(delta_qkv_down[rank...]
    reduce_scatter x8 -> x0, waiting for transfers between devices: 279 us -> none  [the longest x1 74.4 us: shards(): lax.psum_scatter(main_part, 'tensor', scatter_dimension=0, tiled=True)]
    ppermute x0 -> x48, waiting for transfers between devices: none -> 156 us  [the longest x12 80.2 us: to_chip(): return lax.ppermute(v, 'tensor', chip_pairs)]
    ppermute x0 -> x48, starting transfers between devices: none -> 50.5 us  [the longest x22 20.1 us: to_core(): return lax.ppermute(v, 'tensor', core_pairs)]
    dot_general x18 -> x40, matrix products: 61.1 us -> 92.3 us  [product_cols(): lax.dot_general(left, right, (((1,), (1,)), ((), ())), preferred_element_...]
    unnamed x242 -> x455, local copies, waits for them, and re-layouts: 25.5 us -> 55.3 us
    all_gather x4 -> x0, blocking collectives: 25.6 us -> none  [the longest x1 7.26 us: shards(): lax.all_gather(rank_two, 'tensor', axis=0, tiled=True)]
  transfers between devices with their start and end apart: 20 -> 54, of which waited for: 18 -> 20; matrix products, arithmetic and copies ran while one was open for 13% -> 47% of each run, Pallas kernels for 0% -> 0%
where the time goes in v1:
time: 690 us; the launch traced here: 678 us
  matrix products  223 us (32%)
  waiting for transfers between devices  211 us (31%)
  other arithmetic  91.6 us (13%)
  local copies, waits for them, and re-layouts  82.6 us (12%)
  starting transfers between devices  51 us (7%)
  between operations  18.8 us (3%)
    dot_general x40, matrix products, product_cols(): lax.dot_general(left, right, (((1,), (1,)), ((), ())), preferred_element_...  92.3 us
    dot_general x39, matrix products, product(): return jnp.dot(left, right, preferred_element_type=F32)  82.6 us
    ppermute x12, waiting for transfers between devices, to_chip(): return lax.ppermute(v, 'tensor', chip_pairs)  80.2 us
    all_gather x5, waiting for transfers between devices, fetch(): lax.all_gather(shard, 'dp', axis=0, tiled=True, axis_index_groups=line_gr...  55.5 us
    unnamed x455, local copies, waits for them, and re-layouts  55.3 us
    ppermute x5, waiting for transfers between devices, fetch(): return (own, lax.ppermute(own, 'dp', dp_pairs), 0)  40.9 us
    ppermute x6, waiting for transfers between devices, settle(): lax.ppermute(pair, 'dp', [(i, (i + 2 * s) % dp_size) for i in range(dp_si...  29.6 us
    unnamed x104, other arithmetic  21.4 us
  transfers between devices with their start and end apart: 54, of which 20 were waited for; matrix products, arithmetic and copies ran while one was open for 47% of the time, Pallas kernels for 0%

profile of v1, /device:TPU:17, one launch (start us, length us, event | category | flops | bytes accessed | tf_op | source)
XLA Modules:
  0.0 678.0 jit_solution(3562624718631702198)
XLA Ops:
  49.0 13.2 %all-gather.7.cloned.1.call-done = bf16[1024,1024]{1,0:T(8,128)(2,1)} async-done(((bf16[256,1024]{1,0:T(8,128)(2,1)}), bf16[1024,1024]{1,0:T(8,128)(2,1)}) %all-gather.7.cloned.1.call-update) | async-done | bytes 2097168 | tf_op jit(solution)/shard_map/all_gather | solution.py:158
  81.7 28.3 %all-gather.11.cloned.1.call-done = bf16[1024,1024]{0,1:T(8,128)(2,1)} async-done(((bf16[256,1024]{0,1:T(8,128)(2,1)}), bf16[1024,1024]{0,1:T(8,128)(2,1)}) %all-gather.11.cloned.1.call-update) | async-done | bytes 2097168 | tf_op jit(solution)/shard_map/all_gather | solution.py:158
  112.2 4.7 fusion.103
  116.9 4.1 fusion.113
  137.0 3.3 copy-done.2
  142.7 13.9 %all-gather.9.cloned.1.call-done = bf16[1024,1024]{0,1:T(8,128)(2,1)} async-done(((bf16[256,1024]{0,1:T(8,128)(2,1)}), bf16[1024,1024]{0,1:T(8,128)(2,1)}) %all-gather.9.cloned.1.call-update) | async-done | bytes 2097168 | tf_op jit(solution)/shard_map/all_gather | solution.py:158
  156.6 11.8 %collective-permute-done.3 = bf16[1024,1024]{0,1:T(8,128)(2,1)} collective-permute-done((bf16[1024,1024]{0,1:T(8,128)(2,1)}, bf16[1024,1024]{0,1:T(8,128)(2,1)}, u32[]{:S(2)}, u32[]{:S(2)}) %collective-permute-start.3) | collective-permute-done | bytes 2097184 | tf_op jit(solution)/shard_map/ppermute | solution.py:159
  205.9 14.4 %collective-permute-done.7 = bf16[256,2048]{0,1:T(8,128)(2,1)} collective-permute-done((bf16[256,2048]{0,1:T(8,128)(2,1)}, bf16[256,2048]{0,1:T(8,128)(2,1)}, u32[]{:S(2)}, u32[]{:S(2)}) %collective-permute-start.7) | collective-permute-done | bytes 1048608 | tf_op jit(solution)/shard_map/ppermute | solution.py:101
  220.3 3.5 fusion.68
  238.9 13.4 %collective-permute-done.9 = bf16[256,2048]{0,1:T(8,128)(2,1)} collective-permute-done((bf16[256,2048]{0,1:T(8,128)(2,1)}, bf16[256,2048]{0,1:T(8,128)(2,1)}, u32[]{:S(2)}, u32[]{:S(2)}) %collective-permute-start.9) | collective-permute-done | bytes 1048608 | tf_op jit(solution)/shard_map/ppermute | solution.py:101
  260.8 4.5 fusion.63
  269.1 3.3 fusion.99
  281.3 25.7 %collective-permute-done.15 = bf16[1024,1024]{0,1:T(8,128)(2,1)} collective-permute-done((bf16[1024,1024]{0,1:T(8,128)(2,1)}, bf16[1024,1024]{0,1:T(8,128)(2,1)}, u32[]{:S(2)}, u32[]{:S(2)}) %collective-permute-start.15) | collective-permute-done | bytes 2097184 | tf_op jit(solution)/shard_map/ppermute | solution.py:159
  319.2 3.2 fusion.207
  325.6 4.5 fusion.204
  330.5 4.6 fusion.216
  338.3 3.2 fusion.214
  341.5 4.5 fusion.198
  346.0 4.6 fusion.210
  360.6 3.3 fusion.195
  363.9 3.3 fusion.75
  375.6 3.5 fusion.177
  380.6 4.6 add_add_fusion.1
  385.4 5.4 add_add_fusion
  390.7 3.3 fusion.396
  397.8 3.3 fusion.188
  401.4 5.6 add_add_fusion.3
  409.7 4.5 fusion.173
  414.5 6.4 add_add_fusion.2
  420.9 12.1 %collective-permute-done.23 = bf16[256,2048]{0,1:T(8,128)(2,1)} collective-permute-done((bf16[256,2048]{0,1:T(8,128)(2,1)}, bf16[256,2048]{0,1:T(8,128)(2,1)}, u32[]{:S(2)}, u32[]{:S(2)}) %collective-permute-start.23) | collective-permute-done | bytes 1048608 | tf_op jit(solution)/shard_map/ppermute | solution.py:101
  442.1 4.5 fusion.376
  448.4 13.1 %collective-permute-done.25 = bf16[256,2048]{0,1:T(8,128)(2,1)} collective-permute-done((bf16[256,2048]{0,1:T(8,128)(2,1)S(1)}, bf16[256,2048]{0,1:T(8,128)(2,1)}, u32[]{:S(2)}, u32[]{:S(2)}) %collective-permute-start.25) | collective-permute-done | bytes 1048608 | tf_op jit(solution)/shard_map/ppermute | solution.py:101
  494.1 5.3 multiply_reduce_fusion
  514.4 3.9 fusion.367
  522.5 4.0 convolution_add_fusion.1
  526.6 4.0 fusion.397
  543.5 5.2 collective-permute-done.32
  554.2 8.8 %collective-permute-done.34 = bf16[2,16,3200]{2,1,0:T(8,128)(2,1)S(1)} collective-permute-done((bf16[2,16,3200]{2,1,0:T(8,128)(2,1)S(1)}, bf16[2,16,3200]{2,1,0:T(8,128)(2,1)S(1)}, u32[]{:S(2)}, u32[]{:S(2)}) %collective-permute-start.34) | collective-permute-done | bytes 204832 | tf_op jit(solution)/shard_map/ppermute | solution.py:414
  563.0 4.6 collective-permute-start.42
  571.6 5.8 collective-permute-done.42
  579.3 9.3 %collective-permute-done.43 = bf16[2,16,6272]{2,1,0:T(8,128)(2,1)} collective-permute-done((bf16[2,16,6272]{2,1,0:T(8,128)(2,1)}, bf16[2,16,6272]{2,1,0:T(8,128)(2,1)}, u32[]{:S(2)}, u32[]{:S(2)}) %collective-permute-start.43) | collective-permute-done | bytes 401440 | tf_op jit(solution)/shard_map/ppermute | solution.py:414
  588.6 7.0 %collective-permute-start.36 = (bf16[8,16,1536]{2,0,1:T(8,128)(2,1)S(1)}, bf16[8,16,1536]{2,0,1:T(8,128)(2,1)S(1)}, u32[]{:S(2)}, u32[]{:S(2)}) collective-permute-start(bf16[8,16,1536]{2,0,1:T(8,128)(2,1)S(1)} %slice.2401), channel_id=1, source_target_pairs={{0,2},{2,0},{1,3},{3,1},{4,6},{6,4},{5,7},{7,5},{8,10},{10,8},{9,1... | collective-permute-start | bytes 1179656 | tf_op jit(solution)/shard_map/ppermute | solution.py:101
  597.4 4.1 collective-permute-done.44
  601.5 3.6 collective-permute-start.38
  609.5 3.3 fusion.118
  621.7 7.3 %collective-permute-done.45 = bf16[8,16,1536]{2,0,1:T(8,128)(2,1)S(1)} collective-permute-done((bf16[8,16,1536]{2,0,1:T(8,128)(2,1)S(1)}, bf16[8,16,1536]{2,0,1:T(8,128)(2,1)S(1)}, u32[]{:S(2)}, u32[]{:S(2)}) %collective-permute-start.45) | collective-permute-done | bytes 393248 | tf_op jit(solution)/shard_map/ppermute | solution.py:101
  642.5 18.2 %collective-permute-done.29 = bf16[256,2048]{0,1:T(8,128)(2,1)S(1)} collective-permute-done((bf16[256,2048]{0,1:T(8,128)(2,1)S(1)}, bf16[256,2048]{0,1:T(8,128)(2,1)S(1)}, u32[]{:S(2)}, u32[]{:S(2)}) %collective-permute-start.29) | collective-permute-done | bytes 1048608 | tf_op jit(solution)/shard_map/ppermute | solution.py:101
  663.3 4.2 fusion.19
  (901 shorter events, 319.3 us)
Async XLA Ops:
  7.2 55.0 %all-gather.7.cloned.1.call-start = ((), (), s32[]{:S(2)}) async-start(), calls=%async_computation | async-start | bytes 2621440 | tf_op jit(solution)/shard_map/all_gather | solution.py:158
  15.1 189.2 %collective-permute-start.13 = (bf16[256,2048]{0,1:T(8,128)(2,1)}, bf16[256,2048]{0,1:T(8,128)(2,1)}, u32[]{:S(2)}, u32[]{:S(2)}) collective-permute-start(bf16[256,2048]{0,1:T(8,128)(2,1)} %constant_dynamic-update-slice_fusion.37), channel_id=1, source_target_pairs={{0,2},{2,0},{1,3},{3,1},{4,6},{6,4},{5,7},{7,5},{8,10},{10,8},{9,1... | collective-permute-start | bytes 3145736 | tf_op jit(solution)/shard_map/ppermute | solution.py:101
  16.3 215.3 %collective-permute-start.12 = (bf16[256,2048]{0,1:T(8,128)(2,1)}, bf16[256,2048]{0,1:T(8,128)(2,1)}, u32[]{:S(2)}, u32[]{:S(2)}) collective-permute-start(bf16[256,2048]{0,1:T(8,128)(2,1)} %constant_dynamic-update-slice_fusion.37), channel_id=1, source_target_pairs={{0,1},{1,0},{2,3},{3,2},{4,5},{5,4},{6,7},{7,6},{8,9},{9,8},{10,11... | collective-permute-start | bytes 3145736 | tf_op jit(solution)/shard_map/ppermute | solution.py:98
  18.1 91.9 %all-gather.11.cloned.1.call-start = ((), (), s32[]{:S(2)}) async-start(), calls=%async_computation.2 | async-start | bytes 2621440 | tf_op jit(solution)/shard_map/all_gather | solution.py:158
  21.2 46.4 %collective-permute-start.1 = (bf16[256,2048]{0,1:T(8,128)(2,1)S(1)}, bf16[256,2048]{0,1:T(8,128)(2,1)}, u32[]{:S(2)}, u32[]{:S(2)}) collective-permute-start(bf16[256,2048]{0,1:T(8,128)(2,1)S(1)} %fusion.14), channel_id=1, source_target_pairs={{0,2},{2,0},{1,3},{3,1},{4,6},{6,4},{5,7},{7,5},{8,10},{10,8},{9,1... | collective-permute-start | bytes 3145736 | tf_op jit(solution)/shard_map/ppermute | solution.py:101
  21.5 54.0 %collective-permute-start = (bf16[256,2048]{0,1:T(8,128)(2,1)S(1)}, bf16[256,2048]{0,1:T(8,128)(2,1)}, u32[]{:S(2)}, u32[]{:S(2)}) collective-permute-start(bf16[256,2048]{0,1:T(8,128)(2,1)S(1)} %fusion.14), channel_id=1, source_target_pairs={{0,1},{1,0},{2,3},{3,2},{4,5},{5,4},{6,7},{7,6},{8,9},{9,8},{10,11... | collective-permute-start | bytes 3145736 | tf_op jit(solution)/shard_map/ppermute | solution.py:98
  22.9 133.8 %all-gather.9.cloned.1.call-start = ((), (), s32[]{:S(2)}) async-start(), calls=%async_computation.1 | async-start | bytes 2621440 | tf_op jit(solution)/shard_map/all_gather | solution.py:158
  62.2 161.6 %all-gather.13.cloned.1.call-start = ((), (), s32[]{:S(2)}) async-start(), calls=%async_computation.3 | async-start | bytes 2621440 | tf_op jit(solution)/shard_map/all_gather | solution.py:158
  65.5 46.7 %collective-permute-start.4 = (bf16[1024,1024]{1,0:T(8,128)(2,1)}, bf16[1024,1024]{1,0:T(8,128)(2,1)}, u32[]{:S(2)}, u32[]{:S(2)}) collective-permute-start(bf16[1024,1024]{1,0:T(8,128)(2,1)} %all-gather.7.cloned.1.call-done), channel_id=1, source_target_pairs={{0,4},{4,0},{8,12},{12,8},{16,20},{20,16},{24,28},{28,24},{1,5},{5... | collective-permute-start | bytes 6291464 | tf_op jit(solution)/shard_map/ppermute | solution.py:159
  67.6 8.2 %collective-permute-start.2 = (bf16[256,2048]{0,1:T(8,128)(2,1)}, bf16[256,2048]{0,1:T(8,128)(2,1)}, u32[]{:S(2)}, u32[]{:S(2)}) collective-permute-start(bf16[256,2048]{0,1:T(8,128)(2,1)} %collective-permute-done.1), channel_id=1, source_target_pairs={{0,1},{1,0},{2,3},{3,2},{4,5},{5,4},{6,7},{7,6},{8,9},{9,8},{10,11... | collective-permute-start | bytes 3145736 | tf_op jit(solution)/shard_map/ppermute | solution.py:98
  75.5 153.9 %collective-permute-start.17 = (bf16[256,1024]{0,1:T(8,128)(2,1)}, bf16[256,1024]{0,1:T(8,128)(2,1)}, u32[]{:S(2)}, u32[]{:S(2)}) collective-permute-start(bf16[256,1024]{0,1:T(8,128)(2,1)} %pad_maximum_fusion.18), channel_id=1, source_target_pairs={{0,4},{4,0},{8,12},{12,8},{16,20},{20,16},{24,28},{28,24},{1,5},{5... | collective-permute-start | bytes 1572872 | tf_op jit(solution)/shard_map/ppermute | solution.py:163
  110.1 155.2 %all-gather.15.cloned.1.call-start = ((), (), s32[]{:S(2)}) async-start(), calls=%async_computation.4 | async-start | bytes 2621440 | tf_op jit(solution)/shard_map/all_gather | solution.py:158
  110.1 58.3 %collective-permute-start.3 = (bf16[1024,1024]{0,1:T(8,128)(2,1)}, bf16[1024,1024]{0,1:T(8,128)(2,1)}, u32[]{:S(2)}, u32[]{:S(2)}) collective-permute-start(bf16[1024,1024]{0,1:T(8,128)(2,1)} %all-gather.11.cloned.1.call-done), channel_id=1, source_target_pairs={{0,4},{4,0},{8,12},{12,8},{16,20},{20,16},{24,28},{28,24},{1,5},{5... | collective-permute-start | bytes 6291464 | tf_op jit(solution)/shard_map/ppermute | solution.py:159
  186.6 7.3 %collective-permute-start.6 = (bf16[256,2048]{0,1:T(8,128)(2,1)S(1)}, bf16[256,2048]{0,1:T(8,128)(2,1)S(1)}, u32[]{:S(2)}, u32[]{:S(2)}) collective-permute-start(bf16[256,2048]{0,1:T(8,128)(2,1)S(1)} %get-tuple-element.163), channel_id=1, source_target_pairs={{0,1},{1,0},{2,3},{3,2},{4,5},{5,4},{6,7},{7,6},{8,9},{9,8},{10,11... | collective-permute-start | bytes 3145736 | tf_op jit(solution)/shard_map/ppermute | solution.py:98
  192.5 12.2 %collective-permute-start.5 = (bf16[256,2048]{0,1:T(8,128)(2,1)S(1)}, bf16[256,2048]{0,1:T(8,128)(2,1)S(1)}, u32[]{:S(2)}, u32[]{:S(2)}) collective-permute-start(bf16[256,2048]{0,1:T(8,128)(2,1)S(1)} %get-tuple-element.162), channel_id=1, source_target_pairs={{0,1},{1,0},{2,3},{3,2},{4,5},{5,4},{6,7},{7,6},{8,9},{9,8},{10,11... | collective-permute-start | bytes 3145736 | tf_op jit(solution)/shard_map/ppermute | solution.py:98
  195.3 25.0 %collective-permute-start.7 = (bf16[256,2048]{0,1:T(8,128)(2,1)}, bf16[256,2048]{0,1:T(8,128)(2,1)}, u32[]{:S(2)}, u32[]{:S(2)}) collective-permute-start(bf16[256,2048]{0,1:T(8,128)(2,1)} %fusion.67), channel_id=1, source_target_pairs={{0,2},{2,0},{1,3},{3,1},{4,6},{6,4},{5,7},{7,5},{8,10},{10,8},{9,1... | collective-permute-start | bytes 3145736 | tf_op jit(solution)/shard_map/ppermute | solution.py:101
  204.3 27.3 %collective-permute-start.14 = (bf16[256,2048]{0,1:T(8,128)(2,1)}, bf16[256,2048]{0,1:T(8,128)(2,1)}, u32[]{:S(2)}, u32[]{:S(2)}) collective-permute-start(bf16[256,2048]{0,1:T(8,128)(2,1)} %collective-permute-done.13), channel_id=1, source_target_pairs={{0,1},{1,0},{2,3},{3,2},{4,5},{5,4},{6,7},{7,6},{8,9},{9,8},{10,11... | collective-permute-start | bytes 3145736 | tf_op jit(solution)/shard_map/ppermute | solution.py:98
  204.6 159.2 %all-gather.17.cloned.1.call-start = ((), (), s32[]{:S(2)}) async-start(), calls=%async_computation.5 | async-start | bytes 5242880 | tf_op jit(solution)/shard_map/all_gather | solution.py:166
  204.7 56.1 %collective-permute-start.11 = (bf16[1024,1024]{0,1:T(8,128)(2,1)}, bf16[1024,1024]{0,1:T(8,128)(2,1)}, u32[]{:S(2)}, u32[]{:S(2)}) collective-permute-start(bf16[1024,1024]{0,1:T(8,128)(2,1)} %all-gather.9.cloned.1.call-done), channel_id=1, source_target_pairs={{0,4},{4,0},{8,12},{12,8},{16,20},{20,16},{24,28},{28,24},{1,5},{5... | collective-permute-start | bytes 6291464 | tf_op jit(solution)/shard_map/ppermute | solution.py:159
  228.2 24.2 %collective-permute-start.9 = (bf16[256,2048]{0,1:T(8,128)(2,1)}, bf16[256,2048]{0,1:T(8,128)(2,1)}, u32[]{:S(2)}, u32[]{:S(2)}) collective-permute-start(bf16[256,2048]{0,1:T(8,128)(2,1)} %add_convert_fusion.1), channel_id=1, source_target_pairs={{0,2},{2,0},{1,3},{3,1},{4,6},{6,4},{5,7},{7,5},{8,10},{10,8},{9,1... | collective-permute-start | bytes 3145736 | tf_op jit(solution)/shard_map/ppermute | solution.py:101
  237.8 27.7 %collective-permute-start.8 = (bf16[256,2048]{0,1:T(8,128)(2,1)}, bf16[256,2048]{0,1:T(8,128)(2,1)}, u32[]{:S(2)}, u32[]{:S(2)}) collective-permute-start(bf16[256,2048]{0,1:T(8,128)(2,1)} %add_convert_fusion.1), channel_id=1, source_target_pairs={{0,1},{1,0},{2,3},{3,2},{4,5},{5,4},{6,7},{7,6},{8,9},{9,8},{10,11... | collective-permute-start | bytes 3145736 | tf_op jit(solution)/shard_map/ppermute | solution.py:98
  252.4 13.1 %collective-permute-start.10 = (bf16[256,2048]{0,1:T(8,128)(2,1)}, bf16[256,2048]{0,1:T(8,128)(2,1)}, u32[]{:S(2)}, u32[]{:S(2)}) collective-permute-start(bf16[256,2048]{0,1:T(8,128)(2,1)} %collective-permute-done.9), channel_id=1, source_target_pairs={{0,1},{1,0},{2,3},{3,2},{4,5},{5,4},{6,7},{7,6},{8,9},{9,8},{10,11... | collective-permute-start | bytes 3145736 | tf_op jit(solution)/shard_map/ppermute | solution.py:98
  259.5 47.6 %collective-permute-start.15 = (bf16[1024,1024]{0,1:T(8,128)(2,1)}, bf16[1024,1024]{0,1:T(8,128)(2,1)}, u32[]{:S(2)}, u32[]{:S(2)}) collective-permute-start(bf16[1024,1024]{0,1:T(8,128)(2,1)} %all-gather.13.cloned.1.call-done), channel_id=1, source_target_pairs={{0,4},{4,0},{8,12},{12,8},{16,20},{20,16},{24,28},{28,24},{1,5},{5... | collective-permute-start | bytes 6291464 | tf_op jit(solution)/shard_map/ppermute | solution.py:159
  265.3 86.6 %collective-permute-start.16 = (bf16[1024,1024]{0,1:T(8,128)(2,1)}, bf16[1024,1024]{0,1:T(8,128)(2,1)S(1)}, u32[]{:S(2)}, u32[]{:S(2)}) collective-permute-start(bf16[1024,1024]{0,1:T(8,128)(2,1)} %all-gather.15.cloned.1.call-done), channel_id=1, source_target_pairs={{0,4},{4,0},{8,12},{12,8},{16,20},{20,16},{24,28},{28,24},{1,5},{5... | collective-permute-start | bytes 6291464 | tf_op jit(solution)/shard_map/ppermute | solution.py:159
  396.9 10.2 %collective-permute-start.22 = (bf16[256,2048]{0,1:T(8,128)(2,1)S(1)}, bf16[256,2048]{0,1:T(8,128)(2,1)S(1)}, u32[]{:S(2)}, u32[]{:S(2)}) collective-permute-start(bf16[256,2048]{0,1:T(8,128)(2,1)S(1)} %get-tuple-element.159), channel_id=1, source_target_pairs={{0,1},{1,0},{2,3},{3,2},{4,5},{5,4},{6,7},{7,6},{8,9},{9,8},{10,11... | collective-permute-start | bytes 3145736 | tf_op jit(solution)/shard_map/ppermute | solution.py:98
  401.4 19.5 %collective-permute-start.21 = (bf16[256,2048]{0,1:T(8,128)(2,1)}, bf16[256,2048]{0,1:T(8,128)(2,1)}, u32[]{:S(2)}, u32[]{:S(2)}) collective-permute-start(bf16[256,2048]{0,1:T(8,128)(2,1)} %get-tuple-element.158), channel_id=1, source_target_pairs={{0,1},{1,0},{2,3},{3,2},{4,5},{5,4},{6,7},{7,6},{8,9},{9,8},{10,11... | collective-permute-start | bytes 3145736 | tf_op jit(solution)/shard_map/ppermute | solution.py:98
  408.4 24.5 %collective-permute-start.23 = (bf16[256,2048]{0,1:T(8,128)(2,1)}, bf16[256,2048]{0,1:T(8,128)(2,1)}, u32[]{:S(2)}, u32[]{:S(2)}) collective-permute-start(bf16[256,2048]{0,1:T(8,128)(2,1)} %fusion.55), channel_id=1, source_target_pairs={{0,2},{2,0},{1,3},{3,1},{4,6},{6,4},{5,7},{7,5},{8,10},{10,8},{9,1... | collective-permute-start | bytes 3145736 | tf_op jit(solution)/shard_map/ppermute | solution.py:101
  437.9 23.5 %collective-permute-start.25 = (bf16[256,2048]{0,1:T(8,128)(2,1)S(1)}, bf16[256,2048]{0,1:T(8,128)(2,1)}, u32[]{:S(2)}, u32[]{:S(2)}) collective-permute-start(bf16[256,2048]{0,1:T(8,128)(2,1)S(1)} %fusion.366), channel_id=1, source_target_pairs={{0,2},{2,0},{1,3},{3,1},{4,6},{6,4},{5,7},{7,5},{8,10},{10,8},{9,1... | collective-permute-start | bytes 3145736 | tf_op jit(solution)/shard_map/ppermute | solution.py:101
  446.6 19.4 %collective-permute-start.19 = (bf16[256,2048]{0,1:T(8,128)(2,1)S(1)}, bf16[256,2048]{0,1:T(8,128)(2,1)S(1)}, u32[]{:S(2)}, u32[]{:S(2)}) collective-permute-start(bf16[256,2048]{0,1:T(8,128)(2,1)S(1)} %get-tuple-element.161), channel_id=1, source_target_pairs={{0,1},{1,0},{2,3},{3,2},{4,5},{5,4},{6,7},{7,6},{8,9},{9,8},{10,11... | collective-permute-start | bytes 3145736 | tf_op jit(solution)/shard_map/ppermute | solution.py:98
  448.3 20.4 %collective-permute-start.24 = (bf16[256,2048]{0,1:T(8,128)(2,1)S(1)}, bf16[256,2048]{0,1:T(8,128)(2,1)S(1)}, u32[]{:S(2)}, u32[]{:S(2)}) collective-permute-start(bf16[256,2048]{0,1:T(8,128)(2,1)S(1)} %fusion.366), channel_id=1, source_target_pairs={{0,1},{1,0},{2,3},{3,2},{4,5},{5,4},{6,7},{7,6},{8,9},{9,8},{10,11... | collective-permute-start | bytes 3145736 | tf_op jit(solution)/shard_map/ppermute | solution.py:98
  464.8 198.4 %collective-permute-start.18 = (bf16[256,2048]{0,1:T(8,128)(2,1)}, bf16[256,2048]{0,1:T(8,128)(2,1)}, u32[]{:S(2)}, u32[]{:S(2)}) collective-permute-start(bf16[256,2048]{0,1:T(8,128)(2,1)} %get-tuple-element.160), channel_id=1, source_target_pairs={{0,1},{1,0},{2,3},{3,2},{4,5},{5,4},{6,7},{7,6},{8,9},{9,8},{10,11... | collective-permute-start | bytes 3145736 | tf_op jit(solution)/shard_map/ppermute | solution.py:98
  467.4 195.8 %collective-permute-start.20 = (bf16[256,2048]{0,1:T(8,128)(2,1)}, bf16[256,2048]{0,1:T(8,128)(2,1)}, u32[]{:S(2)}, u32[]{:S(2)}) collective-permute-start(bf16[256,2048]{0,1:T(8,128)(2,1)} %fusion.58), channel_id=1, source_target_pairs={{0,2},{2,0},{1,3},{3,1},{4,6},{6,4},{5,7},{7,5},{8,10},{10,8},{9,1... | collective-permute-start | bytes 3145736 | tf_op jit(solution)/shard_map/ppermute | solution.py:101
  513.4 19.1 %collective-permute-start.30 = (bf16[96,512]{1,0:T(8,128)(2,1)S(1)}, bf16[96,512]{1,0:T(8,128)(2,1)S(1)}, u32[]{:S(2)}, u32[]{:S(2)}) collective-permute-start(bf16[96,512]{1,0:T(8,128)(2,1)S(1)} %pad_maximum_fusion.30), channel_id=1, source_target_pairs={{0,1},{1,0},{2,3},{3,2},{4,5},{5,4},{6,7},{7,6},{8,9},{9,8},{10,11... | collective-permute-start | bytes 294920 | tf_op jit(solution)/shard_map/ppermute | solution.py:98
  514.4 18.6 %collective-permute-start.39 = (bf16[96,512]{1,0:T(8,128)(2,1)S(1)}, bf16[96,512]{1,0:T(8,128)(2,1)S(1)}, u32[]{:S(2)}, u32[]{:S(2)}) collective-permute-start(bf16[96,512]{1,0:T(8,128)(2,1)S(1)} %pad_maximum_fusion.31), channel_id=1, source_target_pairs={{0,1},{1,0},{2,3},{3,2},{4,5},{5,4},{6,7},{7,6},{8,9},{9,8},{10,11... | collective-permute-start | bytes 294920 | tf_op jit(solution)/shard_map/ppermute | solution.py:98
  532.0 86.9 %collective-permute-start.28 = (bf16[256,2048]{0,1:T(8,128)(2,1)}, bf16[256,2048]{0,1:T(8,128)(2,1)}, u32[]{:S(2)}, u32[]{:S(2)}) collective-permute-start(bf16[256,2048]{0,1:T(8,128)(2,1)} %get-tuple-element.157), channel_id=1, source_target_pairs={{0,1},{1,0},{2,3},{3,2},{4,5},{5,4},{6,7},{7,6},{8,9},{9,8},{10,11... | collective-permute-start | bytes 3145736 | tf_op jit(solution)/shard_map/ppermute | solution.py:98
  541.3 8.1 %collective-permute-start.41 = (bf16[16,6272]{1,0:T(8,128)(2,1)S(1)}, bf16[16,6272]{1,0:T(8,128)(2,1)S(1)}, u32[]{:S(2)}, u32[]{:S(2)}) collective-permute-start(bf16[16,6272]{1,0:T(8,128)(2,1)S(1)} %get-tuple-element.283), channel_id=1, source_target_pairs={{0,4},{4,0},{8,12},{12,8},{16,20},{20,16},{24,28},{28,24},{1,5},{5... | collective-permute-start | bytes 602120 | tf_op jit(solution)/shard_map/ppermute | solution.py:412
  549.4 13.6 %collective-permute-start.34 = (bf16[2,16,3200]{2,1,0:T(8,128)(2,1)S(1)}, bf16[2,16,3200]{2,1,0:T(8,128)(2,1)S(1)}, u32[]{:S(2)}, u32[]{:S(2)}) collective-permute-start(bf16[2,16,3200]{2,1,0:T(8,128)(2,1)S(1)} %pad_maximum_fusion.22), channel_id=1, source_target_pairs={{0,16},{4,20},{8,24},{12,28},{16,0},{20,4},{24,8},{28,12},{1,17},{... | collective-permute-start | bytes 614408 | tf_op jit(solution)/shard_map/ppermute | solution.py:414
  553.4 14.2 %collective-permute-start.35 = (bf16[2,16,3200]{2,1,0:T(8,128)(2,1)S(1)}, bf16[2,16,3200]{2,1,0:T(8,128)(2,1)S(1)}, u32[]{:S(2)}, u32[]{:S(2)}) collective-permute-start(bf16[2,16,3200]{2,1,0:T(8,128)(2,1)S(1)} %pad_maximum_fusion.22), channel_id=1, source_target_pairs={{0,24},{4,28},{8,0},{12,4},{16,8},{20,12},{24,16},{28,20},{1,25},{... | collective-permute-start | bytes 614408 | tf_op jit(solution)/shard_map/ppermute | solution.py:414
  563.0 14.3 %collective-permute-start.42 = (bf16[2,16,6272]{2,1,0:T(8,128)(2,1)}, bf16[2,16,6272]{2,1,0:T(8,128)(2,1)}, u32[]{:S(2)}, u32[]{:S(2)}) collective-permute-start(bf16[2,16,6272]{2,1,0:T(8,128)(2,1)} %pad_maximum_fusion.21), channel_id=1, source_target_pairs={{0,8},{4,12},{8,16},{12,20},{16,24},{20,28},{24,0},{28,4},{1,9},{5... | collective-permute-start | bytes 1204232 | tf_op jit(solution)/shard_map/ppermute | solution.py:414
  567.7 20.9 %collective-permute-start.43 = (bf16[2,16,6272]{2,1,0:T(8,128)(2,1)}, bf16[2,16,6272]{2,1,0:T(8,128)(2,1)}, u32[]{:S(2)}, u32[]{:S(2)}) collective-permute-start(bf16[2,16,6272]{2,1,0:T(8,128)(2,1)} %pad_maximum_fusion.21), channel_id=1, source_target_pairs={{0,16},{4,20},{8,24},{12,28},{16,0},{20,4},{24,8},{28,12},{1,17},{... | collective-permute-start | bytes 1204232 | tf_op jit(solution)/shard_map/ppermute | solution.py:414
  577.3 24.2 %collective-permute-start.44 = (bf16[2,16,6272]{2,1,0:T(8,128)(2,1)}, bf16[2,16,6272]{2,1,0:T(8,128)(2,1)S(1)}, u32[]{:S(2)}, u32[]{:S(2)}) collective-permute-start(bf16[2,16,6272]{2,1,0:T(8,128)(2,1)} %pad_maximum_fusion.21), channel_id=1, source_target_pairs={{0,24},{4,28},{8,0},{12,4},{16,8},{20,12},{24,16},{28,20},{1,25},{... | collective-permute-start | bytes 1204232 | tf_op jit(solution)/shard_map/ppermute | solution.py:414
  588.6 29.8 %collective-permute-start.36 = (bf16[8,16,1536]{2,0,1:T(8,128)(2,1)S(1)}, bf16[8,16,1536]{2,0,1:T(8,128)(2,1)S(1)}, u32[]{:S(2)}, u32[]{:S(2)}) collective-permute-start(bf16[8,16,1536]{2,0,1:T(8,128)(2,1)S(1)} %slice.2401), channel_id=1, source_target_pairs={{0,2},{2,0},{1,3},{3,1},{4,6},{6,4},{5,7},{7,5},{8,10},{10,8},{9,1... | collective-permute-start | bytes 1179656 | tf_op jit(solution)/shard_map/ppermute | solution.py:101
  601.5 19.9 %collective-permute-start.38 = (bf16[8,16,1536]{2,0,1:T(8,128)(2,1)S(1)}, bf16[8,16,1536]{2,0,1:T(8,128)(2,1)}, u32[]{:S(2)}, u32[]{:S(2)}) collective-permute-start(bf16[8,16,1536]{2,0,1:T(8,128)(2,1)S(1)} %slice.2401), channel_id=1, source_target_pairs={{0,1},{1,0},{2,3},{3,2},{4,5},{5,4},{6,7},{7,6},{8,9},{9,8},{10,11... | collective-permute-start | bytes 1179656 | tf_op jit(solution)/shard_map/ppermute | solution.py:98
  618.4 10.7 %collective-permute-start.45 = (bf16[8,16,1536]{2,0,1:T(8,128)(2,1)S(1)}, bf16[8,16,1536]{2,0,1:T(8,128)(2,1)S(1)}, u32[]{:S(2)}, u32[]{:S(2)}) collective-permute-start(bf16[8,16,1536]{2,0,1:T(8,128)(2,1)S(1)} %slice.2400), channel_id=1, source_target_pairs={{0,2},{2,0},{1,3},{3,1},{4,6},{6,4},{5,7},{7,5},{8,10},{10,8},{9,1... | collective-permute-start | bytes 1179656 | tf_op jit(solution)/shard_map/ppermute | solution.py:101
  618.9 11.0 %collective-permute-start.37 = (bf16[8,16,1536]{2,0,1:T(8,128)(2,1)S(1)}, bf16[8,16,1536]{2,0,1:T(8,128)(2,1)S(1)}, u32[]{:S(2)}, u32[]{:S(2)}) collective-permute-start(bf16[8,16,1536]{2,0,1:T(8,128)(2,1)S(1)} %collective-permute-done.36), channel_id=1, source_target_pairs={{0,1},{1,0},{2,3},{3,2},{4,5},{5,4},{6,7},{7,6},{8,9},{9,8},{10,11... | collective-permute-start | bytes 1179656 | tf_op jit(solution)/shard_map/ppermute | solution.py:98
  621.5 21.1 %collective-permute-start.27 = (bf16[256,2048]{0,1:T(8,128)(2,1)S(1)}, bf16[256,2048]{0,1:T(8,128)(2,1)S(1)}, u32[]{:S(2)}, u32[]{:S(2)}) collective-permute-start(bf16[256,2048]{0,1:T(8,128)(2,1)S(1)} %copy-done.80), channel_id=1, source_target_pairs={{0,1},{1,0},{2,3},{3,2},{4,5},{5,4},{6,7},{7,6},{8,9},{9,8},{10,11... | collective-permute-start | bytes 3145736 | tf_op jit(solution)/shard_map/ppermute | solution.py:98
  629.1 7.5 %collective-permute-start.47 = (bf16[8,16,1536]{2,0,1:T(8,128)(2,1)S(1)}, bf16[8,16,1536]{2,0,1:T(8,128)(2,1)S(1)}, u32[]{:S(2)}, u32[]{:S(2)}) collective-permute-start(bf16[8,16,1536]{2,0,1:T(8,128)(2,1)S(1)} %slice.2400), channel_id=1, source_target_pairs={{0,1},{1,0},{2,3},{3,2},{4,5},{5,4},{6,7},{7,6},{8,9},{9,8},{10,11... | collective-permute-start | bytes 1179656 | tf_op jit(solution)/shard_map/ppermute | solution.py:98
  636.6 24.2 %collective-permute-start.29 = (bf16[256,2048]{0,1:T(8,128)(2,1)S(1)}, bf16[256,2048]{0,1:T(8,128)(2,1)S(1)}, u32[]{:S(2)}, u32[]{:S(2)}) collective-permute-start(bf16[256,2048]{0,1:T(8,128)(2,1)S(1)} %fusion.48), channel_id=1, source_target_pairs={{0,2},{2,0},{1,3},{3,1},{4,6},{6,4},{5,7},{7,5},{8,10},{10,8},{9,1... | collective-permute-start | bytes 3145736 | tf_op jit(solution)/shard_map/ppermute | solution.py:101
  (210 other events, 2108.5 us)
Sparse Core Ops, SparseCore 0:
  18.2 43.9 all-gather.6
  64.3 45.6 all-gather.10
  112.2 44.4 all-gather.8
  158.6 44.4 all-gather.12
  205.1 44.4 all-gather.14
  259.6 79.3 all-gather.16

commit v2 on v1

v2 whole, which is shorter than its diff:
```python
import functools

import jax
import jax.numpy as jnp
from jax import lax
from jax.experimental import pallas as pl
from jax.experimental.pallas import tpu as pltpu
from jax.sharding import PartitionSpec as P

HEAD_DIM = 128
SEGS = 13
BF = jnp.bfloat16
F32 = jnp.float32


def ancestry(parents):
    seg_range = jnp.arange(SEGS, dtype=jnp.int32)
    current = seg_range
    ancestors = current[:, None] == seg_range[None, :]
    for hop_index in range(SEGS - 1):
        current = jnp.sum(
            jnp.where(current[:, None] == seg_range[None, :], parents[None, :], 0), axis=1
        )
        ancestors = jnp.logical_or(ancestors, current[:, None] == seg_range[None, :])
    return ancestors


def product(left, right):
    return jnp.dot(left, right, preferred_element_type=F32)


def product_cols(left, right):
    return lax.dot_general(
        left, right, (((1,), (1,)), ((), ())), preferred_element_type=F32
    )


def product_rows(left, right):
    return lax.dot_general(
        left, right, (((0,), (0,)), ((), ())), preferred_element_type=F32
    )


def feed_kernel(first, last, pieces, *refs):
    rows, cots, rank_in, rank_grad, lift, bias, down = refs[:7]
    weights, refs = refs[7 : 7 + pieces], refs[7 + pieces :]
    if not first:
        main_in, grad_in, rank_main_in, rank_back_in = refs[:4]
        refs = refs[4:]
    if last:
        lift_after, down_before = refs[:2]
        refs = refs[2:]
    mains, grads = refs[: len(refs) // 2 - 2], refs[len(refs) // 2 - 2 : -4]
    rank_main, rank_back, down_delta, up_delta = refs[-4:]
    chunk = lift.shape[1]
    parts, at = [], 0
    for weight in weights:
        parts.append((slice(at, at + weight.shape[0]), weight))
        at += weight.shape[0]

    pre_act = (
        sum(product(rows[:, here], weight[:, :chunk]) for here, weight in parts)
        + product(rank_in[...], lift[...])
        + bias[...]
    )
    grad_hidden = sum(
        product(cots[:, here], weight[:, chunk:]) for here, weight in parts
    ) + product(rank_grad[...], down[...])
    bell = 0.5 * (1.0 + lax.erf(pre_act * (0.5**0.5)))
    slope = bell + pre_act * jnp.exp(-0.5 * pre_act * pre_act) * (0.5 / jnp.pi) ** 0.5
    hidden = (pre_act * bell).astype(BF)
    grad_pre = (grad_hidden * slope).astype(BF)

    main_rank = product_cols(hidden, down[...])
    back_rank = product_cols(grad_pre, lift[...])
    if not first:
        main_rank = main_rank + rank_main_in[...]
        back_rank = back_rank + rank_back_in[...]
    rank_main[...] = main_rank
    rank_back[...] = back_rank
    for here, weight in parts:
        ahead = product_cols(hidden, weight[:, chunk:])
        back = product_cols(grad_pre, weight[:, :chunk])
        if not first:
            ahead = ahead + main_in[:, here]
            back = back + grad_in[:, here]
        if last:
            ahead = ahead + product(main_rank.astype(BF), lift_after[:, here])
            back = back + product(back_rank.astype(BF), down_before[:, here])
        for k, (main, grad) in enumerate(zip(mains, grads)):

            @pl.when((pl.program_id(0) == k) | (len(mains) == 1))
            def _(main=main, grad=grad, here=here, ahead=ahead, back=back):
                main[:, here] = ahead.astype(main.dtype)
                grad[:, here] = back.astype(grad.dtype)

    down_part = product_rows(rank_grad[...], hidden)
    up_part = product_rows(rank_in[...], grad_pre)

    @pl.when(pl.program_id(0) == 0)
    def _():
        down_delta[...] = down_part
        up_delta[...] = up_part

    @pl.when(pl.program_id(0) > 0)
    def _():
        down_delta[...] += down_part
        up_delta[...] += up_part


def feed_forward(rows, cots, rank_in, rank_grad, weight, lift, bias, down, at, before, final, span):
    tile = 256
    feats = rows.shape[1]
    chunk = bias.shape[0]
    rank = lift.shape[0]
    begin, count = span[0] // tile, (span[1] - span[0]) // tile
    first, last = before is None, final is not None

    def row_block(width):
        return pl.BlockSpec((tile, width), lambda i: (begin + i, 0))

    def out_block(width):
        return pl.BlockSpec((tile, width), lambda i: (i, 0))

    def fixed(shape, column=0):
        return pl.BlockSpec(shape, lambda i: (0, column), pipeline_mode=pl.Buffered(1))

    args = [rows, cots, rank_in, rank_grad, lift, bias[None], down]
    specs = [
        row_block(feats),
        row_block(feats),
        row_block(rank),
        row_block(rank),
        fixed((rank, chunk), at),
        fixed((1, chunk), 0),
        fixed((rank, chunk), at),
    ]
    for piece, column in weight:
        args.append(piece)
        specs.append(fixed((piece.shape[0], 2 * chunk), column))
    if not first:
        args += [before[0][0], before[1][0], before[2], before[3]]
        specs += [row_block(feats), row_block(feats), row_block(rank), row_block(rank)]
    if last:
        args += list(final)
        specs += [fixed((rank, feats)), fixed((rank, feats))]
    size = span[1] - span[0]
    flops = size * feats * chunk
    if last:
        wide_specs = [fixed((tile, feats))] * (2 * count)
        wide_shapes = [jax.ShapeDtypeStruct((tile, feats), BF)] * (2 * count)
    else:
        wide_specs = [out_block(feats)] * 2
        wide_shapes = [jax.ShapeDtypeStruct((size, feats), F32)] * 2
    results = pl.pallas_call(
        functools.partial(feed_kernel, first, last, len(weight)),
        grid=(count,),
        in_specs=specs,
        out_specs=wide_specs
        + [
            out_block(rank),
            out_block(rank),
            pl.BlockSpec((rank, chunk), lambda i: (0, 0)),
            pl.BlockSpec((rank, chunk), lambda i: (0, 0)),
        ],
        out_shape=wide_shapes
        + [
            jax.ShapeDtypeStruct((size, rank), F32),
            jax.ShapeDtypeStruct((size, rank), F32),
            jax.ShapeDtypeStruct((rank, chunk), F32),
            jax.ShapeDtypeStruct((rank, chunk), F32),
        ],
        cost_estimate=pl.CostEstimate(
            flops=flops, bytes_accessed=size * feats * 20, transcendentals=size * chunk * 2
        ),
        name="feed_forward",
    )(*args)
    wide = len(wide_specs) // 2
    return results[:wide], results[wide : 2 * wide], *results[2 * wide :]


def attend_kernel(scale, turn, *refs):
    count = (len(refs) - 3) // 3
    query, key, value = refs[:count], refs[count : 2 * count], refs[2 * count : 3 * count]
    bias, attended, level = refs[3 * count :]
    rows = query[0].shape[0]
    for i in range(count):
        here = slice(i * rows, (i + 1) * rows)
        scores = [
            product_cols(query[i][...], key[j][...]) * scale
            + bias[here, j * rows : (j + 1) * rows]
            for j in range(i + 1)
        ]
        top = functools.reduce(
            jnp.maximum, [jnp.max(v, axis=-1, keepdims=True) for v in scores]
        )
        raised = [jnp.exp(v - top) for v in scores]
        total = sum(jnp.sum(v, axis=-1, keepdims=True) for v in raised)
        share = 1.0 / total
        mixed = sum(
            product((v * share).astype(BF), value[j][...]) for j, v in enumerate(raised)
        )
        to = pl.multiple_of((i ^ turn[0]) * rows, rows)
        attended[pl.ds(to, rows), :] = mixed.astype(BF)
        level[here, :] = jnp.broadcast_to(top + jnp.log(total), (rows, level.shape[1]))


def attend_back_kernel(scale, turn, *refs):
    count = (len(refs) - 7) // 4 if len(refs) % 4 == 3 else (len(refs) - 10) // 4
    query, key, value, grad = (refs[n * count : (n + 1) * count] for n in range(4))
    bias, level = refs[4 * count : 4 * count + 2]
    grad_query, grad_key, grad_value, key_sum, value_sum = refs[-5:]
    rows = query[0].shape[0]
    for i in range(count):
        here = slice(i * rows, (i + 1) * rows)
        row_level = level[here, :1]
        probs = [
            jnp.exp(
                product_cols(query[i][...], key[j][...]) * scale
                + bias[here, j * rows : (j + 1) * rows]
                - row_level
            )
            for j in range(i + 1)
        ]
        grad_probs = [product_cols(grad[i][...], value[j][...]) for j in range(i + 1)]
        mean = sum(
            jnp.sum(p * g, axis=-1, keepdims=True) for p, g in zip(probs, grad_probs)
        )
        query_sum = 0.0
        for j in range(i + 1):
            there = slice(j * rows, (j + 1) * rows)
            grad_score = (probs[j] * (grad_probs[j] - mean)).astype(BF)
            query_sum = query_sum + product(grad_score, key[j][...])
            key_part = product_rows(grad_score, query[i][...])
            value_part = product_rows(probs[j].astype(BF), grad[i][...])
            if i > j:
                key_part = key_part + key_sum[there, :]
                value_part = value_part + value_sum[there, :]
            key_sum[there, :] = key_part
            value_sum[there, :] = value_part
        to = pl.multiple_of((i ^ turn[0]) * rows, rows)
        grad_query[pl.ds(to, rows), :] = (query_sum * scale).astype(BF)
    for j in range(count):
        there = slice(j * rows, (j + 1) * rows)
        to = pl.multiple_of((j ^ turn[0]) * rows, rows)
        grad_key[pl.ds(to, rows), :] = (key_sum[there, :] * scale).astype(BF)
        grad_value[pl.ds(to, rows), :] = value_sum[there, :].astype(BF)


def by_head(kernel, turn, blocked, whole, outs, scratch, heads, name, before=()):
    first, count = heads
    seq_len, width = blocked[0].shape
    blocks = 4
    rows = seq_len // blocks
    specs, args = [], []
    for v in blocked:
        for k in range(blocks):
            specs.append(
                pl.BlockSpec((rows, HEAD_DIM), lambda h, turn, k=k: (k ^ turn[0], first + h))
            )
            args.append(v)
    for v in whole:
        if v.shape[1] == seq_len:
            specs.append(
                pl.BlockSpec(v.shape, lambda h, turn: (0, 0), pipeline_mode=pl.Buffered(1))
            )
        else:
            specs.append(pl.BlockSpec((seq_len, HEAD_DIM), lambda h, turn: (0, first + h)))
        args.append(v)
    aliases = {1 + len(args) + n: n for n in range(len(before))}
    specs += [pl.BlockSpec(memory_space=pl.ANY)] * len(before)
    args += before
    return pl.pallas_call(
        functools.partial(kernel, HEAD_DIM ** (-0.5)),
        grid_spec=pltpu.PrefetchScalarGridSpec(
            num_scalar_prefetch=1,
            grid=(count,),
            in_specs=specs,
            out_specs=[pl.BlockSpec((seq_len, HEAD_DIM), lambda h, turn: (0, first + h))] * len(outs),
            scratch_shapes=scratch,
        ),
        out_shape=[jax.ShapeDtypeStruct((seq_len, width), t) for t in outs],
        input_output_aliases=aliases,
        cost_estimate=pl.CostEstimate(flops=10**8, bytes_accessed=10**6, transcendentals=0),
        name=name,
    )(turn, *args)


def back_kernel(query, key, value, rank, qk_own, qk_other, vo_own, vo_other, down, *outs):
    width = query.shape[1]
    half = qk_own.shape[0]
    for at, qk, vo in ((0, qk_own, vo_own), (half, qk_other, vo_other)):
        rows = (
            product_cols(query[...], qk[:, :width])
            + product_cols(key[...], qk[:, width:])
            + product_cols(value[...], vo[...])
            + product(rank[...], down[:, at : at + half])
        ).astype(BF)
        for k, out in enumerate(outs):

            @pl.when(pl.program_id(0) == k)
            def _(out=out, rows=rows, at=at):
                out[:, at : at + half] = rows


def back_rows(grads, weight_qk, weight_vo, down, tile, first):
    half, width = weight_vo[0].shape[0], grads[0].shape[1]

    def fixed(shape):
        return pl.BlockSpec(shape, lambda i: (0, 0), pipeline_mode=pl.Buffered(1))

    return pl.pallas_call(
        back_kernel,
        grid=(2,),
        in_specs=[pl.BlockSpec((tile, v.shape[1]), lambda i: (first - i, 0)) for v in grads]
        + [fixed((half, 2 * width))] * 2
        + [fixed((half, width))] * 2
        + [fixed(down.shape)],
        out_specs=[fixed((tile, down.shape[1]))] * 2,
        out_shape=[jax.ShapeDtypeStruct((tile, down.shape[1]), BF)] * 2,
        cost_estimate=pl.CostEstimate(flops=10**8, bytes_accessed=10**6, transcendentals=0),
        name="back_rows",
    )(*grads, *weight_qk[:2], *weight_vo[:2], down)


def flat_kernel(rank, *refs):
    base, near, far, *slim, marks, out = refs
    mine = (
        base[...].astype(F32) + near[...].astype(F32) + far[...].astype(F32)
    ).astype(BF)
    width = mine.shape[1]
    at = 0
    for k in range(mine.shape[0] // rank):
        out[:, at : at + width] = mine[k * rank : (k + 1) * rank]
        at += width
    for part in slim:
        out[:, at : at + part.shape[1]] = part[...].astype(BF)
        at += part.shape[1]
    out[:, at:] = marks[...]


def slots_kernel(slot_count, rank, *refs):
    tree_count = len(refs) - 4
    trees = jnp.concatenate([ref[...] for ref in refs[:tree_count]], axis=0)
    lanes = slot_count * rank
    width = trees.shape[1] - lanes
    source = lax.broadcasted_iota(jnp.int32, (lanes, lanes), 0)
    target = lax.broadcasted_iota(jnp.int32, (lanes, lanes), 1)
    spread = jnp.where(source == target // rank, 1.0, 0.0).astype(BF)
    marks = product(trees[:, width:], spread)
    row = lax.broadcasted_iota(jnp.int32, marks.shape, 0)
    lane = lax.broadcasted_iota(jnp.int32, marks.shape, 1)
    marks = jnp.where(row % rank == lane % rank, marks, 0.0).astype(BF)
    at = 0
    for out in refs[tree_count:]:
        size = out.shape[1]
        out[...] = product_rows(marks, trees[:, at : at + size]).astype(out.dtype)
        at += size


def sum_slots(trees, slot_count, rank, wide, slim):
    rows = slot_count * rank
    wide_sum, *slim_sums = pl.pallas_call(
        functools.partial(slots_kernel, slot_count, rank),
        out_shape=[jax.ShapeDtypeStruct((rows, wide), BF)]
        + [jax.ShapeDtypeStruct((rows, n), F32) for n in slim],
        cost_estimate=pl.CostEstimate(
            flops=2 * rows * rows * (wide + sum(slim)),
            bytes_accessed=rows * (4 * wide + 6 * sum(slim)),
            transcendentals=0,
        ),
        name="sum_slots",
    )(*trees)
    return [v.reshape(slot_count, rank, -1) for v in (wide_sum, *slim_sums)]


def shards(
    dp_size,
    inputs,
    cotangent,
    segment_ids,
    parent_links,
    adapter_choice,
    gain_one,
    shift_one,
    gain_two,
    shift_two,
    query_weight,
    key_weight,
    value_weight,
    output_weight,
    expand_weight,
    shrink_weight,
    query_bias,
    value_bias,
    output_bias,
    expand_bias,
    shrink_bias,
    query_down,
    query_up,
    key_down,
    key_up,
    value_down,
    value_up,
    output_down,
    output_up,
    expand_down,
    expand_up,
    shrink_down,
    shrink_up,
):
    slot_count = query_down.shape[0]
    rank_width = query_down.shape[1]
    feats = inputs.shape[1]
    row_count = inputs.shape[0]
    width_local = query_weight.shape[1]
    hidden_local = expand_weight.shape[1]
    pair_count = dp_size // 2
    block = feats // dp_size
    half = feats // 2

    tensor_index = lax.axis_index("tensor")
    core_odd = (tensor_index % 2) == 1
    chip_odd = (tensor_index // 2) == 1
    dp_odd = (lax.axis_index("dp") % 2) == 1

    core_pairs = [(0, 1), (1, 0), (2, 3), (3, 2)]
    chip_pairs = [(0, 2), (2, 0), (1, 3), (3, 1)]
    dp_pairs = [(i, i ^ 1) for i in range(dp_size)]
    line_groups = [list(range(0, dp_size, 2)), list(range(1, dp_size, 2))]

    def to_core(v):
        return lax.ppermute(v, "tensor", core_pairs)

    def to_chip(v):
        return lax.ppermute(v, "tensor", chip_pairs)

    def own_first(v):
        parts = [v[..., b * block : (b + 1) * block] for b in range(dp_size)]
        pairs = [(parts[2 * p], parts[2 * p + 1]) for p in range(pair_count)]
        return jnp.concatenate(
            [jnp.where(dp_odd, odd, even) for even, odd in pairs]
            + [jnp.where(dp_odd, even, odd) for even, odd in pairs],
            axis=-1,
        )

    def natural(v):
        parts = [v[..., b * block : (b + 1) * block] for b in range(dp_size)]
        pairs = [(parts[p], parts[pair_count + p]) for p in range(pair_count)]
        return jnp.concatenate(
            [
                jnp.where(dp_odd, a, b)
                for own, other in pairs
                for a, b in ((other, own), (own, other))
            ],
            axis=-1,
        )

    def after(value, *others):
        return lax.optimization_barrier((value,) + others)[0]

    def gather_rows(rows, *held):
        near = to_core(rows)
        far = to_chip(rows)
        if held:
            far = after(far, *held)
        far_near = to_core(far)
        return jnp.concatenate([rows, near, far, far_near], axis=0)

    def reduce_rows(partial):
        parts = [partial[k * row_count : (k + 1) * row_count] for k in range(4)]
        far = parts[2] + to_core(parts[3].astype(BF)).astype(F32)
        far_sum = to_chip(far.astype(BF))
        near = parts[0] + to_core(parts[1].astype(BF)).astype(F32)
        return near + far_sum.astype(F32)

    def line_gather(shard, held):
        if held:
            shard = after(shard, *held)
        return lax.all_gather(shard, "dp", axis=0, tiled=True, axis_index_groups=line_groups)

    def fetch(shard, *held):
        own = line_gather(shard, held)
        return own, lax.ppermute(own, "dp", dp_pairs), 0

    def fetch_pieces(shard, *held):
        own = line_gather(shard, held)
        middle = own.shape[0] // 2
        swapped = [
            lax.ppermute(v, "dp", dp_pairs) for v in (own[:middle], own[middle:])
        ]
        return [(v, 0) for v in (own, *swapped)]

    def fetch_paired(pair, *held):
        both = line_gather(pair, held)
        return [(both, 0), (both, 1)]

    def into(left, weight, first, last):
        own, other, skip = weight
        return product(left[:, :half], own[:, first:last]) + product(
            left[:, half:], other[:, skip + first : skip + last]
        )

    def out_of(left, weight, first, last, base=None):
        own, other, skip = weight
        near = product_cols(left, own[:, first:last])
        far = product_cols(left, other[:, skip + first : skip + last])
        if base is not None:
            near, far = base[0] + near, base[1] + far
        return near, far

    def beside(pair):
        return jnp.concatenate(pair, axis=1)

    chunk_count = 4
    chunk = hidden_local // chunk_count
    output_turned = output_weight.T
    shrink_turned = shrink_weight.T
    def feed_shard(h):
        return jnp.concatenate(
            [
                expand_weight[:, h * chunk : (h + 1) * chunk],
                shrink_turned[:, h * chunk : (h + 1) * chunk],
            ],
            axis=1,
        )

    last_shard = feed_shard(chunk_count - 1)
    last_pair = jnp.concatenate([last_shard, lax.ppermute(last_shard, "dp", dp_pairs)], axis=1)
    weight_qk = fetch(jnp.concatenate([query_weight, key_weight], axis=1))
    weight_vo = fetch(jnp.concatenate([value_weight, output_turned], axis=1))
    weight_ffn, held = [], [weight_qk[0], weight_vo[0]]
    for h in range(chunk_count - 1):
        more = (last_pair,) if h == 0 else ()
        weight_ffn.append(fetch_pieces(feed_shard(h), held[h], *more))
        held.append(weight_ffn[-1][0][0])
    weight_ffn.append(fetch_paired(last_pair, held[-2]))

    select = (jnp.arange(slot_count, dtype=jnp.int32) == adapter_choice[0]).astype(BF)

    def adapter_of(adapter_table):
        return jnp.einsum(
            "a,ard->rd", select, adapter_table, preferred_element_type=F32
        ).astype(BF)

    down_qkv = own_first(
        jnp.concatenate(
            [adapter_of(query_down), adapter_of(key_down), adapter_of(value_down)], axis=0
        )
    )
    lift_query = adapter_of(query_up)
    lift_key = adapter_of(key_up)
    lift_value = adapter_of(value_up)
    down_output = adapter_of(output_down)
    lift_output = own_first(adapter_of(output_up))
    down_expand = own_first(adapter_of(expand_down))
    lift_expand = adapter_of(expand_up)
    down_shrink = adapter_of(shrink_down)
    lift_shrink = own_first(adapter_of(shrink_up))

    gain_a, shift_a = own_first(gain_one), own_first(shift_one)
    gain_b, shift_b = own_first(gain_two), own_first(shift_two)
    out_bias = own_first(output_bias)
    last_bias = own_first(shrink_bias)

    def normalize(values):
        row_mean = jnp.mean(values, axis=-1, keepdims=True)
        centred = values - row_mean
        row_var = jnp.mean(centred * centred, axis=-1, keepdims=True)
        scale = lax.rsqrt(row_var + 1e-05)
        return centred * scale, scale

    def norm_back(grad, gain, unit, scale):
        scaled = grad * gain
        return (
            scaled
            - jnp.mean(scaled, axis=-1, keepdims=True)
            - unit * jnp.mean(scaled * unit, axis=-1, keepdims=True)
        ) * scale

    inputs_wide = own_first(inputs).astype(F32)
    cot = own_first(cotangent)
    unit_one, scale_one = normalize(inputs_wide)
    rows_one = (unit_one * gain_a + shift_a).astype(BF)
    full_one = gather_rows(rows_one)
    full_cot = gather_rows(cot)
    seq_len = full_one.shape[0]
    head_count = width_local // HEAD_DIM

    rank_one = product_cols(full_one, down_qkv).astype(BF)
    rank_query = rank_one[:, :rank_width]
    rank_key = rank_one[:, rank_width : 2 * rank_width]
    rank_value = rank_one[:, 2 * rank_width :]
    query_key = into(after(full_one, weight_vo[0]), weight_qk, 0, 2 * width_local)
    queries = (query_key[:, :width_local] + product(rank_query, lift_query) + query_bias).astype(BF)
    keys_low = (query_key[:, width_local:] + product(rank_key, lift_key)).astype(BF)
    values_low = (
        into(after(full_one, held[2]), weight_vo, 0, width_local)
        + product(rank_value, lift_value)
        + value_bias
    ).astype(BF)
    seg_range = jnp.arange(SEGS, dtype=jnp.int32)
    seg_hot = (segment_ids[0][:, None] == seg_range[None, :]).astype(BF)
    path_hot = product(seg_hot, ancestry(parent_links[0]).astype(BF)).astype(BF)
    positions = jnp.arange(seq_len, dtype=jnp.int32)
    allowed = jnp.logical_and(
        product_cols(path_hot, seg_hot) > 0.5, positions[:, None] >= positions[None, :]
    )
    bias = jnp.where(allowed, 0.0, -1e30)
    turn = tensor_index.astype(jnp.int32).reshape(1)
    attended, level = by_head(
        attend_kernel,
        turn,
        [queries, keys_low, values_low],
        [bias],
        [BF, F32],
        [],
        (0, head_count),
        "attend",
    )
    attended = after(attended, weight_ffn[0][1][0])
    rank_out = product_cols(attended, down_output).astype(BF)
    main_rows = reduce_rows(
        beside(out_of(attended, weight_vo, width_local, 2 * width_local))
        + product(rank_out, lift_output)
    )
    main_rows = after(main_rows, weight_ffn[0][2][0], held[3])
    residual = inputs_wide + main_rows + out_bias
    unit_two, scale_two = normalize(residual)
    rows_two = (unit_two * gain_b + shift_b).astype(BF)
    full_two = after(gather_rows(rows_two, weight_ffn[1][1][0]), held[4])
    rank_two = product_cols(full_two, down_expand).astype(BF)
    rank_grad = product_cols(full_cot, lift_shrink).astype(BF)

    state = None
    down_parts, up_parts = [], []

    def feed(h, rows, span):
        last = h == chunk_count - 1
        results = feed_forward(
            rows,
            full_cot,
            rank_two,
            rank_grad,
            weight_ffn[h],
            lift_expand,
            expand_bias[h * chunk : (h + 1) * chunk],
            down_shrink,
            h,
            state,
            (lift_shrink, down_expand) if last else None,
            span,
        )
        return results[:4], results[4], results[5]

    for h in range(chunk_count - 1):
        state, down_part, up_part = feed(h, full_two, (0, seq_len))
        down_parts.append(down_part)
        up_parts.append(up_part)

    def far_part(two, three):
        return (two.astype(F32) + to_core(three).astype(F32)).astype(BF)

    def near_part(zero, one):
        return zero.astype(F32) + to_core(one).astype(F32)

    last = chunk_count - 1
    third, *third_deltas = feed(last, full_two, (3 * row_count, seq_len))
    second, *second_deltas = feed(
        last, after(full_two, third[1][0]), (2 * row_count, 3 * row_count)
    )
    grad_far = far_part(second[1][0], third[1][0])
    near, *near_deltas = feed(last, after(full_two, grad_far), (0, 2 * row_count))
    down_parts.append(third_deltas[0] + second_deltas[0] + near_deltas[0])
    up_parts.append(third_deltas[1] + second_deltas[1] + near_deltas[1])
    grad_rank_two = jnp.concatenate([near[3], second[3], third[3]], axis=0).astype(BF)
    rank_shrink = jnp.concatenate([near[2], second[2], third[2]], axis=0).astype(BF)
    far_arrived = to_chip(grad_far)
    grad_norm_two = near_part(near[1][0], after(near[1][1], far_arrived)) + far_arrived.astype(F32)
    grad_residual = cot.astype(F32) + norm_back(grad_norm_two, gain_b, unit_two, scale_two)
    grad_branch = grad_residual.astype(BF)

    branch_near = to_core(grad_branch)
    branch_far = to_chip(grad_branch)
    delta_shrink_up = product_rows(after(rank_shrink, grad_branch), full_cot)
    delta_expand_down = product_rows(after(grad_rank_two, grad_branch), full_two)
    main_far = far_part(after(second[0][0], grad_branch), after(third[0][0], grad_branch))
    main_near = near_part(*near[0])
    branch_held = after(branch_far, delta_shrink_up, delta_expand_down, main_far)
    full_branch = jnp.concatenate(
        [grad_branch, branch_near, branch_held, to_core(branch_held)], axis=0
    )
    rank_grad_out = product_cols(full_branch, lift_output).astype(BF)
    delta_output_up = product_rows(rank_out, full_branch)

    hot_lanes = (
        jnp.arange(128, dtype=jnp.int32)[None, :] == adapter_choice[0]
    ).astype(BF) * jnp.ones((rank_width, 1), BF)

    def by_tensor(parts):
        low = [jnp.where(core_odd, parts[1], parts[0]), jnp.where(core_odd, parts[0], parts[1])]
        high = [jnp.where(core_odd, parts[3], parts[2]), jnp.where(core_odd, parts[2], parts[3])]
        return [jnp.where(chip_odd, b, a) for a, b in zip(low + high, high + low)]

    quarter = feats // 4

    def settle_core(wide):
        stacked = natural(jnp.concatenate(wide, axis=0).astype(BF))
        parts = by_tensor([stacked[:, t * quarter : (t + 1) * quarter] for t in range(4)])
        near = to_core(jnp.concatenate([parts[1], parts[3]], axis=0))
        rows = stacked.shape[0]
        far = (parts[2].astype(F32) + near[rows:].astype(F32)).astype(BF)
        return parts[0], near[:rows], far

    def settle_flat(base, near, far, slim):
        parts = [base, near, to_chip(far), *slim, hot_lanes]
        rows = base.shape[0] // rank_width
        width = rows * quarter + sum(v.shape[1] for v in slim) + hot_lanes.shape[1]
        return pl.pallas_call(
            functools.partial(flat_kernel, rank_width),
            out_shape=jax.ShapeDtypeStruct((rank_width, width), BF),
            name="flatten",
        )(*parts)

    def settle_pair(flat):
        return jnp.concatenate([flat, lax.ppermute(flat, "dp", dp_pairs)], axis=0)

    def settle_line(pair):
        return [pair] + [
            lax.ppermute(pair, "dp", [(i, (i + 2 * s) % dp_size) for i in range(dp_size)])
            for s in range(1, pair_count)
        ]

    def settle_across(own, count):
        away = to_chip(own)
        across = by_tensor([own, to_core(own), away, to_core(away)])
        return [
            jnp.concatenate(
                [piece[:, :, k * quarter : (k + 1) * quarter] for piece in across], axis=-1
            ).astype(F32)
            for k in range(count)
        ]

    early_parts = settle_core([delta_shrink_up, delta_expand_down, delta_output_up])
    grad_attended = (
        into(after(full_branch, early_parts[0]), weight_vo, width_local, 2 * width_local)
        + product(rank_grad_out, down_output)
    ).astype(BF)
    delta_output_down = product_rows(rank_grad_out, attended)
    main_arrived = to_chip(after(main_far, early_parts[2], branch_far))

    def attend_back(grad, heads, before=()):
        return by_head(
            attend_back_kernel,
            turn,
            [queries, keys_low, values_low, grad],
            [bias, level],
            [BF, BF, BF],
            [pltpu.VMEM((seq_len, HEAD_DIM), F32)] * 2,
            heads,
            "attend_back",
            before,
        )

    grads = attend_back(after(grad_attended, early_parts[2]), (0, 1))
    early_flat = settle_flat(
        after(early_parts[0], grads[0]),
        *early_parts[1:],
        [*down_parts, *up_parts, delta_output_down],
    )
    early_pair = settle_pair(early_flat)
    grads = attend_back(after(grad_attended, early_flat), (1, 1), grads)
    early_trees = settle_line(after(early_pair, grads[0]))
    grads = attend_back(after(grad_attended, early_pair), (2, head_count - 2), grads)
    *grads, main_arrived = lax.optimization_barrier((*grads, main_arrived))
    grad_query_low, grad_key_low, grad_value_low = grads
    grad_rank_one = jnp.concatenate(
        [
            product_cols(grad_query_low, lift_query),
            product_cols(grad_key_low, lift_key),
            product_cols(grad_value_low, lift_value),
        ],
        axis=1,
    ).astype(BF)
    delta_qkv_down = product_rows(grad_rank_one, full_one)
    delta_query_up = product_rows(rank_query, grad_query_low)
    delta_key_up = product_rows(rank_key, grad_key_low)
    delta_value_up = product_rows(rank_value, grad_value_low)
    late_parts = settle_core(
        [
            delta_qkv_down[:rank_width],
            delta_qkv_down[rank_width : 2 * rank_width],
            delta_qkv_down[2 * rank_width :],
        ]
    )
    late_flat = settle_flat(*late_parts, [delta_query_up, delta_key_up, delta_value_up])
    def rows_back(first, *held):
        rank = after(grad_rank_one, *held) if held else grad_rank_one
        return back_rows(
            [grad_query_low, grad_key_low, grad_value_low, rank],
            weight_qk,
            weight_vo,
            down_qkv,
            row_count,
            first,
        )

    back_third, back_second = rows_back(3, late_parts[2])
    back_far = far_part(back_second, back_third)
    late_pair = settle_pair(late_flat)
    early_own, shrink_down_out, expand_up_out, output_down_out = sum_slots(
        [after(early_trees[0], late_flat), *early_trees[1:]],
        slot_count,
        rank_width,
        3 * quarter,
        [hidden_local, hidden_local, width_local],
    )
    late_trees = settle_line(after(late_pair, early_own))
    back_first, back_zero = rows_back(1, back_far, late_pair, early_own)
    back_arrived = to_chip(back_far)
    early_own = after(early_own, back_zero)
    shrink_up_out, expand_down_out, output_up_out = settle_across(early_own, 3)
    main_rows_two = main_near + main_arrived.astype(F32)
    output = natural((residual + main_rows_two + last_bias).astype(BF))
    grad_norm_one = near_part(back_zero, after(back_first, back_arrived)) + back_arrived.astype(F32)
    input_delta = natural(
        (grad_residual + norm_back(grad_norm_one, gain_a, unit_one, scale_one)).astype(BF)
    )
    late_own, query_up_out, key_up_out, value_up_out = sum_slots(
        [after(late_trees[0], back_arrived, shrink_up_out), *late_trees[1:]],
        slot_count,
        rank_width,
        3 * quarter,
        [width_local] * 3,
    )
    query_down_out, key_down_out, value_down_out = settle_across(late_own, 3)
    return (
        output,
        input_delta,
        query_down_out,
        query_up_out,
        key_down_out,
        key_up_out,
        value_down_out,
        value_up_out,
        output_down_out,
        output_up_out,
        expand_down_out,
        expand_up_out,
        shrink_down_out,
        shrink_up_out,
    )


def solution(mesh):
    rows = P(("dp", "tensor"), None)
    tree = P("dp", None)
    whole = P()
    slim = P(None, None, "tensor")
    inward = P("dp", "tensor")
    outward = P("tensor", "dp")
    return jax.shard_map(
        functools.partial(shards, mesh.shape["dp"]),
        mesh=mesh,
        in_specs=(
            rows,
            rows,
            tree,
            tree,
            P("dp"),
            whole,
            whole,
            whole,
            whole,
            inward,
            inward,
            inward,
            outward,
            inward,
            outward,
            P("tensor"),
            P("tensor"),
            whole,
            P("tensor"),
            whole,
            whole,
            slim,
            whole,
            slim,
            whole,
            slim,
            slim,
            whole,
            whole,
            slim,
            slim,
            whole,
        ),
        out_specs=(
            rows,
            rows,
            whole,
            slim,
            whole,
            slim,
            whole,
            slim,
            slim,
            whole,
            whole,
            slim,
            slim,
            whole,
        ),
        check_vma=False,
    )
```

time: 690 us -> 612 us (0.89)
  Pallas kernels: 0 us -> 158 us
  matrix products: 223 us -> 67 us
  local copies, waits for them, and re-layouts: 82.6 us -> 31.7 us
  waiting for transfers between devices: 211 us -> 193 us
  other arithmetic: 91.6 us -> 76 us
    pallas_call x0 -> x16, Pallas kernels: none -> 158 us  [the longest x6 93 us: feed_forward(): pl.pallas_call(functools.partial(feed_kernel, first, last, len(weight)),...]
    dot_general x40 -> x11, matrix products: 92.3 us -> 21.4 us  [product_cols(): lax.dot_general(left, right, (((1,), (1,)), ((), ())), preferred_element_...]
    dot_general x39 -> x11, matrix products: 82.6 us -> 25.5 us  [product(): return jnp.dot(left, right, preferred_element_type=F32)]
    unnamed x455 -> x232, local copies, waits for them, and re-layouts: 55.3 us -> 12.2 us
    ppermute x5 -> x2, waiting for transfers between devices: 40.9 us -> 0.06 us  [fetch(): return (own, lax.ppermute(own, 'dp', dp_pairs), 0)]
    dot_general x14 -> x0, matrix products: 29.2 us -> none  [the longest x2 8.45 us: shards(): jnp.einsum('qhd,khd->hqk', grad_block, value_heads[:key_end], preferred_e...]
    all_gather x6, waiting for transfers between devices: 55.5 us -> 77.6 us  [line_gather(): lax.all_gather(shard, 'dp', axis=0, tiled=True, axis_index_groups=line_gr...]
    convert_element_type x14 -> x12, other arithmetic: 4.11 us -> 18.8 us  [the longest x3 8.51 us: far_part(): return (two.astype(F32) + to_core(three).astype(F32)).astype(BF)]
  transfers between devices with their start and end apart: 54 -> 57, of which waited for: 20 -> 20; matrix products, arithmetic and copies ran while one was open for 47% -> 23% of each run, Pallas kernels for 0% -> 23%
where the time goes in v2:
time: 612 us; the launch traced here: 601 us
  waiting for transfers between devices  193 us (32%)
  Pallas kernels  158 us (26%)
  other arithmetic  76 us (12%)
  matrix products  67 us (11%)
  starting transfers between devices  57.9 us (9%)
  local copies, waits for them, and re-layouts  31.7 us (5%)
  between operations  17.4 us (3%)
    pallas_call x6, Pallas kernels, feed_forward(): pl.pallas_call(functools.partial(feed_kernel, first, last, len(weight)),...  93 us
    all_gather x6, waiting for transfers between devices, line_gather(): lax.all_gather(shard, 'dp', axis=0, tiled=True, axis_index_groups=line_gr...  77.6 us
    ppermute x12, waiting for transfers between devices, to_chip(): return lax.ppermute(v, 'tensor', chip_pairs)  74 us
    pallas_call x4, Pallas kernels, by_head(): pl.pallas_call(functools.partial(kernel, HEAD_DIM ** (-0.5)), grid_spec=p...  36.6 us
    ppermute x6, waiting for transfers between devices, fetch_pieces(): lax.ppermute(v, 'dp', dp_pairs)  35.6 us
    ppermute x22, starting transfers between devices, to_core(): return lax.ppermute(v, 'tensor', core_pairs)  26.8 us
    dot_general x11, matrix products, product(): return jnp.dot(left, right, preferred_element_type=F32)  25.5 us
    dot_general x11, matrix products, product_cols(): lax.dot_general(left, right, (((1,), (1,)), ((), ())), preferred_element_...  21.4 us
  transfers between devices with their start and end apart: 57, of which 20 were waited for; matrix products, arithmetic and copies ran while one was open for 23% of the time, Pallas kernels for 23%

profile of v2, /device:TPU:17, one launch (start us, length us, event | category | flops | bytes accessed | tf_op | source)
XLA Modules:
  0.0 600.7 jit_solution(11447842505789227076)
XLA Ops:
  42.9 12.7 %all-gather.9.cloned.1.call-done.qk_own = bf16[1024,1024]{1,0:T(8,128)(2,1)} async-done(((bf16[256,1024]{1,0:T(8,128)(2,1)}), bf16[1024,1024]{1,0:T(8,128)(2,1)}) %all-gather.9.cloned.1.call-update) | async-done | bytes 2097168 | tf_op jit(solution)/shard_map/all_gather | solution.py:480
  64.8 4.1 fusion.1.refs_12_.refs_16_
  68.9 33.3 %all-gather.7.cloned.1.call-done.vo_own = bf16[1024,1024]{1,0:T(8,128)(2,1)} async-done(((bf16[256,1024]{1,0:T(8,128)(2,1)}), bf16[1024,1024]{1,0:T(8,128)(2,1)}) %all-gather.7.cloned.1.call-update) | async-done | bytes 2097168 | tf_op jit(solution)/shard_map/all_gather | solution.py:480
  109.4 3.9 fusion.29
  119.1 29.7 %all-gather.11.cloned.1.call-done.refs_7_ = bf16[1024,1024]{1,0:T(8,128)(2,1)} async-done(((bf16[256,1024]{1,0:T(8,128)(2,1)}), bf16[1024,1024]{1,0:T(8,128)(2,1)}) %all-gather.11.cloned.1.call-update) | async-done | bytes 2097168 | tf_op jit(solution)/shard_map/all_gather | solution.py:480
  148.9 3.2 fusion.155
  154.8 3.2 fusion.25
  158.7 3.5 add_convert_fusion.6.refs_8_.refs_9_.refs_10_.refs_11_
  162.2 12.9 %attend.1 = (bf16[1024,512]{1,0:T(8,128)(2,1)}, f32[1024,512]{1,0:T(8,128)}) custom-call(s32[1]{0:T(128)} %bitcast.turn, bf16[1024,512]{1,0:T(8,128)(2,1)} %fusion.20.refs_0_.refs_1_.refs_2_.refs_3_, bf16[1024,512]{1,0:T(8,128)(2,1)} %fusion.20.refs_0_.refs_1_.refs_2_.refs_3_, bf16[1024,512]{1,0:T(8,128)(2,1)} %fusion.20.refs_0_.refs_1_.refs_2_.refs_3_, ...), custom_call_target="tpu_custom_call" | custom-call | flops 100000000 | bytes 1000000 | tf_op jit(solution)/shard_map/attend/pallas_call | solution.py:273
  179.1 2.9 fusion.46
  196.1 2.7 fusion.153
  199.1 16.3 %collective-permute-done.9 = bf16[256,2048]{1,0:T(8,128)(2,1)} collective-permute-done((bf16[256,2048]{1,0:T(8,128)(2,1)}, bf16[256,2048]{1,0:T(8,128)(2,1)}, u32[]{:S(2)}, u32[]{:S(2)}) %collective-permute-start.9) | collective-permute-done | bytes 1048608 | tf_op jit(solution)/shard_map/ppermute | solution.py:436
  215.4 2.6 fusion.17
  222.9 3.2 collective-permute-start.17
  227.4 14.0 %collective-permute-done.13.refs_8_ = bf16[512,1024]{1,0:T(8,128)(2,1)} collective-permute-done((bf16[512,1024]{1,0:T(8,128)(2,1)S(1)}, bf16[512,1024]{1,0:T(8,128)(2,1)}, u32[]{:S(2)}, u32[]{:S(2)}) %collective-permute-start.13) | collective-permute-done | bytes 1048608 | tf_op jit(solution)/shard_map/ppermute | solution.py:490
  243.8 3.8 collective-permute-start.14
  248.2 3.7 pad_maximum_fusion.2.refs_1_
  253.0 3.4 fusion.154
  259.8 2.6 pad_maximum_fusion.1.refs_0_
  264.5 16.9 %feed_forward.6 = (f32[1024,2048]{1,0:T(8,128)}, f32[1024,2048]{1,0:T(8,128)}, f32[1024,16]{1,0:T(8,128)}, f32[1024,16]{1,0:T(8,128)}, f32[16,512]{1,0:T(8,128)}, /*index=5*/f32[16,512]{1,0:T(8,128)}) custom-call(bf16[1024,2048]{1,0:T(8,128)(2,1)} %copy-done.4, bf16[1024,2048]{1,0:T(8,128)(2,1)} %pad_maximum_fusion.2.refs_1_, ...), custom_call_target="tpu_custom_call" | custom-call | flops 1073741824 | bytes 41943040 | tf_op jit(solution)/shard_map/feed_forward/pallas_call | solution.py:155
  281.5 21.8 %feed_forward.7 = (f32[1024,2048]{1,0:T(8,128)}, f32[1024,2048]{1,0:T(8,128)}, f32[1024,16]{1,0:T(8,128)}, f32[1024,16]{1,0:T(8,128)}, f32[16,512]{1,0:T(8,128)}, /*index=5*/f32[16,512]{1,0:T(8,128)}) custom-call(bf16[1024,2048]{1,0:T(8,128)(2,1)} %copy-done.4, bf16[1024,2048]{1,0:T(8,128)(2,1)} %pad_maximum_fusion.2.refs_1_, ...), custom_call_target="tpu_custom_call" | custom-call | flops 1073741824 | bytes 41943040 | tf_op jit(solution)/shard_map/feed_forward/pallas_call | solution.py:155
  303.3 18.4 %collective-permute-done.19.refs_9_ = bf16[512,1024]{1,0:T(8,128)(2,1)} collective-permute-done((bf16[512,1024]{1,0:T(8,128)(2,1)}, bf16[512,1024]{1,0:T(8,128)(2,1)}, u32[]{:S(2)}, u32[]{:S(2)}) %collective-permute-start.19) | collective-permute-done | bytes 1048608 | tf_op jit(solution)/shard_map/ppermute | solution.py:490
  321.8 21.9 %feed_forward.8 = (f32[1024,2048]{1,0:T(8,128)}, f32[1024,2048]{1,0:T(8,128)}, f32[1024,16]{1,0:T(8,128)}, f32[1024,16]{1,0:T(8,128)}, f32[16,512]{1,0:T(8,128)}, /*index=5*/f32[16,512]{1,0:T(8,128)}) custom-call(bf16[1024,2048]{1,0:T(8,128)(2,1)} %copy-done.4, bf16[1024,2048]{1,0:T(8,128)(2,1)} %pad_maximum_fusion.2.refs_1_, ...), custom_call_target="tpu_custom_call" | custom-call | flops 1073741824 | bytes 41943040 | tf_op jit(solution)/shard_map/feed_forward/pallas_call | solution.py:155
  343.7 8.7 %feed_forward.9 = (bf16[256,2048]{1,0:T(8,128)(2,1)}, bf16[256,2048]{1,0:T(8,128)(2,1)}, f32[256,16]{1,0:T(8,128)}, f32[256,16]{1,0:T(8,128)}, f32[16,512]{1,0:T(8,128)}, /*index=5*/f32[16,512]{1,0:T(8,128)}) custom-call(bf16[1024,2048]{1,0:T(8,128)(2,1)} %copy-done.4, bf16[1024,2048]{1,0:T(8,128)(2,1)} %pad_maximum_fusion.2.refs_1_, ...), custom_call_target="tpu_custom_call" | custom-call | flops 268435456 | bytes 10485760 | tf_op jit(solution)/shard_map/feed_forward/pallas_call | solution.py:155
  353.3 8.7 %feed_forward.10 = (bf16[256,2048]{1,0:T(8,128)(2,1)}, bf16[256,2048]{1,0:T(8,128)(2,1)}, f32[256,16]{1,0:T(8,128)}, f32[256,16]{1,0:T(8,128)}, f32[16,512]{1,0:T(8,128)}, /*index=5*/f32[16,512]{1,0:T(8,128)}) custom-call(bf16[1024,2048]{1,0:T(8,128)(2,1)} %copy-done.4, bf16[1024,2048]{1,0:T(8,128)(2,1)} %pad_maximum_fusion.2.refs_1_, ...), custom_call_target="tpu_custom_call" | custom-call | flops 268435456 | bytes 10485760 | tf_op jit(solution)/shard_map/feed_forward/pallas_call | solution.py:155
  362.0 2.9 add_convert_fusion.4
  366.1 14.9 %feed_forward.11 = (bf16[256,2048]{1,0:T(8,128)(2,1)}, bf16[256,2048]{1,0:T(8,128)(2,1)}, bf16[256,2048]{1,0:T(8,128)(2,1)}, bf16[256,2048]{1,0:T(8,128)(2,1)}, ...) custom-call(bf16[1024,2048]{1,0:T(8,128)(2,1)} %copy-done.4, ...), custom_call_target="tpu_custom_call" | custom-call | flops 536870912 | bytes 20971520 | tf_op jit(solution)/shard_map/feed_forward/pallas_call | solution.py:155
  381.1 8.9 %collective-permute-done.23 = bf16[256,2048]{1,0:T(8,128)(2,1)} collective-permute-done((bf16[256,2048]{1,0:T(8,128)(2,1)}, bf16[256,2048]{1,0:T(8,128)(2,1)}, u32[]{:S(2)}, u32[]{:S(2)}) %collective-permute-start.23) | collective-permute-done | bytes 1048608 | tf_op jit(solution)/shard_map/ppermute | solution.py:436
  393.5 2.8 fusion.64
  396.4 4.9 fusion.149
  404.0 3.0 fusion.169
  411.2 16.0 %collective-permute-done.26 = bf16[256,2048]{1,0:T(8,128)(2,1)} collective-permute-done((bf16[256,2048]{1,0:T(8,128)(2,1)}, bf16[256,2048]{1,0:T(8,128)(2,1)}, u32[]{:S(2)}, u32[]{:S(2)}) %collective-permute-start.26) | collective-permute-done | bytes 1048608 | tf_op jit(solution)/shard_map/ppermute | solution.py:436
  430.9 2.9 pad_maximum_fusion.3
  439.7 3.6 add_convert_fusion.2.refs_12_.refs_13_.refs_14_.refs_15_
  445.8 6.6 %attend_back.3 = (bf16[1024,512]{1,0:T(8,128)(2,1)}, bf16[1024,512]{1,0:T(8,128)(2,1)}, bf16[1024,512]{1,0:T(8,128)(2,1)}) custom-call(s32[1]{0:T(128)} %bitcast.turn, bf16[1024,512]{1,0:T(8,128)(2,1)} %fusion.20.refs_0_.refs_1_.refs_2_.refs_3_, bf16[1024,512]{1,0:T(8,128)(2,1)} %fusion.20.refs_0_.refs_1_.refs_2_.refs_3_, ...), custom_call_target="tpu_custom_call" | custom-call | flops 100000000 | bytes 1000000 | tf_op jit(solution)/shard_map/attend_back/pallas_call | solution.py:273
  457.6 6.7 %attend_back.4 = (bf16[1024,512]{1,0:T(8,128)(2,1)}, bf16[1024,512]{1,0:T(8,128)(2,1)}, bf16[1024,512]{1,0:T(8,128)(2,1)}) custom-call(s32[1]{0:T(128)} %bitcast.turn, bf16[1024,512]{1,0:T(8,128)(2,1)} %fusion.20.refs_0_.refs_1_.refs_2_.refs_3_, ...), custom_call_target="tpu_custom_call", output_to_operand_aliasing={{0}: (19, {}), {1}: (20, {}), {2}: (21, {})} | custom-call | flops 100000000 | bytes 1000000 | tf_op jit(solution)/shard_map/attend_back/pallas_call | solution.py:273
  468.2 10.4 %attend_back.5 = (bf16[1024,512]{1,0:T(8,128)(2,1)}, bf16[1024,512]{1,0:T(8,128)(2,1)}, bf16[1024,512]{1,0:T(8,128)(2,1)}) custom-call(s32[1]{0:T(128)} %bitcast.turn, bf16[1024,512]{1,0:T(8,128)(2,1)} %fusion.20.refs_0_.refs_1_.refs_2_.refs_3_, ...), custom_call_target="tpu_custom_call", output_to_operand_aliasing={{0}: (19, {}), {1}: (20, {}), {2}: (21, {})} | custom-call | flops 100000000 | bytes 1000000 | tf_op jit(solution)/shard_map/attend_back/pallas_call | solution.py:273
  482.4 3.1 convolution_convert_fusion
  489.0 3.1 add_convert_fusion.1
  494.3 9.5 %back_rows.2 = (bf16[256,2048]{1,0:T(8,128)(2,1)}, bf16[256,2048]{1,0:T(8,128)(2,1)}) custom-call(bf16[1024,512]{1,0:T(8,128)(2,1)} %get-tuple-element.185.query, bf16[1024,512]{1,0:T(8,128)(2,1)} %get-tuple-element.186.key, bf16[1024,512]{1,0:T(8,128)(2,1)} %get-tuple-element.187.value, bf16[1024,48]{1,0:T(8,128)(2,1)} %copy.87.rank, ...), custom_call_target="tpu_custom_call" | custom-call | flops 100000000 | bytes 1000000 | tf_op jit(solution)/shard_map/back_rows/pallas_call | solution.py:312
  511.2 3.3 sum_slots.2
  515.5 3.0 add_convert_fusion
  519.3 9.4 %back_rows.3 = (bf16[256,2048]{1,0:T(8,128)(2,1)}, bf16[256,2048]{1,0:T(8,128)(2,1)}) custom-call(bf16[1024,512]{1,0:T(8,128)(2,1)} %get-tuple-element.185.query, bf16[1024,512]{1,0:T(8,128)(2,1)} %get-tuple-element.186.key, bf16[1024,512]{1,0:T(8,128)(2,1)} %get-tuple-element.187.value, bf16[1024,48]{1,0:T(8,128)(2,1)} %copy.88.rank, ...), custom_call_target="tpu_custom_call" | custom-call | flops 100000000 | bytes 1000000 | tf_op jit(solution)/shard_map/back_rows/pallas_call | solution.py:312
  532.4 5.2 collective-permute-done.42
  537.5 2.8 collective-permute-start.43
  547.8 20.2 %collective-permute-done.40 = bf16[256,2048]{1,0:T(8,128)(2,1)S(1)} collective-permute-done((bf16[256,2048]{1,0:T(8,128)(2,1)}, bf16[256,2048]{1,0:T(8,128)(2,1)S(1)}, u32[]{:S(2)}, u32[]{:S(2)}) %collective-permute-start.40) | collective-permute-done | bytes 1048608 | tf_op jit(solution)/shard_map/ppermute | solution.py:436
  569.3 2.7 sum_slots.3
  576.6 4.6 collective-permute-done.48
  (589 shorter events, 174.7 us)
Async XLA Ops:
  7.2 48.4 %all-gather.9.cloned.1.call-start = ((), (), s32[]{:S(2)}) async-start(), calls=%async_computation.1 | async-start | bytes 2621440 | tf_op jit(solution)/shard_map/all_gather | solution.py:480
  9.3 92.9 %all-gather.7.cloned.1.call-start = ((), (), s32[]{:S(2)}) async-start(), calls=%async_computation | async-start | bytes 2621440 | tf_op jit(solution)/shard_map/all_gather | solution.py:480
  13.6 45.6 %collective-permute-start.1 = (bf16[256,2048]{1,0:T(8,128)(2,1)}, bf16[256,2048]{1,0:T(8,128)(2,1)}, u32[]{:S(2)}, u32[]{:S(2)}) collective-permute-start(bf16[256,2048]{1,0:T(8,128)(2,1)} %fusion.8), channel_id=1, source_target_pairs={{0,2},{2,0},{1,3},{3,1},{4,6},{6,4},{5,7},{7,5},{8,10},{10,8},{9,1... | collective-permute-start | bytes 3145736 | tf_op jit(solution)/shard_map/ppermute | solution.py:436
  14.8 87.7 %collective-permute-start = (bf16[256,2048]{1,0:T(8,128)(2,1)}, bf16[256,2048]{1,0:T(8,128)(2,1)}, u32[]{:S(2)}, u32[]{:S(2)}) collective-permute-start(bf16[256,2048]{1,0:T(8,128)(2,1)} %fusion.8), channel_id=1, source_target_pairs={{0,1},{1,0},{2,3},{3,2},{4,5},{5,4},{6,7},{7,6},{8,9},{9,8},{10,11... | collective-permute-start | bytes 3145736 | tf_op jit(solution)/shard_map/ppermute | solution.py:433
  21.3 201.6 %collective-permute-start.16 = (bf16[256,2048]{1,0:T(8,128)(2,1)}, bf16[256,2048]{1,0:T(8,128)(2,1)}, u32[]{:S(2)}, u32[]{:S(2)}) collective-permute-start(bf16[256,2048]{1,0:T(8,128)(2,1)} %constant_dynamic-update-slice_fusion.29), channel_id=1, source_target_pairs={{0,2},{2,0},{1,3},{3,1},{4,6},{6,4},{5,7},{7,5},{8,10},{10,8},{9,1... | collective-permute-start | bytes 3145736 | tf_op jit(solution)/shard_map/ppermute | solution.py:436
  21.5 226.6 %collective-permute-start.15 = (bf16[256,2048]{1,0:T(8,128)(2,1)}, bf16[256,2048]{1,0:T(8,128)(2,1)}, u32[]{:S(2)}, u32[]{:S(2)}) collective-permute-start(bf16[256,2048]{1,0:T(8,128)(2,1)} %constant_dynamic-update-slice_fusion.29), channel_id=1, source_target_pairs={{0,1},{1,0},{2,3},{3,2},{4,5},{5,4},{6,7},{7,6},{8,9},{9,8},{10,11... | collective-permute-start | bytes 3145736 | tf_op jit(solution)/shard_map/ppermute | solution.py:433
  25.5 15.2 %collective-permute-start.4 = (bf16[256,1024]{1,0:T(8,128)(2,1)}, bf16[256,1024]{1,0:T(8,128)(2,1)}, u32[]{:S(2)}, u32[]{:S(2)}) collective-permute-start(bf16[256,1024]{1,0:T(8,128)(2,1)} %pad_maximum_fusion.8), channel_id=1, source_target_pairs={{0,4},{4,0},{8,12},{12,8},{16,20},{20,16},{24,28},{28,24},{1,5},{5... | collective-permute-start | bytes 1572872 | tf_op jit(solution)/shard_map/ppermute | solution.py:529
  29.7 119.2 %all-gather.11.cloned.1.call-start = ((), (), s32[]{:S(2)}) async-start(), calls=%async_computation.2 | async-start | bytes 2621440 | tf_op jit(solution)/shard_map/all_gather | solution.py:480
  55.6 139.2 %all-gather.13.cloned.1.call-start = ((), (), s32[]{:S(2)}) async-start(), calls=%async_computation.3 | async-start | bytes 2621440 | tf_op jit(solution)/shard_map/all_gather | solution.py:480
  59.1 43.4 %collective-permute-start.2 = (bf16[256,2048]{1,0:T(8,128)(2,1)}, bf16[256,2048]{1,0:T(8,128)(2,1)}, u32[]{:S(2)}, u32[]{:S(2)}) collective-permute-start(bf16[256,2048]{1,0:T(8,128)(2,1)} %collective-permute-done.1), channel_id=1, source_target_pairs={{0,1},{1,0},{2,3},{3,2},{4,5},{5,4},{6,7},{7,6},{8,9},{9,8},{10,11... | collective-permute-start | bytes 3145736 | tf_op jit(solution)/shard_map/ppermute | solution.py:433
  60.0 49.3 %collective-permute-start.3 = (bf16[1024,1024]{1,0:T(8,128)(2,1)S(1)}, bf16[1024,1024]{1,0:T(8,128)(2,1)}, u32[]{:S(2)}, u32[]{:S(2)}) collective-permute-start(bf16[1024,1024]{1,0:T(8,128)(2,1)S(1)} %copy-done.17), channel_id=1, source_target_pairs={{0,4},{4,0},{8,12},{12,8},{16,20},{20,16},{24,28},{28,24},{1,5},{5... | collective-permute-start | bytes 6291464 | tf_op jit(solution)/shard_map/ppermute | solution.py:484
  102.2 150.8 %all-gather.15.cloned.1.call-start = ((), (), s32[]{:S(2)}) async-start(), calls=%async_computation.4 | async-start | bytes 2621440 | tf_op jit(solution)/shard_map/all_gather | solution.py:480
  108.2 46.7 %collective-permute-start.5 = (bf16[1024,1024]{1,0:T(8,128)(2,1)}, bf16[1024,1024]{1,0:T(8,128)(2,1)}, u32[]{:S(2)}, u32[]{:S(2)}) collective-permute-start(bf16[1024,1024]{1,0:T(8,128)(2,1)} %all-gather.7.cloned.1.call-done.vo_own), channel_id=1, source_target_pairs={{0,4},{4,0},{8,12},{12,8},{16,20},{20,16},{24,28},{28,24},{1,5},{5... | collective-permute-start | bytes 6291464 | tf_op jit(solution)/shard_map/ppermute | solution.py:484
  152.0 25.5 %collective-permute-start.6 = (bf16[512,1024]{1,0:T(8,128)(2,1)}, bf16[512,1024]{1,0:T(8,128)(2,1)}, u32[]{:S(2)}, u32[]{:S(2)}) collective-permute-start(bf16[512,1024]{1,0:T(8,128)(2,1)} %get-tuple-element.223), channel_id=1, source_target_pairs={{0,4},{4,0},{8,12},{12,8},{16,20},{20,16},{24,28},{28,24},{1,5},{5... | collective-permute-start | bytes 3145736 | tf_op jit(solution)/shard_map/ppermute | solution.py:490
  154.7 189.0 %all-gather.17.cloned.1.call-start = ((), (), s32[]{:S(2)}) async-start(), calls=%async_computation.5 | async-start | bytes 5242880 | tf_op jit(solution)/shard_map/all_gather | solution.py:480
  187.7 11.1 %collective-permute-start.7 = (bf16[256,2048]{1,0:T(8,128)(2,1)S(1)}, bf16[256,2048]{1,0:T(8,128)(2,1)}, u32[]{:S(2)}, u32[]{:S(2)}) collective-permute-start(bf16[256,2048]{1,0:T(8,128)(2,1)S(1)} %get-tuple-element.216), channel_id=1, source_target_pairs={{0,1},{1,0},{2,3},{3,2},{4,5},{5,4},{6,7},{7,6},{8,9},{9,8},{10,11... | collective-permute-start | bytes 3145736 | tf_op jit(solution)/shard_map/ppermute | solution.py:433
  191.2 24.2 %collective-permute-start.9 = (bf16[256,2048]{1,0:T(8,128)(2,1)}, bf16[256,2048]{1,0:T(8,128)(2,1)}, u32[]{:S(2)}, u32[]{:S(2)}) collective-permute-start(bf16[256,2048]{1,0:T(8,128)(2,1)} %fusion.16), channel_id=1, source_target_pairs={{0,2},{2,0},{1,3},{3,1},{4,6},{6,4},{5,7},{7,5},{8,10},{10,8},{9,1... | collective-permute-start | bytes 3145736 | tf_op jit(solution)/shard_map/ppermute | solution.py:436
  194.8 24.0 %collective-permute-start.10 = (bf16[512,1024]{1,0:T(8,128)(2,1)S(1)}, bf16[512,1024]{1,0:T(8,128)(2,1)S(1)}, u32[]{:S(2)}, u32[]{:S(2)}) collective-permute-start(bf16[512,1024]{1,0:T(8,128)(2,1)S(1)} %copy-done.33), channel_id=1, source_target_pairs={{0,4},{4,0},{8,12},{12,8},{16,20},{20,16},{24,28},{28,24},{1,5},{5... | collective-permute-start | bytes 3145736 | tf_op jit(solution)/shard_map/ppermute | solution.py:490
  198.8 42.5 %collective-permute-start.13 = (bf16[512,1024]{1,0:T(8,128)(2,1)S(1)}, bf16[512,1024]{1,0:T(8,128)(2,1)}, u32[]{:S(2)}, u32[]{:S(2)}) collective-permute-start(bf16[512,1024]{1,0:T(8,128)(2,1)S(1)} %get-tuple-element.219), channel_id=1, source_target_pairs={{0,4},{4,0},{8,12},{12,8},{16,20},{20,16},{24,28},{28,24},{1,5},{5... | collective-permute-start | bytes 3145736 | tf_op jit(solution)/shard_map/ppermute | solution.py:490
  221.6 22.1 %collective-permute-start.12 = (bf16[256,2048]{1,0:T(8,128)(2,1)}, bf16[256,2048]{1,0:T(8,128)(2,1)}, u32[]{:S(2)}, u32[]{:S(2)}) collective-permute-start(bf16[256,2048]{1,0:T(8,128)(2,1)} %add_convert_fusion.5), channel_id=1, source_target_pairs={{0,2},{2,0},{1,3},{3,1},{4,6},{6,4},{5,7},{7,5},{8,10},{10,8},{9,1... | collective-permute-start | bytes 3145736 | tf_op jit(solution)/shard_map/ppermute | solution.py:436
  222.9 25.3 %collective-permute-start.17 = (bf16[256,2048]{1,0:T(8,128)(2,1)}, bf16[256,2048]{1,0:T(8,128)(2,1)S(1)}, u32[]{:S(2)}, u32[]{:S(2)}) collective-permute-start(bf16[256,2048]{1,0:T(8,128)(2,1)} %collective-permute-done.16), channel_id=1, source_target_pairs={{0,1},{1,0},{2,3},{3,2},{4,5},{5,4},{6,7},{7,6},{8,9},{9,8},{10,11... | collective-permute-start | bytes 3145736 | tf_op jit(solution)/shard_map/ppermute | solution.py:433
  227.3 32.5 %collective-permute-start.11 = (bf16[256,2048]{1,0:T(8,128)(2,1)}, bf16[256,2048]{1,0:T(8,128)(2,1)}, u32[]{:S(2)}, u32[]{:S(2)}) collective-permute-start(bf16[256,2048]{1,0:T(8,128)(2,1)} %add_convert_fusion.5), channel_id=1, source_target_pairs={{0,1},{1,0},{2,3},{3,2},{4,5},{5,4},{6,7},{7,6},{8,9},{9,8},{10,11... | collective-permute-start | bytes 3145736 | tf_op jit(solution)/shard_map/ppermute | solution.py:433
  243.8 16.0 %collective-permute-start.14 = (bf16[256,2048]{1,0:T(8,128)(2,1)}, bf16[256,2048]{1,0:T(8,128)(2,1)}, u32[]{:S(2)}, u32[]{:S(2)}) collective-permute-start(bf16[256,2048]{1,0:T(8,128)(2,1)} %collective-permute-done.12), channel_id=1, source_target_pairs={{0,1},{1,0},{2,3},{3,2},{4,5},{5,4},{6,7},{7,6},{8,9},{9,8},{10,11... | collective-permute-start | bytes 3145736 | tf_op jit(solution)/shard_map/ppermute | solution.py:433
  251.8 29.7 %collective-permute-start.20 = (bf16[512,1024]{1,0:T(8,128)(2,1)}, bf16[512,1024]{1,0:T(8,128)(2,1)}, u32[]{:S(2)}, u32[]{:S(2)}) collective-permute-start(bf16[512,1024]{1,0:T(8,128)(2,1)} %get-tuple-element.218), channel_id=1, source_target_pairs={{0,4},{4,0},{8,12},{12,8},{16,20},{20,16},{24,28},{28,24},{1,5},{5... | collective-permute-start | bytes 3145736 | tf_op jit(solution)/shard_map/ppermute | solution.py:490
  256.4 46.9 %collective-permute-start.18 = (bf16[512,1024]{1,0:T(8,128)(2,1)}, bf16[512,1024]{1,0:T(8,128)(2,1)}, u32[]{:S(2)}, u32[]{:S(2)}) collective-permute-start(bf16[512,1024]{1,0:T(8,128)(2,1)} %get-tuple-element.221), channel_id=1, source_target_pairs={{0,4},{4,0},{8,12},{12,8},{16,20},{20,16},{24,28},{28,24},{1,5},{5... | collective-permute-start | bytes 3145736 | tf_op jit(solution)/shard_map/ppermute | solution.py:490
  256.5 65.2 %collective-permute-start.19 = (bf16[512,1024]{1,0:T(8,128)(2,1)}, bf16[512,1024]{1,0:T(8,128)(2,1)}, u32[]{:S(2)}, u32[]{:S(2)}) collective-permute-start(bf16[512,1024]{1,0:T(8,128)(2,1)} %get-tuple-element.220), channel_id=1, source_target_pairs={{0,4},{4,0},{8,12},{12,8},{16,20},{20,16},{24,28},{28,24},{1,5},{5... | collective-permute-start | bytes 3145736 | tf_op jit(solution)/shard_map/ppermute | solution.py:490
  352.4 9.6 %collective-permute-start.21 = (bf16[256,2048]{1,0:T(8,128)(2,1)}, bf16[256,2048]{1,0:T(8,128)(2,1)}, u32[]{:S(2)}, u32[]{:S(2)}) collective-permute-start(bf16[256,2048]{1,0:T(8,128)(2,1)} %get-tuple-element.134), channel_id=1, source_target_pairs={{0,1},{1,0},{2,3},{3,2},{4,5},{5,4},{6,7},{7,6},{8,9},{9,8},{10,11... | collective-permute-start | bytes 3145736 | tf_op jit(solution)/shard_map/ppermute | solution.py:433
  364.9 25.0 %collective-permute-start.23 = (bf16[256,2048]{1,0:T(8,128)(2,1)}, bf16[256,2048]{1,0:T(8,128)(2,1)}, u32[]{:S(2)}, u32[]{:S(2)}) collective-permute-start(bf16[256,2048]{1,0:T(8,128)(2,1)} %add_convert_fusion.4), channel_id=1, source_target_pairs={{0,2},{2,0},{1,3},{3,1},{4,6},{6,4},{5,7},{7,5},{8,10},{10,8},{9,1... | collective-permute-start | bytes 3145736 | tf_op jit(solution)/shard_map/ppermute | solution.py:436
  402.3 25.0 %collective-permute-start.26 = (bf16[256,2048]{1,0:T(8,128)(2,1)}, bf16[256,2048]{1,0:T(8,128)(2,1)}, u32[]{:S(2)}, u32[]{:S(2)}) collective-permute-start(bf16[256,2048]{1,0:T(8,128)(2,1)} %get-tuple-element.212), channel_id=1, source_target_pairs={{0,2},{2,0},{1,3},{3,1},{4,6},{6,4},{5,7},{7,5},{8,10},{10,8},{9,1... | collective-permute-start | bytes 3145736 | tf_op jit(solution)/shard_map/ppermute | solution.py:436
  403.5 26.0 %collective-permute-start.25 = (bf16[256,2048]{1,0:T(8,128)(2,1)}, bf16[256,2048]{1,0:T(8,128)(2,1)}, u32[]{:S(2)}, u32[]{:S(2)}) collective-permute-start(bf16[256,2048]{1,0:T(8,128)(2,1)} %get-tuple-element.212), channel_id=1, source_target_pairs={{0,1},{1,0},{2,3},{3,2},{4,5},{5,4},{6,7},{7,6},{8,9},{9,8},{10,11... | collective-permute-start | bytes 3145736 | tf_op jit(solution)/shard_map/ppermute | solution.py:433
  436.4 7.0 %collective-permute-start.29 = (bf16[96,512]{1,0:T(8,128)(2,1)S(1)}, bf16[96,512]{1,0:T(8,128)(2,1)S(1)}, u32[]{:S(2)}, u32[]{:S(2)}) collective-permute-start(bf16[96,512]{1,0:T(8,128)(2,1)S(1)} %pad_maximum_fusion.15), channel_id=1, source_target_pairs={{0,1},{1,0},{2,3},{3,2},{4,5},{5,4},{6,7},{7,6},{8,9},{9,8},{10,11... | collective-permute-start | bytes 294920 | tf_op jit(solution)/shard_map/ppermute | solution.py:433
  443.4 9.7 %collective-permute-start.30 = (bf16[48,512]{1,0:T(8,128)(2,1)S(1)}, bf16[48,512]{1,0:T(8,128)(2,1)S(1)}, u32[]{:S(2)}, u32[]{:S(2)}) collective-permute-start(bf16[48,512]{1,0:T(8,128)(2,1)S(1)} %add_convert_fusion.8), channel_id=1, source_target_pairs={{0,2},{2,0},{1,3},{3,1},{4,6},{6,4},{5,7},{7,5},{8,10},{10,8},{9,1... | collective-permute-start | bytes 147464 | tf_op jit(solution)/shard_map/ppermute | solution.py:436
  445.5 33.1 %collective-permute-start.32 = (bf16[256,2048]{1,0:T(8,128)(2,1)}, bf16[256,2048]{1,0:T(8,128)(2,1)}, u32[]{:S(2)}, u32[]{:S(2)}) collective-permute-start(bf16[256,2048]{1,0:T(8,128)(2,1)} %add_convert_fusion.3), channel_id=1, source_target_pairs={{0,2},{2,0},{1,3},{3,1},{4,6},{6,4},{5,7},{7,5},{8,10},{10,8},{9,1... | collective-permute-start | bytes 3145736 | tf_op jit(solution)/shard_map/ppermute | solution.py:436
  455.4 8.9 %collective-permute-start.31 = (bf16[16,6272]{1,0:T(8,128)(2,1)}, bf16[16,6272]{1,0:T(8,128)(2,1)S(1)}, u32[]{:S(2)}, u32[]{:S(2)}) collective-permute-start(bf16[16,6272]{1,0:T(8,128)(2,1)} %flatten.2), channel_id=1, source_target_pairs={{0,4},{4,0},{8,12},{12,8},{16,20},{20,16},{24,28},{28,24},{1,5},{5... | collective-permute-start | bytes 602120 | tf_op jit(solution)/shard_map/ppermute | solution.py:726
  456.6 32.4 %collective-permute-start.22 = (bf16[256,2048]{1,0:T(8,128)(2,1)}, bf16[256,2048]{1,0:T(8,128)(2,1)}, u32[]{:S(2)}, u32[]{:S(2)}) collective-permute-start(bf16[256,2048]{1,0:T(8,128)(2,1)} %get-tuple-element.139), channel_id=1, source_target_pairs={{0,1},{1,0},{2,3},{3,2},{4,5},{5,4},{6,7},{7,6},{8,9},{9,8},{10,11... | collective-permute-start | bytes 3145736 | tf_op jit(solution)/shard_map/ppermute | solution.py:433
  464.3 46.0 %collective-permute-start.37 = (bf16[32,6272]{1,0:T(8,128)(2,1)S(1)}, bf16[32,6272]{1,0:T(8,128)(2,1)S(1)}, u32[]{:S(2)}, u32[]{:S(2)}) collective-permute-start(bf16[32,6272]{1,0:T(8,128)(2,1)S(1)} %pad_maximum_fusion.11.refs_0_), channel_id=1, source_target_pairs={{0,8},{4,12},{8,16},{12,20},{16,24},{20,28},{24,0},{28,4},{1,9},{5... | collective-permute-start | bytes 1204232 | tf_op jit(solution)/shard_map/ppermute | solution.py:730
  465.2 45.2 %collective-permute-start.38 = (bf16[32,6272]{1,0:T(8,128)(2,1)S(1)}, bf16[32,6272]{1,0:T(8,128)(2,1)S(1)}, u32[]{:S(2)}, u32[]{:S(2)}) collective-permute-start(bf16[32,6272]{1,0:T(8,128)(2,1)S(1)} %pad_maximum_fusion.11.refs_0_), channel_id=1, source_target_pairs={{0,16},{4,20},{8,24},{12,28},{16,0},{20,4},{24,8},{28,12},{1,17},{... | collective-permute-start | bytes 1204232 | tf_op jit(solution)/shard_map/ppermute | solution.py:730
  466.0 44.4 %collective-permute-start.39 = (bf16[32,6272]{1,0:T(8,128)(2,1)S(1)}, bf16[32,6272]{1,0:T(8,128)(2,1)}, u32[]{:S(2)}, u32[]{:S(2)}) collective-permute-start(bf16[32,6272]{1,0:T(8,128)(2,1)S(1)} %pad_maximum_fusion.11.refs_0_), channel_id=1, source_target_pairs={{0,24},{4,28},{8,0},{12,4},{16,8},{20,12},{24,16},{28,20},{1,25},{... | collective-permute-start | bytes 1204232 | tf_op jit(solution)/shard_map/ppermute | solution.py:730
  503.8 11.7 %collective-permute-start.34 = (bf16[256,2048]{1,0:T(8,128)(2,1)}, bf16[256,2048]{1,0:T(8,128)(2,1)}, u32[]{:S(2)}, u32[]{:S(2)}) collective-permute-start(bf16[256,2048]{1,0:T(8,128)(2,1)} %get-tuple-element.190), channel_id=1, source_target_pairs={{0,1},{1,0},{2,3},{3,2},{4,5},{5,4},{6,7},{7,6},{8,9},{9,8},{10,11... | collective-permute-start | bytes 3145736 | tf_op jit(solution)/shard_map/ppermute | solution.py:433
  528.7 8.8 %collective-permute-start.42 = (bf16[8,16,1536]{2,1,0:T(8,128)(2,1)S(1)}, bf16[8,16,1536]{2,1,0:T(8,128)(2,1)S(1)}, u32[]{:S(2)}, u32[]{:S(2)}) collective-permute-start(bf16[8,16,1536]{2,1,0:T(8,128)(2,1)S(1)} %bitcast.160), channel_id=1, source_target_pairs={{0,2},{2,0},{1,3},{3,1},{4,6},{6,4},{5,7},{7,5},{8,10},{10,8},{9,1... | collective-permute-start | bytes 1179656 | tf_op jit(solution)/shard_map/ppermute | solution.py:436
  530.0 13.8 %collective-permute-start.44 = (bf16[8,16,1536]{2,1,0:T(8,128)(2,1)S(1)}, bf16[8,16,1536]{2,1,0:T(8,128)(2,1)S(1)}, u32[]{:S(2)}, u32[]{:S(2)}) collective-permute-start(bf16[8,16,1536]{2,1,0:T(8,128)(2,1)S(1)} %bitcast.161), channel_id=1, source_target_pairs={{0,1},{1,0},{2,3},{3,2},{4,5},{5,4},{6,7},{7,6},{8,9},{9,8},{10,11... | collective-permute-start | bytes 1179656 | tf_op jit(solution)/shard_map/ppermute | solution.py:433
  537.5 7.5 %collective-permute-start.43 = (bf16[8,16,1536]{2,1,0:T(8,128)(2,1)S(1)}, bf16[8,16,1536]{2,1,0:T(8,128)(2,1)S(1)}, u32[]{:S(2)}, u32[]{:S(2)}) collective-permute-start(bf16[8,16,1536]{2,1,0:T(8,128)(2,1)S(1)} %collective-permute-done.42), channel_id=1, source_target_pairs={{0,1},{1,0},{2,3},{3,2},{4,5},{5,4},{6,7},{7,6},{8,9},{9,8},{10,11... | collective-permute-start | bytes 1179656 | tf_op jit(solution)/shard_map/ppermute | solution.py:433
  540.4 27.5 %collective-permute-start.45 = (bf16[32,3200]{1,0:T(8,128)(2,1)S(1)}, bf16[32,3200]{1,0:T(8,128)(2,1)S(1)}, u32[]{:S(2)}, u32[]{:S(2)}) collective-permute-start(bf16[32,3200]{1,0:T(8,128)(2,1)S(1)} %pad_maximum_fusion.12.refs_0_), channel_id=1, source_target_pairs={{0,8},{4,12},{8,16},{12,20},{16,24},{20,28},{24,0},{28,4},{1,9},{5... | collective-permute-start | bytes 614408 | tf_op jit(solution)/shard_map/ppermute | solution.py:730
  540.5 27.4 %collective-permute-start.46 = (bf16[32,3200]{1,0:T(8,128)(2,1)S(1)}, bf16[32,3200]{1,0:T(8,128)(2,1)S(1)}, u32[]{:S(2)}, u32[]{:S(2)}) collective-permute-start(bf16[32,3200]{1,0:T(8,128)(2,1)S(1)} %pad_maximum_fusion.12.refs_0_), channel_id=1, source_target_pairs={{0,16},{4,20},{8,24},{12,28},{16,0},{20,4},{24,8},{28,12},{1,17},{... | collective-permute-start | bytes 614408 | tf_op jit(solution)/shard_map/ppermute | solution.py:730
  541.5 27.8 %collective-permute-start.47 = (bf16[32,3200]{1,0:T(8,128)(2,1)S(1)}, bf16[32,3200]{1,0:T(8,128)(2,1)}, u32[]{:S(2)}, u32[]{:S(2)}) collective-permute-start(bf16[32,3200]{1,0:T(8,128)(2,1)S(1)} %pad_maximum_fusion.12.refs_0_), channel_id=1, source_target_pairs={{0,24},{4,28},{8,0},{12,4},{16,8},{20,12},{24,16},{28,20},{1,25},{... | collective-permute-start | bytes 614408 | tf_op jit(solution)/shard_map/ppermute | solution.py:730
  543.8 24.1 %collective-permute-start.40 = (bf16[256,2048]{1,0:T(8,128)(2,1)}, bf16[256,2048]{1,0:T(8,128)(2,1)S(1)}, u32[]{:S(2)}, u32[]{:S(2)}) collective-permute-start(bf16[256,2048]{1,0:T(8,128)(2,1)} %add_convert_fusion), channel_id=1, source_target_pairs={{0,2},{2,0},{1,3},{3,1},{4,6},{6,4},{5,7},{7,5},{8,10},{10,8},{9,1... | collective-permute-start | bytes 3145736 | tf_op jit(solution)/shard_map/ppermute | solution.py:436
  572.0 9.2 %collective-permute-start.48 = (bf16[8,16,1536]{2,1,0:T(8,128)(2,1)}, bf16[8,16,1536]{2,1,0:T(8,128)(2,1)S(1)}, u32[]{:S(2)}, u32[]{:S(2)}) collective-permute-start(bf16[8,16,1536]{2,1,0:T(8,128)(2,1)} %bitcast.163), channel_id=1, source_target_pairs={{0,2},{2,0},{1,3},{3,1},{4,6},{6,4},{5,7},{7,5},{8,10},{10,8},{9,1... | collective-permute-start | bytes 1179656 | tf_op jit(solution)/shard_map/ppermute | solution.py:436
  574.6 11.3 %collective-permute-start.50 = (bf16[8,16,1536]{2,1,0:T(8,128)(2,1)}, bf16[8,16,1536]{2,1,0:T(8,128)(2,1)S(1)}, u32[]{:S(2)}, u32[]{:S(2)}) collective-permute-start(bf16[8,16,1536]{2,1,0:T(8,128)(2,1)} %bitcast.164), channel_id=1, source_target_pairs={{0,1},{1,0},{2,3},{3,2},{4,5},{5,4},{6,7},{7,6},{8,9},{9,8},{10,11... | collective-permute-start | bytes 1179656 | tf_op jit(solution)/shard_map/ppermute | solution.py:433
  (124 other events, 1291.8 us)
Sparse Core Ops, SparseCore 0:
  10.2 45.3 all-gather.8
  57.7 44.4 all-gather.6
  104.4 44.4 all-gather.10
  150.3 44.4 all-gather.12
  196.7 44.4 all-gather.14
  243.2 79.2 all-gather.16

commit v3 on v2

--- a/solution.py
+++ b/solution.py
@@ -206,7 +206,7 @@
 
 
 def attend_back_kernel(scale, turn, *refs):
-    count = (len(refs) - 7) // 4 if len(refs) % 4 == 3 else (len(refs) - 10) // 4
+    count = (len(refs) - 7) // 4
     query, key, value, grad = (refs[n * count : (n + 1) * count] for n in range(4))
     bias, level = refs[4 * count : 4 * count + 2]
     grad_query, grad_key, grad_value, key_sum, value_sum = refs[-5:]
@@ -286,6 +286,39 @@
     )(turn, *args)
 
 
+def branch_kernel(zero, one, far, base, unit, scale, gain, wide, low):
+    unit_rows = unit[...]
+    scaled = (
+        zero[...].astype(F32) + one[...].astype(F32) + far[...].astype(F32)
+    ) * gain[...]
+    total = base[...].astype(F32) + scale[...] * (
+        scaled
+        - jnp.mean(scaled, axis=-1, keepdims=True)
+        - unit_rows * jnp.mean(scaled * unit_rows, axis=-1, keepdims=True)
+    )
+    wide[...] = total
+    low[...] = total.astype(BF)
+
+
+def branch_rows(zero, one, far, base, unit, scale, gain):
+    rows, feats = unit.shape
+    tile = rows // 4
+    wide = pl.BlockSpec((tile, feats), lambda i: (i, 0))
+    return pl.pallas_call(
+        branch_kernel,
+        grid=(rows // tile,),
+        in_specs=[wide] * 5
+        + [pl.BlockSpec((tile, 1), lambda i: (i, 0)), pl.BlockSpec((1, feats), lambda i: (0, 0))],
+        out_specs=[wide, wide],
+        out_shape=[
+            jax.ShapeDtypeStruct((rows, feats), F32),
+            jax.ShapeDtypeStruct((rows, feats), BF),
+        ],
+        cost_estimate=pl.CostEstimate(flops=10**7, bytes_accessed=10**6, transcendentals=0),
+        name="branch_rows",
+    )(zero, one, far, base, unit, scale, gain[None])
+
+
 def back_kernel(query, key, value, rank, qk_own, qk_other, vo_own, vo_other, down, *outs):
     width = query.shape[1]
     half = qk_own.shape[0]
@@ -303,7 +336,39 @@
                 out[:, at : at + half] = rows
 
 
-def back_rows(grads, weight_qk, weight_vo, down, tile, first):
+def out_kernel(rows, down, lift, own, other, *outs):
+    half = own.shape[0]
+    rank = product_cols(rows[...], down[...]).astype(BF)
+    for at, weight in ((0, own), (half, other)):
+        here = slice(at, at + half)
+        mixed = product_cols(rows[...], weight[...]) + product(rank, lift[:, here])
+        for k, out in enumerate(outs):
+
+            @pl.when(pl.program_id(0) == k)
+            def _(out=out, mixed=mixed, here=here):
+                out[:, here] = mixed.astype(BF)
+
+
+def out_rows(rows, down, lift, weight, tile, first, count):
+    half, width = weight[0].shape[0], rows.shape[1]
+
+    def fixed(shape, column=0):
+        return pl.BlockSpec(shape, lambda i: (0, column), pipeline_mode=pl.Buffered(1))
+
+    return pl.pallas_call(
+        out_kernel,
+        grid=(count,),
+        in_specs=[pl.BlockSpec((tile, width), lambda i: (first - i, 0))]
+        + [fixed(down.shape), fixed(lift.shape)]
+        + [fixed((half, width), 1)] * 2,
+        out_specs=[fixed((tile, lift.shape[1]))] * count,
+        out_shape=[jax.ShapeDtypeStruct((tile, lift.shape[1]), BF)] * count,
+        cost_estimate=pl.CostEstimate(flops=10**7, bytes_accessed=10**5, transcendentals=0),
+        name="out_rows",
+    )(rows, down, lift, *weight[:2])
+
+
+def back_rows(grads, weight_qk, weight_vo, down, tile, first, count):
     half, width = weight_vo[0].shape[0], grads[0].shape[1]
 
     def fixed(shape):
@@ -311,16 +376,147 @@
 
     return pl.pallas_call(
         back_kernel,
-        grid=(2,),
+        grid=(count,),
         in_specs=[pl.BlockSpec((tile, v.shape[1]), lambda i: (first - i, 0)) for v in grads]
         + [fixed((half, 2 * width))] * 2
         + [fixed((half, width))] * 2
         + [fixed(down.shape)],
-        out_specs=[fixed((tile, down.shape[1]))] * 2,
-        out_shape=[jax.ShapeDtypeStruct((tile, down.shape[1]), BF)] * 2,
+        out_specs=[fixed((tile, down.shape[1]))] * count,
+        out_shape=[jax.ShapeDtypeStruct((tile, down.shape[1]), BF)] * count,
         cost_estimate=pl.CostEstimate(flops=10**8, bytes_accessed=10**6, transcendentals=0),
         name="back_rows",
     )(*grads, *weight_qk[:2], *weight_vo[:2], down)
+
+
+def by_place(place, parts):
+    core_odd, chip_odd = place[1] % 2 == 1, place[1] // 2 == 1
+    low = [jnp.where(core_odd, parts[1], parts[0]), jnp.where(core_odd, parts[0], parts[1])]
+    high = [jnp.where(core_odd, parts[3], parts[2]), jnp.where(core_odd, parts[2], parts[3])]
+    return [jnp.where(chip_odd, b, a) for a, b in zip(low + high, high + low)]
+
+
+def in_order(place, blocks, values):
+    size = values.shape[1] // blocks
+    parts = [values[:, k * size : (k + 1) * size] for k in range(blocks)]
+    ordered = []
+    for own, other in zip(parts[: blocks // 2], parts[blocks // 2 :]):
+        ordered.append(jnp.where(place[0] == 1, other, own))
+        ordered.append(jnp.where(place[0] == 1, own, other))
+    return jnp.concatenate(ordered, axis=1)
+
+
+def pack(place, blocks, wide, base, send, far):
+    total = base.shape[0]
+    for k, values in enumerate(wide):
+        ordered = in_order(place, blocks, values)
+        size = ordered.shape[1] // 4
+        parts = by_place(place, [ordered[:, t * size : (t + 1) * size] for t in range(4)])
+        at, rows = k * values.shape[0], values.shape[0]
+        base[at : at + rows] = parts[0].astype(BF)
+        send[at : at + rows] = parts[1].astype(BF)
+        send[total + at : total + at + rows] = parts[3].astype(BF)
+        far[at : at + rows] = parts[2].astype(BF)
+
+
+def pack_kernel(blocks, place, *refs):
+    *wide, rank, first, second, base, send, far = refs
+    tile = first.shape[0]
+    wide = [ref[...] for ref in wide]
+    wide[-1] = (
+        wide[-1] + product_rows(rank[:tile], first[...]) + product_rows(rank[tile:], second[...])
+    )
+    pack(place, blocks, wide, base, send, far)
+
+
+def in_kernel(first, second, lift, down, own, other, grad, rank):
+    half, tile = own.shape[0], first.shape[0]
+    for k, rows in enumerate((first, second)):
+        here = slice(k * tile, (k + 1) * tile)
+        ranks = product_cols(rows[...], lift[...]).astype(BF)
+        rank[here, :] = ranks
+        grad[here, :] = (
+            product(rows[:, :half], own[...])
+            + product(rows[:, half:], other[...])
+            + product(ranks, down[...])
+        ).astype(BF)
+
+
+def in_rows(first, second, lift, down, weight):
+    half, width = weight[0].shape[0], down.shape[1]
+    rows = 2 * first.shape[0]
+    whole = [pl.BlockSpec(v.shape, lambda i: (0, 0)) for v in (first, second, lift, down)]
+    return pl.pallas_call(
+        in_kernel,
+        grid=(1,),
+        in_specs=whole + [pl.BlockSpec((half, width), lambda i: (0, 1))] * 2,
+        out_specs=[
+            pl.BlockSpec((rows, width), lambda i: (0, 0)),
+            pl.BlockSpec((rows, lift.shape[0]), lambda i: (0, 0)),
+        ],
+        out_shape=[
+            jax.ShapeDtypeStruct((rows, width), BF),
+            jax.ShapeDtypeStruct((rows, lift.shape[0]), BF),
+        ],
+        cost_estimate=pl.CostEstimate(flops=10**7, bytes_accessed=10**5, transcendentals=0),
+        name="in_rows",
+    )(first, second, lift, down, *weight[:2])
+
+
+def late_kernel(blocks, place, *refs):
+    grads, lifts, rows, ranks = refs[:3], refs[3:6], refs[6], refs[7]
+    rank_grad, base, send, far, *ups = refs[8:]
+    width = lifts[0].shape[0]
+    wide = []
+    for k, (grad, lift, up) in enumerate(zip(grads, lifts, ups)):
+        here = slice(k * width, (k + 1) * width)
+        rank = product_cols(grad[...], lift[...]).astype(BF)
+        rank_grad[:, here] = rank
+        wide.append(product_rows(rank, rows[...]))
+        up[...] = product_rows(ranks[:, here], grad[...])
+    pack(place, blocks, wide, base, send, far)
+
+
+def across_kernel(place, *refs):
+    parts, outs = refs[:4], refs[4:]
+    size = parts[0].shape[1] // len(outs)
+    for k, out in enumerate(outs):
+        here = slice(k * size, (k + 1) * size)
+        for t, part in enumerate(by_place(place, [v[:, here].astype(F32) for v in parts])):
+            out[:, t * size : (t + 1) * size] = part
+
+
+def output_kernel(blocks, place, zero, one, far, base, bias, out):
+    total = base[...] + bias[...] + zero[...].astype(F32)
+    total = total + one[...].astype(F32) + far[...].astype(F32)
+    out[...] = in_order(place, blocks, total).astype(BF)
+
+
+def local_call(kernel, name, place, args, shapes, tile=None):
+    specs = [pl.BlockSpec(memory_space=pltpu.SMEM)]
+    options = {}
+    if tile is None:
+        specs += [pl.BlockSpec(memory_space=pltpu.VMEM) for _ in args]
+        out_specs = [pl.BlockSpec(memory_space=pltpu.VMEM) for _ in shapes]
+    else:
+        rows = shapes[0][0][0]
+
+        def spec(shape):
+            if shape[0] == rows:
+                return pl.BlockSpec((tile, shape[1]), lambda i: (i, 0))
+            return pl.BlockSpec(shape, lambda i: (0, 0))
+
+        options = {"grid": (rows // tile,)}
+        specs += [spec(v.shape) for v in args]
+        out_specs = [spec(shape) for shape, _ in shapes]
+    return pl.pallas_call(
+        kernel,
+        in_specs=specs,
+        out_specs=out_specs,
+        out_shape=[jax.ShapeDtypeStruct(shape, kind) for shape, kind in shapes],
+        cost_estimate=pl.CostEstimate(flops=10**6, bytes_accessed=10**5, transcendentals=0),
+        name=name,
+        **options,
+    )(place, *args)
 
 
 def flat_kernel(rank, *refs):
@@ -364,11 +560,7 @@
         functools.partial(slots_kernel, slot_count, rank),
         out_shape=[jax.ShapeDtypeStruct((rows, wide), BF)]
         + [jax.ShapeDtypeStruct((rows, n), F32) for n in slim],
-        cost_estimate=pl.CostEstimate(
-            flops=2 * rows * rows * (wide + sum(slim)),
-            bytes_accessed=rows * (4 * wide + 6 * sum(slim)),
-            transcendentals=0,
-        ),
+        cost_estimate=pl.CostEstimate(flops=10**6, bytes_accessed=10**5, transcendentals=0),
         name="sum_slots",
     )(*trees)
     return [v.reshape(slot_count, rank, -1) for v in (wide_sum, *slim_sums)]
@@ -467,13 +659,6 @@
         far_near = to_core(far)
         return jnp.concatenate([rows, near, far, far_near], axis=0)
 
-    def reduce_rows(partial):
-        parts = [partial[k * row_count : (k + 1) * row_count] for k in range(4)]
-        far = parts[2] + to_core(parts[3].astype(BF)).astype(F32)
-        far_sum = to_chip(far.astype(BF))
-        near = parts[0] + to_core(parts[1].astype(BF)).astype(F32)
-        return near + far_sum.astype(F32)
-
     def line_gather(shard, held):
         if held:
             shard = after(shard, *held)
@@ -483,11 +668,11 @@
         own = line_gather(shard, held)
         return own, lax.ppermute(own, "dp", dp_pairs), 0
 
-    def fetch_pieces(shard, *held):
+    def fetch_pieces(shard, parts, *held):
         own = line_gather(shard, held)
-        middle = own.shape[0] // 2
+        size = own.shape[0] // parts
         swapped = [
-            lax.ppermute(v, "dp", dp_pairs) for v in (own[:middle], own[middle:])
+            lax.ppermute(own[k * size : (k + 1) * size], "dp", dp_pairs) for k in range(parts)
         ]
         return [(v, 0) for v in (own, *swapped)]
 
@@ -532,7 +717,7 @@
     weight_ffn, held = [], [weight_qk[0], weight_vo[0]]
     for h in range(chunk_count - 1):
         more = (last_pair,) if h == 0 else ()
-        weight_ffn.append(fetch_pieces(feed_shard(h), held[h], *more))
+        weight_ffn.append(fetch_pieces(feed_shard(h), 2 if h == 1 else 1, held[h], *more))
         held.append(weight_ffn[-1][0][0])
     weight_ffn.append(fetch_paired(last_pair, held[-2]))
 
@@ -582,7 +767,7 @@
     cot = own_first(cotangent)
     unit_one, scale_one = normalize(inputs_wide)
     rows_one = (unit_one * gain_a + shift_a).astype(BF)
-    full_one = gather_rows(rows_one)
+    full_one = gather_rows(rows_one, gain_b, shift_b, out_bias, last_bias)
     full_cot = gather_rows(cot)
     seq_len = full_one.shape[0]
     head_count = width_local // HEAD_DIM
@@ -618,19 +803,28 @@
         (0, head_count),
         "attend",
     )
-    attended = after(attended, weight_ffn[0][1][0])
     rank_out = product_cols(attended, down_output).astype(BF)
-    main_rows = reduce_rows(
-        beside(out_of(attended, weight_vo, width_local, 2 * width_local))
-        + product(rank_out, lift_output)
-    )
-    main_rows = after(main_rows, weight_ffn[0][2][0], held[3])
+
+    def far_part(two, three):
+        return (two.astype(F32) + to_core(three).astype(F32)).astype(BF)
+
+    def near_part(zero, one):
+        return zero.astype(F32) + to_core(one).astype(F32)
+
+    def out_blocks(rows, first):
+        return out_rows(rows, down_output, lift_output, weight_vo, row_count, first, 2)
+
+    out_third, out_second = out_blocks(attended, 3)
+    out_far = far_part(out_second, out_third)
+    out_first, out_zero = out_blocks(after(attended, out_far, weight_ffn[0][1][0]), 1)
+    main_rows = near_part(out_zero, out_first) + to_chip(out_far).astype(F32)
+    main_rows = after(main_rows, held[3])
+    rank_grad = product_cols(full_cot, lift_shrink).astype(BF)
     residual = inputs_wide + main_rows + out_bias
     unit_two, scale_two = normalize(residual)
     rows_two = (unit_two * gain_b + shift_b).astype(BF)
-    full_two = after(gather_rows(rows_two, weight_ffn[1][1][0]), held[4])
+    full_two = after(gather_rows(rows_two, weight_ffn[1][1][0], weight_ffn[1][2][0], rank_grad), held[4])
     rank_two = product_cols(full_two, down_expand).astype(BF)
-    rank_grad = product_cols(full_cot, lift_shrink).astype(BF)
 
     state = None
     down_parts, up_parts = [], []
@@ -658,12 +852,6 @@
         down_parts.append(down_part)
         up_parts.append(up_part)
 
-    def far_part(two, three):
-        return (two.astype(F32) + to_core(three).astype(F32)).astype(BF)
-
-    def near_part(zero, one):
-        return zero.astype(F32) + to_core(one).astype(F32)
-
     last = chunk_count - 1
     third, *third_deltas = feed(last, full_two, (3 * row_count, seq_len))
     second, *second_deltas = feed(
@@ -676,51 +864,72 @@
     grad_rank_two = jnp.concatenate([near[3], second[3], third[3]], axis=0).astype(BF)
     rank_shrink = jnp.concatenate([near[2], second[2], third[2]], axis=0).astype(BF)
     far_arrived = to_chip(grad_far)
-    grad_norm_two = near_part(near[1][0], after(near[1][1], far_arrived)) + far_arrived.astype(F32)
-    grad_residual = cot.astype(F32) + norm_back(grad_norm_two, gain_b, unit_two, scale_two)
-    grad_branch = grad_residual.astype(BF)
+    grad_residual, grad_branch = branch_rows(
+        near[1][0],
+        to_core(after(near[1][1], far_arrived)),
+        far_arrived,
+        cot,
+        unit_two,
+        scale_two,
+        gain_b,
+    )
 
     branch_near = to_core(grad_branch)
     branch_far = to_chip(grad_branch)
     delta_shrink_up = product_rows(after(rank_shrink, grad_branch), full_cot)
     delta_expand_down = product_rows(after(grad_rank_two, grad_branch), full_two)
     main_far = far_part(after(second[0][0], grad_branch), after(third[0][0], grad_branch))
-    main_near = near_part(*near[0])
-    branch_held = after(branch_far, delta_shrink_up, delta_expand_down, main_far)
-    full_branch = jnp.concatenate(
-        [grad_branch, branch_near, branch_held, to_core(branch_held)], axis=0
-    )
-    rank_grad_out = product_cols(full_branch, lift_output).astype(BF)
-    delta_output_up = product_rows(rank_out, full_branch)
+    main_one = to_core(near[0][1])
+    near_grad, near_rank = in_rows(
+        grad_branch, branch_near, lift_output, down_output, weight_vo
+    )
+    middle = 2 * row_count
+    delta_near = product_rows(rank_out[:row_count], grad_branch) + product_rows(
+        rank_out[row_count:middle], branch_near
+    )
+    branch_held = after(
+        branch_far, delta_shrink_up, delta_expand_down, main_far, near_grad, delta_near
+    )
+    branch_last = to_core(branch_held)
 
     hot_lanes = (
         jnp.arange(128, dtype=jnp.int32)[None, :] == adapter_choice[0]
     ).astype(BF) * jnp.ones((rank_width, 1), BF)
 
-    def by_tensor(parts):
-        low = [jnp.where(core_odd, parts[1], parts[0]), jnp.where(core_odd, parts[0], parts[1])]
-        high = [jnp.where(core_odd, parts[3], parts[2]), jnp.where(core_odd, parts[2], parts[3])]
-        return [jnp.where(chip_odd, b, a) for a, b in zip(low + high, high + low)]
-
     quarter = feats // 4
 
-    def settle_core(wide):
-        stacked = natural(jnp.concatenate(wide, axis=0).astype(BF))
-        parts = by_tensor([stacked[:, t * quarter : (t + 1) * quarter] for t in range(4)])
-        near = to_core(jnp.concatenate([parts[1], parts[3]], axis=0))
-        rows = stacked.shape[0]
-        far = (parts[2].astype(F32) + near[rows:].astype(F32)).astype(BF)
-        return parts[0], near[:rows], far
+    place = jnp.stack([dp_odd.astype(jnp.int32), tensor_index.astype(jnp.int32)])
+
+    def packed(count):
+        rows = count * rank_width
+        return [((rows, quarter), BF), ((2 * rows, quarter), BF), ((rows, quarter), BF)]
+
+    def settle_near(base, send, far):
+        near = to_core(send)
+        far = (far.astype(F32) + near[base.shape[0] :].astype(F32)).astype(BF)
+        return base, near, far
 
     def settle_flat(base, near, far, slim):
-        parts = [base, near, to_chip(far), *slim, hot_lanes]
+        parts = [base, near, far, *slim, hot_lanes]
         rows = base.shape[0] // rank_width
         width = rows * quarter + sum(v.shape[1] for v in slim) + hot_lanes.shape[1]
+        shapes = [v.shape for v in parts]
+        shapes[1] = base.shape
         return pl.pallas_call(
             functools.partial(flat_kernel, rank_width),
+            grid=(1,),
+            in_specs=[pl.BlockSpec(shape, lambda i: (0, 0)) for shape in shapes],
+            out_specs=pl.BlockSpec((rank_width, width), lambda i: (0, 0)),
             out_shape=jax.ShapeDtypeStruct((rank_width, width), BF),
+            cost_estimate=pl.CostEstimate(flops=10**6, bytes_accessed=10**5, transcendentals=0),
             name="flatten",
         )(*parts)
+
+    def settle_outs(own, near, away, away_near):
+        flat = [v.reshape(slot_count * rank_width, -1) for v in (own, near, away, away_near)]
+        shapes = [((slot_count * rank_width, feats), F32)] * 3
+        outs = local_call(across_kernel, "across", place, flat, shapes)
+        return [v.reshape(slot_count, rank_width, feats) for v in outs]
 
     def settle_pair(flat):
         return jnp.concatenate([flat, lax.ppermute(flat, "dp", dp_pairs)], axis=0)
@@ -731,21 +940,27 @@
             for s in range(1, pair_count)
         ]
 
-    def settle_across(own, count):
-        away = to_chip(own)
-        across = by_tensor([own, to_core(own), away, to_core(away)])
-        return [
-            jnp.concatenate(
-                [piece[:, :, k * quarter : (k + 1) * quarter] for piece in across], axis=-1
-            ).astype(F32)
-            for k in range(count)
-        ]
-
-    early_parts = settle_core([delta_shrink_up, delta_expand_down, delta_output_up])
-    grad_attended = (
-        into(after(full_branch, early_parts[0]), weight_vo, width_local, 2 * width_local)
-        + product(rank_grad_out, down_output)
-    ).astype(BF)
+    early_parts = settle_near(
+        *local_call(
+            functools.partial(pack_kernel, dp_size),
+            "pack",
+            place,
+            [
+                delta_shrink_up,
+                delta_expand_down,
+                delta_near,
+                rank_out[middle:],
+                branch_held,
+                branch_last,
+            ],
+            packed(3),
+        )
+    )
+    far_grad, far_rank = in_rows(
+        after(branch_held, early_parts[2]), branch_last, lift_output, down_output, weight_vo
+    )
+    rank_grad_out = jnp.concatenate([near_rank, far_rank], axis=0)
+    grad_attended = jnp.concatenate([near_grad, far_grad], axis=0)
     delta_output_down = product_rows(rank_grad_out, attended)
     main_arrived = to_chip(after(main_far, early_parts[2], branch_far))
 
@@ -765,36 +980,31 @@
     grads = attend_back(after(grad_attended, early_parts[2]), (0, 1))
     early_flat = settle_flat(
         after(early_parts[0], grads[0]),
-        *early_parts[1:],
+        early_parts[1],
+        to_chip(early_parts[2]),
         [*down_parts, *up_parts, delta_output_down],
     )
     early_pair = settle_pair(early_flat)
     grads = attend_back(after(grad_attended, early_flat), (1, 1), grads)
-    early_trees = settle_line(after(early_pair, grads[0]))
+    early_trees = lax.all_gather(
+        after(early_pair, grads[0]), "dp", axis=0, tiled=True, axis_index_groups=line_groups
+    )
     grads = attend_back(after(grad_attended, early_pair), (2, head_count - 2), grads)
-    *grads, main_arrived = lax.optimization_barrier((*grads, main_arrived))
     grad_query_low, grad_key_low, grad_value_low = grads
-    grad_rank_one = jnp.concatenate(
-        [
-            product_cols(grad_query_low, lift_query),
-            product_cols(grad_key_low, lift_key),
-            product_cols(grad_value_low, lift_value),
-        ],
-        axis=1,
-    ).astype(BF)
-    delta_qkv_down = product_rows(grad_rank_one, full_one)
-    delta_query_up = product_rows(rank_query, grad_query_low)
-    delta_key_up = product_rows(rank_key, grad_key_low)
-    delta_value_up = product_rows(rank_value, grad_value_low)
-    late_parts = settle_core(
-        [
-            delta_qkv_down[:rank_width],
-            delta_qkv_down[rank_width : 2 * rank_width],
-            delta_qkv_down[2 * rank_width :],
-        ]
-    )
-    late_flat = settle_flat(*late_parts, [delta_query_up, delta_key_up, delta_value_up])
-    def rows_back(first, *held):
+    grad_rank_one, *late_parts, delta_query_up, delta_key_up, delta_value_up = local_call(
+        functools.partial(late_kernel, dp_size),
+        "late_deltas",
+        place,
+        [*grads, lift_query, lift_key, lift_value, full_one, rank_one],
+        [((seq_len, 3 * rank_width), BF)]
+        + packed(3)
+        + [((rank_width, width_local), F32)] * 3,
+    )
+    late_parts[1] = after(late_parts[1], main_arrived)
+    late_base, late_near, late_far = settle_near(*late_parts)
+    late_chip = to_chip(late_far)
+
+    def rows_back(first, count, *held):
         rank = after(grad_rank_one, *held) if held else grad_rank_one
         return back_rows(
             [grad_query_low, grad_key_low, grad_value_low, rank],
@@ -803,37 +1013,61 @@
             down_qkv,
             row_count,
             first,
-        )
-
-    back_third, back_second = rows_back(3, late_parts[2])
-    back_far = far_part(back_second, back_third)
-    late_pair = settle_pair(late_flat)
+            count,
+        )
+
+    late_flat = settle_flat(
+        late_base, late_near, late_chip, [delta_query_up, delta_key_up, delta_value_up]
+    )
+    late_other = lax.ppermute(late_flat, "dp", dp_pairs)
     early_own, shrink_down_out, expand_up_out, output_down_out = sum_slots(
-        [after(early_trees[0], late_flat), *early_trees[1:]],
+        [after(early_trees, late_flat)],
         slot_count,
         rank_width,
         3 * quarter,
         [hidden_local, hidden_local, width_local],
     )
-    late_trees = settle_line(after(late_pair, early_own))
-    back_first, back_zero = rows_back(1, back_far, late_pair, early_own)
+    late_pair = jnp.concatenate([late_flat, after(late_other, early_own)], axis=0)
+    late_trees = settle_line(late_pair)
+    (back_third,) = rows_back(3, 1, late_pair)
+    back_core = to_core(back_third)
+    (back_second,) = rows_back(2, 1, back_third)
+    early_away = to_chip(early_own)
+    back_far = (back_second.astype(F32) + back_core.astype(F32)).astype(BF)
+    back_far = after(back_far, early_away)
     back_arrived = to_chip(back_far)
-    early_own = after(early_own, back_zero)
-    shrink_up_out, expand_down_out, output_up_out = settle_across(early_own, 3)
-    main_rows_two = main_near + main_arrived.astype(F32)
-    output = natural((residual + main_rows_two + last_bias).astype(BF))
-    grad_norm_one = near_part(back_zero, after(back_first, back_arrived)) + back_arrived.astype(F32)
-    input_delta = natural(
-        (grad_residual + norm_back(grad_norm_one, gain_a, unit_one, scale_one)).astype(BF)
-    )
+    (output,) = local_call(
+        functools.partial(output_kernel, dp_size),
+        "output",
+        place,
+        [near[0][0], main_one, after(main_arrived, back_far), residual, last_bias[None]],
+        [((row_count, feats), BF)],
+        row_count // 4,
+    )
+    (back_first,) = rows_back(1, 1, output, late_trees[1])
+    (back_zero,) = rows_back(0, 1, back_first, *late_trees[1:])
     late_own, query_up_out, key_up_out, value_up_out = sum_slots(
-        [after(late_trees[0], back_arrived, shrink_up_out), *late_trees[1:]],
+        [after(late_trees[0], back_zero), *late_trees[1:]],
         slot_count,
         rank_width,
         3 * quarter,
         [width_local] * 3,
     )
-    query_down_out, key_down_out, value_down_out = settle_across(late_own, 3)
+    late_away = to_chip(after(late_own, back_far))
+    early_outs = settle_outs(
+        early_own, to_core(early_own), early_away, to_core(after(early_away, late_own))
+    )
+    shrink_up_out, expand_down_out, output_up_out = early_outs
+    back_one = to_core(after(back_first, back_arrived, late_own))
+    grad_norm_one = (
+        back_zero.astype(F32) + back_one.astype(F32) + back_arrived.astype(F32)
+    )
+    input_delta = natural(
+        (grad_residual + norm_back(grad_norm_one, gain_a, unit_one, scale_one)).astype(BF)
+    )
+    query_down_out, key_down_out, value_down_out = settle_outs(
+        late_own, to_core(late_own), late_away, to_core(after(late_away, input_delta, early_outs[0]))
+    )
     return (
         output,
         input_delta,

time: 612 us -> 582 us (0.951)
  Pallas kernels: 158 us -> 215 us
  waiting for transfers between devices: 193 us -> 159 us
  other arithmetic: 76 us -> 59.2 us
  matrix products: 67 us -> 54.8 us
  starting transfers between devices: 57.9 us -> 47 us
  local copies, waits for them, and re-layouts: 31.7 us -> 22.1 us
    pallas_call x4 -> x16, Pallas kernels: 22.1 us -> 79.6 us  [the longest x4 24.7 us: back_rows(): pl.pallas_call(back_kernel, grid=(count,), in_specs=[pl.BlockSpec((tile,...]
    ppermute x12, waiting for transfers between devices: 74 us -> 24.7 us  [to_chip(): return lax.ppermute(v, 'tensor', chip_pairs)]
    convert_element_type x11 -> x3, other arithmetic: 16.5 us -> 4.58 us  [the longest x1 2.91 us: shards(): back_far = (back_second.astype(F32) + back_core.astype(F32)).astype(BF)]
    dot_general x11 -> x5, matrix products: 21.4 us -> 11.1 us  [product_cols(): lax.dot_general(left, right, (((1,), (1,)), ((), ())), preferred_element_...]
    all_gather x6, waiting for transfers between devices: 77.6 us -> 87.9 us  [line_gather(): lax.all_gather(shard, 'dp', axis=0, tiled=True, axis_index_groups=line_gr...]
    slice x14 -> x2, local copies, waits for them, and re-layouts: 13.1 us -> 3.77 us  [the longest x1 3.1 us: fetch_pieces(): own[k * size:(k + 1) * size]]
    ppermute x6 -> x5, waiting for transfers between devices: 35.6 us -> 27.4 us  [the longest x4 27.4 us: fetch_pieces(): lax.ppermute(own[k * size:(k + 1) * size], 'dp', dp_pairs)]
    dot_general x11 -> x7, matrix products: 25.5 us -> 22.6 us  [product(): return jnp.dot(left, right, preferred_element_type=F32)]
  transfers between devices with their start and end apart: 57 -> 53, of which waited for: 20 -> 21; matrix products, arithmetic and copies ran while one was open for 23% -> 21% of each run, Pallas kernels for 23% -> 32%
where the time goes in v3:
time: 582 us; the launch traced here: 574 us
  Pallas kernels  215 us (37%)
  waiting for transfers between devices  159 us (27%)
  other arithmetic  59.2 us (10%)
  matrix products  54.8 us (9%)
  starting transfers between devices  47 us (8%)
  local copies, waits for them, and re-layouts  22.1 us (4%)
  between operations  17.2 us (3%)
    pallas_call x6, Pallas kernels, feed_forward(): pl.pallas_call(functools.partial(feed_kernel, first, last, len(weight)),...  93 us
    all_gather x6, waiting for transfers between devices, line_gather(): lax.all_gather(shard, 'dp', axis=0, tiled=True, axis_index_groups=line_gr...  87.9 us
    pallas_call x4, Pallas kernels, by_head(): pl.pallas_call(functools.partial(kernel, HEAD_DIM ** (-0.5)), grid_spec=p...  36.3 us
    ppermute x4, waiting for transfers between devices, fetch_pieces(): lax.ppermute(own[k * size:(k + 1) * size], 'dp', dp_pairs)  27.4 us
    ppermute x12, waiting for transfers between devices, to_chip(): return lax.ppermute(v, 'tensor', chip_pairs)  24.7 us
    pallas_call x4, Pallas kernels, back_rows(): pl.pallas_call(back_kernel, grid=(count,), in_specs=[pl.BlockSpec((tile,...  24.7 us
    dot_general x7, matrix products, product(): return jnp.dot(left, right, preferred_element_type=F32)  22.6 us
    ppermute x22, starting transfers between devices, to_core(): return lax.ppermute(v, 'tensor', core_pairs)  22.4 us
  transfers between devices with their start and end apart: 53, of which 21 were waited for; matrix products, arithmetic and copies ran while one was open for 21% of the time, Pallas kernels for 32%

profile of v3, /device:TPU:17, one launch (start us, length us, event | category | flops | bytes accessed | tf_op | source)
XLA Modules:
  0.0 574.1 jit_solution(5760678871763446327)
XLA Ops:
  42.0 13.5 %all-gather.10.cloned.1.call-done.qk_own = bf16[1024,1024]{1,0:T(8,128)(2,1)} async-done(((bf16[256,1024]{1,0:T(8,128)(2,1)}), bf16[1024,1024]{1,0:T(8,128)(2,1)}) %all-gather.10.cloned.1.call-update) | async-done | bytes 2097168 | tf_op jit(solution)/shard_map/all_gather | solution.py:665
  64.6 37.6 %all-gather.8.cloned.1.call-done.own.vo_own = bf16[1024,1024]{1,0:T(8,128)(2,1)} async-done(((bf16[256,1024]{1,0:T(8,128)(2,1)}), bf16[1024,1024]{1,0:T(8,128)(2,1)}) %all-gather.8.cloned.1.call-update) | async-done | bytes 2097168 | tf_op jit(solution)/shard_map/all_gather | solution.py:665
  103.7 3.3 fusion.1.refs_12_.refs_16_
  114.9 3.9 fusion.23
  118.8 5.9 %fusion.27 = f32[1024,1024]{1,0:T(8,128)} fusion(f32[1024,1024]{1,0:T(8,128)S(1)} %fusion.23, bf16[1024,1024]{1,0:T(8,128)(2,1)} %all-gather.10.cloned.1.call-done.qk_own, bf16[1024,2048]{1,0:T(8,128)(2,1)S(1)} %pad_maximum_fusion.refs_6_), kind=kOutput, calls=%fused_computation.47 | convolution fusion | flops 2148532224 | bytes 12582912 | tf_op jit(solution)/shard_map/dot_general | solution.py:29
  124.8 24.1 %all-gather.12.cloned.1.call-done.refs_7_ = bf16[1024,1024]{1,0:T(8,128)(2,1)} async-done(((bf16[256,1024]{1,0:T(8,128)(2,1)}), bf16[1024,1024]{1,0:T(8,128)(2,1)}) %all-gather.12.cloned.1.call-update) | async-done | bytes 2097168 | tf_op jit(solution)/shard_map/all_gather | solution.py:665
  149.2 3.2 fusion.16.refs_4_.refs_5_.refs_6_.refs_7_
  152.4 3.0 fusion.18.refs_0_.refs_1_.refs_2_.refs_3_
  163.1 12.6 %attend.1 = (bf16[1024,512]{1,0:T(8,128)(2,1)}, f32[1024,512]{1,0:T(8,128)}) custom-call(s32[1]{0:T(128)} %bitcast.1.turn, bf16[1024,512]{1,0:T(8,128)(2,1)} %fusion.18.refs_0_.refs_1_.refs_2_.refs_3_, bf16[1024,512]{1,0:T(8,128)(2,1)} %fusion.18.refs_0_.refs_1_.refs_2_.refs_3_, bf16[1024,512]{1,0:T(8,128)(2,1)} %fusion.18.refs_0_.refs_1_.refs_2_.refs_3_, ...), custom_call_target="tpu_custom_call" | custom-call | flops 100000000 | bytes 1000000 | tf_op jit(solution)/shard_map/attend/pallas_call | solution.py:273
  175.7 7.3 %out_rows.2 = (bf16[256,2048]{1,0:T(8,128)(2,1)}, bf16[256,2048]{1,0:T(8,128)(2,1)}) custom-call(bf16[1024,512]{1,0:T(8,128)(2,1)} %get-tuple-element.144.rows, bf16[16,512]{1,0:T(8,128)(2,1)} %bitcast.135, bf16[16,2048]{1,0:T(8,128)(2,1)} %copy-done.20, bf16[1024,1024]{1,0:T(8,128)(2,1)} %all-gather.8.cloned.1.call-done.own.vo_own, ...), custom_call_target="tpu_custom_call" | custom-call | flops 10000000 | bytes 100000 | tf_op jit(solution)/shard_map/out_rows/pallas_call | solution.py:358
  192.1 11.3 %collective-permute-done.7.refs_8_ = bf16[1024,1024]{1,0:T(8,128)(2,1)} collective-permute-done((bf16[1024,1024]{1,0:T(8,128)(2,1)}, bf16[1024,1024]{1,0:T(8,128)(2,1)}, u32[]{:S(2)}, u32[]{:S(2)}) %collective-permute-start.7) | collective-permute-done | bytes 2097184 | tf_op jit(solution)/shard_map/ppermute | solution.py:675
  203.3 7.4 %out_rows.3 = (bf16[256,2048]{1,0:T(8,128)(2,1)}, bf16[256,2048]{1,0:T(8,128)(2,1)}) custom-call(bf16[1024,512]{1,0:T(8,128)(2,1)} %get-tuple-element.144.rows, bf16[16,512]{1,0:T(8,128)(2,1)} %bitcast.136, bf16[16,2048]{1,0:T(8,128)(2,1)} %copy-done.20, bf16[1024,1024]{1,0:T(8,128)(2,1)} %all-gather.8.cloned.1.call-done.own.vo_own, ...), custom_call_target="tpu_custom_call" | custom-call | flops 10000000 | bytes 100000 | tf_op jit(solution)/shard_map/out_rows/pallas_call | solution.py:358
  213.1 3.1 fusion.137
  224.3 3.7 pad_maximum_fusion.1.refs_1_
  228.0 12.7 %all-gather.16.cloned.1.call-done.refs_7_ = bf16[1024,1024]{1,0:T(8,128)(2,1)} async-done(((bf16[256,1024]{1,0:T(8,128)(2,1)}), bf16[1024,1024]{1,0:T(8,128)(2,1)}) %all-gather.16.cloned.1.call-update) | async-done | bytes 2097168 | tf_op jit(solution)/shard_map/all_gather | solution.py:665
  241.9 4.1 convolution_convert_fusion.1.refs_3_
  247.1 16.2 %collective-permute-done.13.refs_9_ = bf16[512,1024]{1,0:T(8,128)(2,1)} collective-permute-done((bf16[512,1024]{1,0:T(8,128)(2,1)}, bf16[512,1024]{1,0:T(8,128)(2,1)}, u32[]{:S(2)}, u32[]{:S(2)}) %collective-permute-start.13) | collective-permute-done | bytes 1048608 | tf_op jit(solution)/shard_map/ppermute | solution.py:675
  267.9 6.1 %pad_maximum_fusion.2.refs_0_ = bf16[1024,2048]{1,0:T(8,128)(2,1)S(1)} fusion(bf16[256,2048]{1,0:T(8,128)(2,1)S(1)} %collective-permute-done.17, bf16[256,2048]{1,0:T(8,128)(2,1)} %collective-permute-done.11, bf16[256,2048]{1,0:T(8,128)(2,1)S(1)} %collective-permute-done.10, bf16[256,2048]{1,0:T(8,128)(2,1)S(1)} %get-tuple-element.262), kind=kLoop, calls=%fused_computation.2 | loop fusion | flops 16777216 | bytes 8388608 | tf_op jit(solution)/shard_map/concatenate | solution.py:660
  276.1 17.0 %feed_forward.6 = (f32[1024,2048]{1,0:T(8,128)}, f32[1024,2048]{1,0:T(8,128)}, f32[1024,16]{1,0:T(8,128)}, f32[1024,16]{1,0:T(8,128)}, f32[16,512]{1,0:T(8,128)}, /*index=5*/f32[16,512]{1,0:T(8,128)}) custom-call(bf16[1024,2048]{1,0:T(8,128)(2,1)} %copy-done.3, bf16[1024,2048]{1,0:T(8,128)(2,1)} %pad_maximum_fusion.1.refs_1_, ...), custom_call_target="tpu_custom_call" | custom-call | flops 1073741824 | bytes 41943040 | tf_op jit(solution)/shard_map/feed_forward/pallas_call | solution.py:155
  293.1 22.0 %feed_forward.7 = (f32[1024,2048]{1,0:T(8,128)}, f32[1024,2048]{1,0:T(8,128)}, f32[1024,16]{1,0:T(8,128)}, f32[1024,16]{1,0:T(8,128)}, f32[16,512]{1,0:T(8,128)}, /*index=5*/f32[16,512]{1,0:T(8,128)}) custom-call(bf16[1024,2048]{1,0:T(8,128)(2,1)} %copy-done.3, bf16[1024,2048]{1,0:T(8,128)(2,1)} %pad_maximum_fusion.1.refs_1_, ...), custom_call_target="tpu_custom_call" | custom-call | flops 1073741824 | bytes 41943040 | tf_op jit(solution)/shard_map/feed_forward/pallas_call | solution.py:155
  315.1 21.8 %feed_forward.8 = (f32[1024,2048]{1,0:T(8,128)}, f32[1024,2048]{1,0:T(8,128)}, f32[1024,16]{1,0:T(8,128)}, f32[1024,16]{1,0:T(8,128)}, f32[16,512]{1,0:T(8,128)}, /*index=5*/f32[16,512]{1,0:T(8,128)}) custom-call(bf16[1024,2048]{1,0:T(8,128)(2,1)} %copy-done.3, bf16[1024,2048]{1,0:T(8,128)(2,1)} %pad_maximum_fusion.1.refs_1_, ...), custom_call_target="tpu_custom_call" | custom-call | flops 1073741824 | bytes 41943040 | tf_op jit(solution)/shard_map/feed_forward/pallas_call | solution.py:155
  336.9 8.7 %feed_forward.9 = (bf16[256,2048]{1,0:T(8,128)(2,1)}, bf16[256,2048]{1,0:T(8,128)(2,1)}, f32[256,16]{1,0:T(8,128)}, f32[256,16]{1,0:T(8,128)}, f32[16,512]{1,0:T(8,128)}, /*index=5*/f32[16,512]{1,0:T(8,128)}) custom-call(bf16[1024,2048]{1,0:T(8,128)(2,1)} %copy-done.3, bf16[1024,2048]{1,0:T(8,128)(2,1)} %pad_maximum_fusion.1.refs_1_, ...), custom_call_target="tpu_custom_call" | custom-call | flops 268435456 | bytes 10485760 | tf_op jit(solution)/shard_map/feed_forward/pallas_call | solution.py:155
  346.0 8.7 %feed_forward.10 = (bf16[256,2048]{1,0:T(8,128)(2,1)}, bf16[256,2048]{1,0:T(8,128)(2,1)}, f32[256,16]{1,0:T(8,128)}, f32[256,16]{1,0:T(8,128)}, f32[16,512]{1,0:T(8,128)}, /*index=5*/f32[16,512]{1,0:T(8,128)}) custom-call(bf16[1024,2048]{1,0:T(8,128)(2,1)} %copy-done.3, bf16[1024,2048]{1,0:T(8,128)(2,1)} %pad_maximum_fusion.1.refs_1_, ...), custom_call_target="tpu_custom_call" | custom-call | flops 268435456 | bytes 10485760 | tf_op jit(solution)/shard_map/feed_forward/pallas_call | solution.py:155
  358.4 14.9 %feed_forward.11 = (bf16[256,2048]{1,0:T(8,128)(2,1)}, bf16[256,2048]{1,0:T(8,128)(2,1)}, bf16[256,2048]{1,0:T(8,128)(2,1)}, bf16[256,2048]{1,0:T(8,128)(2,1)}, ...) custom-call(bf16[1024,2048]{1,0:T(8,128)(2,1)} %copy-done.3, ...), custom_call_target="tpu_custom_call" | custom-call | flops 536870912 | bytes 20971520 | tf_op jit(solution)/shard_map/feed_forward/pallas_call | solution.py:155
  373.4 8.7 %collective-permute-done.21.far = bf16[256,2048]{1,0:T(8,128)(2,1)S(1)} collective-permute-done((bf16[256,2048]{1,0:T(8,128)(2,1)}, bf16[256,2048]{1,0:T(8,128)(2,1)S(1)}, u32[]{:S(2)}, u32[]{:S(2)}) %collective-permute-start.21) | collective-permute-done | bytes 1048608 | tf_op jit(solution)/shard_map/ppermute | solution.py:628
  385.7 6.0 %branch_rows.1 = (f32[256,2048]{1,0:T(8,128)}, bf16[256,2048]{1,0:T(8,128)(2,1)}) custom-call(bf16[256,2048]{1,0:T(8,128)(2,1)} %get-tuple-element.172.zero, bf16[256,2048]{1,0:T(8,128)(2,1)} %collective-permute-done.22.one, bf16[256,2048]{1,0:T(8,128)(2,1)} %copy-done.25, bf16[256,2048]{1,0:T(8,128)(2,1)} %constant_dynamic-update-slice_fusion.30.base, ...), custom_call_target="tpu_custom_call" | custom-call | flops 10000000 | bytes 1000000 | tf_op jit(solution)/shard_map/branch_rows/pallas_call | solution.py:307
  394.9 3.7 fusion.142.refs_1_
  400.0 4.9 in_rows.2
  411.3 6.8 %collective-permute-done.25.refs_4_.first = bf16[256,2048]{1,0:T(8,128)(2,1)S(1)} collective-permute-done((bf16[256,2048]{1,0:T(8,128)(2,1)}, bf16[256,2048]{1,0:T(8,128)(2,1)S(1)}, u32[]{:S(2)}, u32[]{:S(2)}) %collective-permute-start.25) | collective-permute-done | bytes 1048608 | tf_op jit(solution)/shard_map/ppermute | solution.py:628
  421.7 2.9 pack.1
  428.3 4.9 in_rows.3
  438.3 6.6 %attend_back.3 = (bf16[1024,512]{1,0:T(8,128)(2,1)}, bf16[1024,512]{1,0:T(8,128)(2,1)}, bf16[1024,512]{1,0:T(8,128)(2,1)}) custom-call(s32[1]{0:T(128)} %bitcast.1.turn, bf16[1024,512]{1,0:T(8,128)(2,1)} %fusion.18.refs_0_.refs_1_.refs_2_.refs_3_, bf16[1024,512]{1,0:T(8,128)(2,1)} %fusion.18.refs_0_.refs_1_.refs_2_.refs_3_, ...), custom_call_target="tpu_custom_call" | custom-call | flops 100000000 | bytes 1000000 | tf_op jit(solution)/shard_map/attend_back/pallas_call | solution.py:273
  448.4 6.9 %attend_back.4 = (bf16[1024,512]{1,0:T(8,128)(2,1)}, bf16[1024,512]{1,0:T(8,128)(2,1)}, bf16[1024,512]{1,0:T(8,128)(2,1)}) custom-call(s32[1]{0:T(128)} %bitcast.1.turn, bf16[1024,512]{1,0:T(8,128)(2,1)} %fusion.18.refs_0_.refs_1_.refs_2_.refs_3_, ...), custom_call_target="tpu_custom_call", output_to_operand_aliasing={{0}: (19, {}), {1}: (20, {}), {2}: (21, {})} | custom-call | flops 100000000 | bytes 1000000 | tf_op jit(solution)/shard_map/attend_back/pallas_call | solution.py:273
  456.5 10.2 %attend_back.5 = (bf16[1024,512]{1,0:T(8,128)(2,1)}, bf16[1024,512]{1,0:T(8,128)(2,1)}, bf16[1024,512]{1,0:T(8,128)(2,1)}) custom-call(s32[1]{0:T(128)} %bitcast.1.turn, bf16[1024,512]{1,0:T(8,128)(2,1)} %fusion.18.refs_0_.refs_1_.refs_2_.refs_3_, ...), custom_call_target="tpu_custom_call", output_to_operand_aliasing={{0}: (19, {}), {1}: (20, {}), {2}: (21, {})} | custom-call | flops 100000000 | bytes 1000000 | tf_op jit(solution)/shard_map/attend_back/pallas_call | solution.py:273
  466.7 7.5 %late_deltas.1 = (bf16[1024,48]{1,0:T(8,128)(2,1)}, bf16[48,512]{1,0:T(8,128)(2,1)}, bf16[96,512]{1,0:T(8,128)(2,1)}, bf16[48,512]{1,0:T(8,128)(2,1)}, f32[16,51...) custom-call(s32[2]{0:T(128)} %pad_add_fusion.place, bf16[1024,512]{1,0:T(8,128)(2,1)} %get-tuple-element.220.refs_0_.query, ...), custom_call_target="tpu_custom_call" | custom-call | flops 1000000 | bytes 100000 | tf_op jit(solution)/shard_map/late_deltas/pallas_call | solution.py:511
  474.2 6.1 %collective-permute-done.28.far = bf16[256,2048]{1,0:T(8,128)(2,1)} collective-permute-done((bf16[256,2048]{1,0:T(8,128)(2,1)S(1)}, bf16[256,2048]{1,0:T(8,128)(2,1)}, u32[]{:S(2)}, u32[]{:S(2)}) %collective-permute-start.28) | collective-permute-done | bytes 1048608 | tf_op jit(solution)/shard_map/ppermute | solution.py:628
  484.2 3.1 collective-permute-done.32.refs_2_
  491.2 3.4 sum_slots.2
  495.6 6.2 %back_rows.4 = bf16[256,2048]{1,0:T(8,128)(2,1)} custom-call(bf16[1024,512]{1,0:T(8,128)(2,1)} %get-tuple-element.220.refs_0_.query, bf16[1024,512]{1,0:T(8,128)(2,1)} %get-tuple-element.221.refs_1_.key, bf16[1024,512]{1,0:T(8,128)(2,1)} %get-tuple-element.222.refs_2_.value, bf16[1024,48]{1,0:T(8,128)(2,1)} %get-tuple-element.241.rank, ...), custom_call_target="tpu_custom_call" | custom-call | flops 100000000 | bytes 1000000 | tf_op jit(solution)/shard_map/back_rows/pallas_call | solution.py:377
  503.8 6.1 %back_rows.5 = bf16[256,2048]{1,0:T(8,128)(2,1)} custom-call(bf16[1024,512]{1,0:T(8,128)(2,1)} %get-tuple-element.220.refs_0_.query, bf16[1024,512]{1,0:T(8,128)(2,1)} %get-tuple-element.221.refs_1_.key, bf16[1024,512]{1,0:T(8,128)(2,1)} %get-tuple-element.222.refs_2_.value, bf16[1024,48]{1,0:T(8,128)(2,1)} %get-tuple-element.241.rank, ...), custom_call_target="tpu_custom_call" | custom-call | flops 100000000 | bytes 1000000 | tf_op jit(solution)/shard_map/back_rows/pallas_call | solution.py:377
  509.9 2.9 add_convert_fusion
  518.9 4.4 output.1
  523.3 6.2 %back_rows.6 = bf16[256,2048]{1,0:T(8,128)(2,1)} custom-call(bf16[1024,512]{1,0:T(8,128)(2,1)} %get-tuple-element.220.refs_0_.query, bf16[1024,512]{1,0:T(8,128)(2,1)} %get-tuple-element.221.refs_1_.key, bf16[1024,512]{1,0:T(8,128)(2,1)} %get-tuple-element.222.refs_2_.value, bf16[1024,48]{1,0:T(8,128)(2,1)} %get-tuple-element.241.rank, ...), custom_call_target="tpu_custom_call" | custom-call | flops 100000000 | bytes 1000000 | tf_op jit(solution)/shard_map/back_rows/pallas_call | solution.py:377
  529.5 3.7 collective-permute-done.38.refs_3_
  533.2 6.1 %back_rows.7 = bf16[256,2048]{1,0:T(8,128)(2,1)} custom-call(bf16[1024,512]{1,0:T(8,128)(2,1)} %get-tuple-element.220.refs_0_.query, bf16[1024,512]{1,0:T(8,128)(2,1)} %get-tuple-element.221.refs_1_.key, bf16[1024,512]{1,0:T(8,128)(2,1)} %get-tuple-element.222.refs_2_.value, bf16[1024,48]{1,0:T(8,128)(2,1)} %get-tuple-element.241.rank, ...), custom_call_target="tpu_custom_call" | custom-call | flops 100000000 | bytes 1000000 | tf_op jit(solution)/shard_map/back_rows/pallas_call | solution.py:377
  542.1 5.6 collective-permute-start.40
  552.0 3.2 across.2
  563.8 3.2 across.3
  (529 shorter events, 155.6 us)
Async XLA Ops:
  7.2 48.4 %all-gather.10.cloned.1.call-start = ((), (), s32[]{:S(2)}) async-start(), calls=%async_computation.1 | async-start | bytes 2621440 | tf_op jit(solution)/shard_map/all_gather | solution.py:665
  9.3 92.9 %all-gather.8.cloned.1.call-start = ((), (), s32[]{:S(2)}) async-start(), calls=%async_computation | async-start | bytes 2621440 | tf_op jit(solution)/shard_map/all_gather | solution.py:665
  12.2 49.3 %collective-permute-start.1 = (bf16[256,2048]{1,0:T(8,128)(2,1)S(1)}, bf16[256,2048]{1,0:T(8,128)(2,1)}, u32[]{:S(2)}, u32[]{:S(2)}) collective-permute-start(bf16[256,2048]{1,0:T(8,128)(2,1)S(1)} %fusion.8), channel_id=1, source_target_pairs={{0,2},{2,0},{1,3},{3,1},{4,6},{6,4},{5,7},{7,5},{8,10},{10,8},{9,1... | collective-permute-start | bytes 3145736 | tf_op jit(solution)/shard_map/ppermute | solution.py:628
  13.4 93.5 %collective-permute-start = (bf16[256,2048]{1,0:T(8,128)(2,1)S(1)}, bf16[256,2048]{1,0:T(8,128)(2,1)}, u32[]{:S(2)}, u32[]{:S(2)}) collective-permute-start(bf16[256,2048]{1,0:T(8,128)(2,1)S(1)} %fusion.8), channel_id=1, source_target_pairs={{0,1},{1,0},{2,3},{3,2},{4,5},{5,4},{6,7},{7,6},{8,9},{9,8},{10,11... | collective-permute-start | bytes 3145736 | tf_op jit(solution)/shard_map/ppermute | solution.py:625
  19.9 193.0 %collective-permute-start.15 = (bf16[256,2048]{1,0:T(8,128)(2,1)}, bf16[256,2048]{1,0:T(8,128)(2,1)}, u32[]{:S(2)}, u32[]{:S(2)}) collective-permute-start(bf16[256,2048]{1,0:T(8,128)(2,1)} %constant_dynamic-update-slice_fusion.30.base), channel_id=1, source_target_pairs={{0,2},{2,0},{1,3},{3,1},{4,6},{6,4},{5,7},{7,5},{8,10},{10,8},{9,1... | collective-permute-start | bytes 3145736 | tf_op jit(solution)/shard_map/ppermute | solution.py:628
  20.2 204.1 %collective-permute-start.14 = (bf16[256,2048]{1,0:T(8,128)(2,1)}, bf16[256,2048]{1,0:T(8,128)(2,1)}, u32[]{:S(2)}, u32[]{:S(2)}) collective-permute-start(bf16[256,2048]{1,0:T(8,128)(2,1)} %constant_dynamic-update-slice_fusion.30.base), channel_id=1, source_target_pairs={{0,1},{1,0},{2,3},{3,2},{4,5},{5,4},{6,7},{7,6},{8,9},{9,8},{10,11... | collective-permute-start | bytes 3145736 | tf_op jit(solution)/shard_map/ppermute | solution.py:625
  25.2 14.7 %collective-permute-start.4 = (bf16[256,1024]{1,0:T(8,128)(2,1)}, bf16[256,1024]{1,0:T(8,128)(2,1)}, u32[]{:S(2)}, u32[]{:S(2)}) collective-permute-start(bf16[256,1024]{1,0:T(8,128)(2,1)} %pad_maximum_fusion.7), channel_id=1, source_target_pairs={{0,4},{4,0},{8,12},{12,8},{16,20},{20,16},{24,28},{28,24},{1,5},{5... | collective-permute-start | bytes 1572872 | tf_op jit(solution)/shard_map/ppermute | solution.py:714
  29.3 119.5 %all-gather.12.cloned.1.call-start = ((), (), s32[]{:S(2)}) async-start(), calls=%async_computation.2 | async-start | bytes 2621440 | tf_op jit(solution)/shard_map/all_gather | solution.py:665
  55.6 156.8 %all-gather.14.cloned.1.call-start = ((), (), s32[]{:S(2)}) async-start(), calls=%async_computation.3 | async-start | bytes 2621440 | tf_op jit(solution)/shard_map/all_gather | solution.py:665
  61.4 45.6 %collective-permute-start.2 = (bf16[256,2048]{1,0:T(8,128)(2,1)}, bf16[256,2048]{1,0:T(8,128)(2,1)S(1)}, u32[]{:S(2)}, u32[]{:S(2)}) collective-permute-start(bf16[256,2048]{1,0:T(8,128)(2,1)} %collective-permute-done.1), channel_id=1, source_target_pairs={{0,1},{1,0},{2,3},{3,2},{4,5},{5,4},{6,7},{7,6},{8,9},{9,8},{10,11... | collective-permute-start | bytes 3145736 | tf_op jit(solution)/shard_map/ppermute | solution.py:625
  62.3 52.6 %collective-permute-start.3 = (bf16[1024,1024]{1,0:T(8,128)(2,1)}, bf16[1024,1024]{1,0:T(8,128)(2,1)}, u32[]{:S(2)}, u32[]{:S(2)}) collective-permute-start(bf16[1024,1024]{1,0:T(8,128)(2,1)} %all-gather.10.cloned.1.call-done.qk_own), channel_id=1, source_target_pairs={{0,4},{4,0},{8,12},{12,8},{16,20},{20,16},{24,28},{28,24},{1,5},{5... | collective-permute-start | bytes 6291464 | tf_op jit(solution)/shard_map/ppermute | solution.py:669
  102.2 138.5 %all-gather.16.cloned.1.call-start = ((), (), s32[]{:S(2)}) async-start(), calls=%async_computation.4 | async-start | bytes 2621440 | tf_op jit(solution)/shard_map/all_gather | solution.py:665
  111.9 46.4 %collective-permute-start.5 = (bf16[1024,1024]{1,0:T(8,128)(2,1)S(1)}, bf16[1024,1024]{1,0:T(8,128)(2,1)}, u32[]{:S(2)}, u32[]{:S(2)}) collective-permute-start(bf16[1024,1024]{1,0:T(8,128)(2,1)S(1)} %copy-done.5), channel_id=1, source_target_pairs={{0,4},{4,0},{8,12},{12,8},{16,20},{20,16},{24,28},{28,24},{1,5},{5... | collective-permute-start | bytes 6291464 | tf_op jit(solution)/shard_map/ppermute | solution.py:669
  148.9 188.0 %all-gather.18.cloned.1.call-start = ((), (), s32[]{:S(2)}) async-start(), calls=%async_computation.5 | async-start | bytes 5242880 | tf_op jit(solution)/shard_map/all_gather | solution.py:665
  155.4 48.0 %collective-permute-start.7 = (bf16[1024,1024]{1,0:T(8,128)(2,1)}, bf16[1024,1024]{1,0:T(8,128)(2,1)}, u32[]{:S(2)}, u32[]{:S(2)}) collective-permute-start(bf16[1024,1024]{1,0:T(8,128)(2,1)} %all-gather.12.cloned.1.call-done.refs_7_), channel_id=1, source_target_pairs={{0,4},{4,0},{8,12},{12,8},{16,20},{20,16},{24,28},{28,24},{1,5},{5... | collective-permute-start | bytes 6291464 | tf_op jit(solution)/shard_map/ppermute | solution.py:675
  182.9 5.3 collective-permute-start.6
  190.9 26.5 %collective-permute-start.9 = (bf16[256,2048]{1,0:T(8,128)(2,1)}, bf16[256,2048]{1,0:T(8,128)(2,1)S(1)}, u32[]{:S(2)}, u32[]{:S(2)}) collective-permute-start(bf16[256,2048]{1,0:T(8,128)(2,1)} %add_convert_fusion.4), channel_id=1, source_target_pairs={{0,2},{2,0},{1,3},{3,1},{4,6},{6,4},{5,7},{7,5},{8,10},{10,8},{9,1... | collective-permute-start | bytes 3145736 | tf_op jit(solution)/shard_map/ppermute | solution.py:628
  210.7 6.9 %collective-permute-start.8 = (bf16[256,2048]{1,0:T(8,128)(2,1)}, bf16[256,2048]{1,0:T(8,128)(2,1)S(1)}, u32[]{:S(2)}, u32[]{:S(2)}) collective-permute-start(bf16[256,2048]{1,0:T(8,128)(2,1)} %get-tuple-element.146), channel_id=1, source_target_pairs={{0,1},{1,0},{2,3},{3,2},{4,5},{5,4},{6,7},{7,6},{8,9},{9,8},{10,11... | collective-permute-start | bytes 3145736 | tf_op jit(solution)/shard_map/ppermute | solution.py:625
  212.4 278.8 %all-gather.20.cloned.1.call-start = ((), (), s32[]{:S(2)}) async-start(), calls=%async_computation.6 | async-start | bytes 2007040 | tf_op jit(solution)/shard_map/all_gather | solution.py:989
  213.0 11.3 %collective-permute-start.16 = (bf16[256,2048]{1,0:T(8,128)(2,1)}, bf16[256,2048]{1,0:T(8,128)(2,1)S(1)}, u32[]{:S(2)}, u32[]{:S(2)}) collective-permute-start(bf16[256,2048]{1,0:T(8,128)(2,1)} %collective-permute-done.15), channel_id=1, source_target_pairs={{0,1},{1,0},{2,3},{3,2},{4,5},{5,4},{6,7},{7,6},{8,9},{9,8},{10,11... | collective-permute-start | bytes 3145736 | tf_op jit(solution)/shard_map/ppermute | solution.py:625
  216.2 30.9 %collective-permute-start.12 = (bf16[512,1024]{1,0:T(8,128)(2,1)}, bf16[512,1024]{1,0:T(8,128)(2,1)}, u32[]{:S(2)}, u32[]{:S(2)}) collective-permute-start(bf16[512,1024]{1,0:T(8,128)(2,1)} %get-tuple-element.267), channel_id=1, source_target_pairs={{0,4},{4,0},{8,12},{12,8},{16,20},{20,16},{24,28},{28,24},{1,5},{5... | collective-permute-start | bytes 3145736 | tf_op jit(solution)/shard_map/ppermute | solution.py:675
  217.4 45.9 %collective-permute-start.13 = (bf16[512,1024]{1,0:T(8,128)(2,1)}, bf16[512,1024]{1,0:T(8,128)(2,1)}, u32[]{:S(2)}, u32[]{:S(2)}) collective-permute-start(bf16[512,1024]{1,0:T(8,128)(2,1)} %get-tuple-element.266), channel_id=1, source_target_pairs={{0,4},{4,0},{8,12},{12,8},{16,20},{20,16},{24,28},{28,24},{1,5},{5... | collective-permute-start | bytes 3145736 | tf_op jit(solution)/shard_map/ppermute | solution.py:675
  223.1 40.2 %collective-permute-start.11 = (bf16[256,2048]{1,0:T(8,128)(2,1)S(1)}, bf16[256,2048]{1,0:T(8,128)(2,1)}, u32[]{:S(2)}, u32[]{:S(2)}) collective-permute-start(bf16[256,2048]{1,0:T(8,128)(2,1)S(1)} %get-tuple-element.262), channel_id=1, source_target_pairs={{0,2},{2,0},{1,3},{3,1},{4,6},{6,4},{5,7},{7,5},{8,10},{10,8},{9,1... | collective-permute-start | bytes 3145736 | tf_op jit(solution)/shard_map/ppermute | solution.py:628
  240.7 74.4 %collective-permute-start.18 = (bf16[1024,1024]{1,0:T(8,128)(2,1)}, bf16[1024,1024]{1,0:T(8,128)(2,1)}, u32[]{:S(2)}, u32[]{:S(2)}) collective-permute-start(bf16[1024,1024]{1,0:T(8,128)(2,1)} %all-gather.16.cloned.1.call-done.refs_7_), channel_id=1, source_target_pairs={{0,4},{4,0},{8,12},{12,8},{16,20},{20,16},{24,28},{28,24},{1,5},{5... | collective-permute-start | bytes 6291464 | tf_op jit(solution)/shard_map/ppermute | solution.py:675
  246.0 21.7 %collective-permute-start.10 = (bf16[256,2048]{1,0:T(8,128)(2,1)S(1)}, bf16[256,2048]{1,0:T(8,128)(2,1)S(1)}, u32[]{:S(2)}, u32[]{:S(2)}) collective-permute-start(bf16[256,2048]{1,0:T(8,128)(2,1)S(1)} %get-tuple-element.262), channel_id=1, source_target_pairs={{0,1},{1,0},{2,3},{3,2},{4,5},{5,4},{6,7},{7,6},{8,9},{9,8},{10,11... | collective-permute-start | bytes 3145736 | tf_op jit(solution)/shard_map/ppermute | solution.py:625
  263.3 4.6 collective-permute-start.17
  345.6 9.1 %collective-permute-start.19 = (bf16[256,2048]{1,0:T(8,128)(2,1)}, bf16[256,2048]{1,0:T(8,128)(2,1)S(1)}, u32[]{:S(2)}, u32[]{:S(2)}) collective-permute-start(bf16[256,2048]{1,0:T(8,128)(2,1)} %get-tuple-element.165), channel_id=1, source_target_pairs={{0,1},{1,0},{2,3},{3,2},{4,5},{5,4},{6,7},{7,6},{8,9},{9,8},{10,11... | collective-permute-start | bytes 3145736 | tf_op jit(solution)/shard_map/ppermute | solution.py:625
  357.3 24.8 %collective-permute-start.21 = (bf16[256,2048]{1,0:T(8,128)(2,1)}, bf16[256,2048]{1,0:T(8,128)(2,1)S(1)}, u32[]{:S(2)}, u32[]{:S(2)}) collective-permute-start(bf16[256,2048]{1,0:T(8,128)(2,1)} %add_convert_fusion.2), channel_id=1, source_target_pairs={{0,2},{2,0},{1,3},{3,1},{4,6},{6,4},{5,7},{7,5},{8,10},{10,8},{9,1... | collective-permute-start | bytes 3145736 | tf_op jit(solution)/shard_map/ppermute | solution.py:628
  382.1 3.6 collective-permute-start.22
  391.8 8.2 %collective-permute-start.24 = (bf16[256,2048]{1,0:T(8,128)(2,1)}, bf16[256,2048]{1,0:T(8,128)(2,1)}, u32[]{:S(2)}, u32[]{:S(2)}) collective-permute-start(bf16[256,2048]{1,0:T(8,128)(2,1)} %get-tuple-element.175.first), channel_id=1, source_target_pairs={{0,1},{1,0},{2,3},{3,2},{4,5},{5,4},{6,7},{7,6},{8,9},{9,8},{10,11... | collective-permute-start | bytes 3145736 | tf_op jit(solution)/shard_map/ppermute | solution.py:625
  393.3 24.9 %collective-permute-start.25 = (bf16[256,2048]{1,0:T(8,128)(2,1)}, bf16[256,2048]{1,0:T(8,128)(2,1)S(1)}, u32[]{:S(2)}, u32[]{:S(2)}) collective-permute-start(bf16[256,2048]{1,0:T(8,128)(2,1)} %get-tuple-element.175.first), channel_id=1, source_target_pairs={{0,2},{2,0},{1,3},{3,1},{4,6},{6,4},{5,7},{7,5},{8,10},{10,8},{9,1... | collective-permute-start | bytes 3145736 | tf_op jit(solution)/shard_map/ppermute | solution.py:628
  394.5 14.1 %collective-permute-start.23 = (bf16[256,2048]{1,0:T(8,128)(2,1)}, bf16[256,2048]{1,0:T(8,128)(2,1)}, u32[]{:S(2)}, u32[]{:S(2)}) collective-permute-start(bf16[256,2048]{1,0:T(8,128)(2,1)} %get-tuple-element.178), channel_id=1, source_target_pairs={{0,1},{1,0},{2,3},{3,2},{4,5},{5,4},{6,7},{7,6},{8,9},{9,8},{10,11... | collective-permute-start | bytes 3145736 | tf_op jit(solution)/shard_map/ppermute | solution.py:625
  418.1 3.6 collective-permute-start.26
  427.0 17.9 %collective-permute-start.29 = (bf16[48,512]{1,0:T(8,128)(2,1)S(1)}, bf16[48,512]{1,0:T(8,128)(2,1)S(1)}, u32[]{:S(2)}, u32[]{:S(2)}) collective-permute-start(bf16[48,512]{1,0:T(8,128)(2,1)S(1)} %add_convert_fusion.7), channel_id=1, source_target_pairs={{0,2},{2,0},{1,3},{3,1},{4,6},{6,4},{5,7},{7,5},{8,10},{10,8},{9,1... | collective-permute-start | bytes 147464 | tf_op jit(solution)/shard_map/ppermute | solution.py:628
  447.2 8.1 %collective-permute-start.30 = (bf16[16,6272]{1,0:T(8,128)(2,1)}, bf16[16,6272]{1,0:T(8,128)(2,1)S(1)}, u32[]{:S(2)}, u32[]{:S(2)}) collective-permute-start(bf16[16,6272]{1,0:T(8,128)(2,1)} %flatten.2), channel_id=1, source_target_pairs={{0,4},{4,0},{8,12},{12,8},{16,20},{20,16},{24,28},{28,24},{1,5},{5... | collective-permute-start | bytes 602120 | tf_op jit(solution)/shard_map/ppermute | solution.py:935
  456.2 24.2 %collective-permute-start.28 = (bf16[256,2048]{1,0:T(8,128)(2,1)S(1)}, bf16[256,2048]{1,0:T(8,128)(2,1)}, u32[]{:S(2)}, u32[]{:S(2)}) collective-permute-start(bf16[256,2048]{1,0:T(8,128)(2,1)S(1)} %copy-done.21), channel_id=1, source_target_pairs={{0,2},{2,0},{1,3},{3,1},{4,6},{6,4},{5,7},{7,5},{8,10},{10,8},{9,1... | collective-permute-start | bytes 3145736 | tf_op jit(solution)/shard_map/ppermute | solution.py:628
  489.5 5.1 collective-permute-start.33
  501.8 8.2 %collective-permute-start.34 = (bf16[256,2048]{1,0:T(8,128)(2,1)}, bf16[256,2048]{1,0:T(8,128)(2,1)}, u32[]{:S(2)}, u32[]{:S(2)}) collective-permute-start(bf16[256,2048]{1,0:T(8,128)(2,1)} %back_rows.4), channel_id=1, source_target_pairs={{0,1},{1,0},{2,3},{3,2},{4,5},{5,4},{6,7},{7,6},{8,9},{9,8},{10,11... | collective-permute-start | bytes 3145736 | tf_op jit(solution)/shard_map/ppermute | solution.py:625
  502.6 15.3 %collective-permute-start.20 = (bf16[256,2048]{1,0:T(8,128)(2,1)}, bf16[256,2048]{1,0:T(8,128)(2,1)S(1)}, u32[]{:S(2)}, u32[]{:S(2)}) collective-permute-start(bf16[256,2048]{1,0:T(8,128)(2,1)} %get-tuple-element.170), channel_id=1, source_target_pairs={{0,1},{1,0},{2,3},{3,2},{4,5},{5,4},{6,7},{7,6},{8,9},{9,8},{10,11... | collective-permute-start | bytes 3145736 | tf_op jit(solution)/shard_map/ppermute | solution.py:625
  502.6 10.2 %collective-permute-start.35 = (bf16[8,16,1536]{2,1,0:T(8,128)(2,1)S(1)}, bf16[8,16,1536]{2,1,0:T(8,128)(2,1)S(1)}, u32[]{:S(2)}, u32[]{:S(2)}) collective-permute-start(bf16[8,16,1536]{2,1,0:T(8,128)(2,1)S(1)} %bitcast.164), channel_id=1, source_target_pairs={{0,2},{2,0},{1,3},{3,1},{4,6},{6,4},{5,7},{7,5},{8,10},{10,8},{9,1... | collective-permute-start | bytes 1179656 | tf_op jit(solution)/shard_map/ppermute | solution.py:628
  512.9 29.2 %collective-permute-start.39 = (bf16[256,2048]{1,0:T(8,128)(2,1)}, bf16[256,2048]{1,0:T(8,128)(2,1)}, u32[]{:S(2)}, u32[]{:S(2)}) collective-permute-start(bf16[256,2048]{1,0:T(8,128)(2,1)} %add_convert_fusion), channel_id=1, source_target_pairs={{0,2},{2,0},{1,3},{3,1},{4,6},{6,4},{5,7},{7,5},{8,10},{10,8},{9,1... | collective-permute-start | bytes 3145736 | tf_op jit(solution)/shard_map/ppermute | solution.py:628
  514.0 9.3 %collective-permute-start.36 = (bf16[32,3200]{1,0:T(8,128)(2,1)S(1)}, bf16[32,3200]{1,0:T(8,128)(2,1)S(1)}, u32[]{:S(2)}, u32[]{:S(2)}) collective-permute-start(bf16[32,3200]{1,0:T(8,128)(2,1)S(1)} %pad_maximum_fusion.11.refs_0_), channel_id=1, source_target_pairs={{0,8},{4,12},{8,16},{12,20},{16,24},{20,28},{24,0},{28,4},{1,9},{5... | collective-permute-start | bytes 614408 | tf_op jit(solution)/shard_map/ppermute | solution.py:939
  514.4 15.0 %collective-permute-start.37 = (bf16[32,3200]{1,0:T(8,128)(2,1)S(1)}, bf16[32,3200]{1,0:T(8,128)(2,1)}, u32[]{:S(2)}, u32[]{:S(2)}) collective-permute-start(bf16[32,3200]{1,0:T(8,128)(2,1)S(1)} %pad_maximum_fusion.11.refs_0_), channel_id=1, source_target_pairs={{0,16},{4,20},{8,24},{12,28},{16,0},{20,4},{24,8},{28,12},{1,17},{... | collective-permute-start | bytes 614408 | tf_op jit(solution)/shard_map/ppermute | solution.py:939
  515.8 17.4 %collective-permute-start.38 = (bf16[32,3200]{1,0:T(8,128)(2,1)S(1)}, bf16[32,3200]{1,0:T(8,128)(2,1)}, u32[]{:S(2)}, u32[]{:S(2)}) collective-permute-start(bf16[32,3200]{1,0:T(8,128)(2,1)S(1)} %pad_maximum_fusion.11.refs_0_), channel_id=1, source_target_pairs={{0,24},{4,28},{8,0},{12,4},{16,8},{20,12},{24,16},{28,20},{1,25},{... | collective-permute-start | bytes 614408 | tf_op jit(solution)/shard_map/ppermute | solution.py:939
  542.1 13.2 %collective-permute-start.40 = (bf16[256,2048]{1,0:T(8,128)(2,1)}, bf16[256,2048]{1,0:T(8,128)(2,1)}, u32[]{:S(2)}, u32[]{:S(2)}) collective-permute-start(bf16[256,2048]{1,0:T(8,128)(2,1)} %back_rows.6), channel_id=1, source_target_pairs={{0,1},{1,0},{2,3},{3,2},{4,5},{5,4},{6,7},{7,6},{8,9},{9,8},{10,11... | collective-permute-start | bytes 3145736 | tf_op jit(solution)/shard_map/ppermute | solution.py:625
  547.7 3.5 collective-permute-start.44
  548.2 13.4 %collective-permute-start.41 = (bf16[8,16,1536]{2,1,0:T(8,128)(2,1)}, bf16[8,16,1536]{2,1,0:T(8,128)(2,1)}, u32[]{:S(2)}, u32[]{:S(2)}) collective-permute-start(bf16[8,16,1536]{2,1,0:T(8,128)(2,1)} %bitcast.166), channel_id=1, source_target_pairs={{0,1},{1,0},{2,3},{3,2},{4,5},{5,4},{6,7},{7,6},{8,9},{9,8},{10,11... | collective-permute-start | bytes 1179656 | tf_op jit(solution)/shard_map/ppermute | solution.py:625
  548.2 12.8 %collective-permute-start.42 = (bf16[8,16,1536]{2,1,0:T(8,128)(2,1)}, bf16[8,16,1536]{2,1,0:T(8,128)(2,1)}, u32[]{:S(2)}, u32[]{:S(2)}) collective-permute-start(bf16[8,16,1536]{2,1,0:T(8,128)(2,1)} %bitcast.167), channel_id=1, source_target_pairs={{0,2},{2,0},{1,3},{3,1},{4,6},{6,4},{5,7},{7,5},{8,10},{10,8},{9,1... | collective-permute-start | bytes 1179656 | tf_op jit(solution)/shard_map/ppermute | solution.py:628
  (113 other events, 1746.2 us)
Sparse Core Ops, SparseCore 0:
  10.2 45.3 all-gather.9
  57.7 44.4 all-gather.7
  104.3 44.4 all-gather.11
  150.3 44.4 all-gather.13
  196.2 44.4 all-gather.15
  242.7 79.2 all-gather.17
  456.3 34.9 all-gather.19

commit v4 on v3

--- a/solution.py
+++ b/solution.py
@@ -39,6 +39,39 @@
     return lax.dot_general(
         left, right, (((0,), (0,)), ((), ())), preferred_element_type=F32
     )
+
+
+def join_kernel(*refs):
+    *blocks, down, out, rank = refs
+    for k, block in enumerate(blocks):
+
+        @pl.when(pl.program_id(0) == k)
+        def _(block=block):
+            out[...] = block[...]
+            rank[...] = product_cols(block[...], down[...]).astype(BF)
+
+
+def join_rows(blocks, down):
+    tile, feats = blocks[0].shape
+    rank = down.shape[0]
+    return pl.pallas_call(
+        join_kernel,
+        grid=(len(blocks),),
+        in_specs=[
+            pl.BlockSpec(v.shape, lambda i: (0, 0), pipeline_mode=pl.Buffered(1))
+            for v in (*blocks, down)
+        ],
+        out_specs=[
+            pl.BlockSpec((tile, feats), lambda i: (i, 0)),
+            pl.BlockSpec((tile, rank), lambda i: (i, 0)),
+        ],
+        out_shape=[
+            jax.ShapeDtypeStruct((len(blocks) * tile, feats), BF),
+            jax.ShapeDtypeStruct((len(blocks) * tile, rank), BF),
+        ],
+        cost_estimate=pl.CostEstimate(flops=10**6, bytes_accessed=10**5, transcendentals=0),
+        name="join_rows",
+    )(*blocks, down)
 
 
 def feed_kernel(first, last, pieces, *refs):
@@ -151,7 +184,7 @@
         wide_shapes = [jax.ShapeDtypeStruct((tile, feats), BF)] * (2 * count)
     else:
         wide_specs = [out_block(feats)] * 2
-        wide_shapes = [jax.ShapeDtypeStruct((size, feats), F32)] * 2
+        wide_shapes = [jax.ShapeDtypeStruct((size, feats), BF)] * 2
     results = pl.pallas_call(
         functools.partial(feed_kernel, first, last, len(weight)),
         grid=(count,),
@@ -676,6 +709,10 @@
         ]
         return [(v, 0) for v in (own, *swapped)]
 
+    def swap_after(pieces, *held):
+        own = pieces[0][0]
+        return [(own, 0), (lax.ppermute(after(own, *held), "dp", dp_pairs), 0)]
+
     def fetch_paired(pair, *held):
         both = line_gather(pair, held)
         return [(both, 0), (both, 1)]
@@ -714,13 +751,6 @@
     last_pair = jnp.concatenate([last_shard, lax.ppermute(last_shard, "dp", dp_pairs)], axis=1)
     weight_qk = fetch(jnp.concatenate([query_weight, key_weight], axis=1))
     weight_vo = fetch(jnp.concatenate([value_weight, output_turned], axis=1))
-    weight_ffn, held = [], [weight_qk[0], weight_vo[0]]
-    for h in range(chunk_count - 1):
-        more = (last_pair,) if h == 0 else ()
-        weight_ffn.append(fetch_pieces(feed_shard(h), 2 if h == 1 else 1, held[h], *more))
-        held.append(weight_ffn[-1][0][0])
-    weight_ffn.append(fetch_paired(last_pair, held[-2]))
-
     select = (jnp.arange(slot_count, dtype=jnp.int32) == adapter_choice[0]).astype(BF)
 
     def adapter_of(adapter_table):
@@ -773,6 +803,13 @@
     head_count = width_local // HEAD_DIM
 
     rank_one = product_cols(full_one, down_qkv).astype(BF)
+    weight_ffn, held = [], [weight_qk[0], weight_vo[0]]
+    for h in range(chunk_count - 1):
+        more = (last_pair, rank_one) if h == 0 else ()
+        weight_ffn.append(fetch_pieces(feed_shard(h), 2 if h == 1 else 1, held[h], *more))
+        held.append(weight_ffn[-1][0][0])
+    weight_ffn.append(fetch_paired(last_pair, held[-2]))
+
     rank_query = rank_one[:, :rank_width]
     rank_key = rank_one[:, rank_width : 2 * rank_width]
     rank_value = rank_one[:, 2 * rank_width :]
@@ -823,8 +860,11 @@
     residual = inputs_wide + main_rows + out_bias
     unit_two, scale_two = normalize(residual)
     rows_two = (unit_two * gain_b + shift_b).astype(BF)
-    full_two = after(gather_rows(rows_two, weight_ffn[1][1][0], weight_ffn[1][2][0], rank_grad), held[4])
-    rank_two = product_cols(full_two, down_expand).astype(BF)
+    near_two = to_core(rows_two)
+    far_two = after(to_chip(rows_two), weight_ffn[1][1][0], weight_ffn[1][2][0], rank_grad)
+    weight_ffn[2] = swap_after(weight_ffn[2], far_two)
+    last_two = to_core(far_two)
+    full_two, rank_two = join_rows([rows_two, near_two, far_two, last_two], down_expand)
 
     state = None
     down_parts, up_parts = [], []

time: 582 us -> 568 us (0.976)
  other arithmetic: 59.2 us -> 50.5 us
  matrix products: 54.8 us -> 46.5 us
  Pallas kernels: 215 us -> 208 us
  waiting for transfers between devices: 159 us -> 165 us
    ppermute x4 -> x3, waiting for transfers between devices: 27.4 us -> 45.5 us  [fetch_pieces(): lax.ppermute(own[k * size:(k + 1) * size], 'dp', dp_pairs)]
    pallas_call x6, Pallas kernels: 93 us -> 80.6 us  [feed_forward(): pl.pallas_call(functools.partial(feed_kernel, first, last, len(weight)),...]
    all_gather x6, waiting for transfers between devices: 87.9 us -> 77.3 us  [line_gather(): lax.all_gather(shard, 'dp', axis=0, tiled=True, axis_index_groups=line_gr...]
    concatenate x3 -> x2, other arithmetic: 11.5 us -> 4.13 us  [gather_rows(): return jnp.concatenate([rows, near, far, far_near], axis=0)]
    unnamed x219 -> x195, local copies, waits for them, and re-layouts: 9.98 us -> 15 us
  transfers between devices with their start and end apart: 53 -> 53, of which waited for: 21 -> 21; matrix products, arithmetic and copies ran while one was open for 21% -> 18% of each run, Pallas kernels for 32% -> 32%
where the time goes in v4:
time: 568 us; the launch traced here: 560 us
  Pallas kernels  208 us (37%)
  waiting for transfers between devices  165 us (29%)
  other arithmetic  50.5 us (9%)
  matrix products  46.5 us (8%)
  starting transfers between devices  46.3 us (8%)
  local copies, waits for them, and re-layouts  25.9 us (5%)
  between operations  17 us (3%)
    pallas_call x6, Pallas kernels, feed_forward(): pl.pallas_call(functools.partial(feed_kernel, first, last, len(weight)),...  80.6 us
    all_gather x6, waiting for transfers between devices, line_gather(): lax.all_gather(shard, 'dp', axis=0, tiled=True, axis_index_groups=line_gr...  77.3 us
    ppermute x3, waiting for transfers between devices, fetch_pieces(): lax.ppermute(own[k * size:(k + 1) * size], 'dp', dp_pairs)  45.5 us
    pallas_call x4, Pallas kernels, by_head(): pl.pallas_call(functools.partial(kernel, HEAD_DIM ** (-0.5)), grid_spec=p...  36.2 us
    ppermute x12, waiting for transfers between devices, to_chip(): return lax.ppermute(v, 'tensor', chip_pairs)  25.7 us
    pallas_call x4, Pallas kernels, back_rows(): pl.pallas_call(back_kernel, grid=(count,), in_specs=[pl.BlockSpec((tile,...  24.8 us
    ppermute x22, starting transfers between devices, to_core(): return lax.ppermute(v, 'tensor', core_pairs)  21.9 us
    pallas_call x5, Pallas kernels, local_call(): pl.pallas_call(kernel, in_specs=specs, out_specs=out_specs, out_shape=[ja...  21.3 us
  transfers between devices with their start and end apart: 53, of which 21 were waited for; matrix products, arithmetic and copies ran while one was open for 18% of the time, Pallas kernels for 32%

profile of v4, /device:TPU:17, one launch (start us, length us, event | category | flops | bytes accessed | tf_op | source)
XLA Modules:
  0.0 559.5 jit_solution(15350526608226173653)
XLA Ops:
  46.9 8.6 %all-gather.10.cloned.1.call-done.qk_own = bf16[1024,1024]{1,0:T(8,128)(2,1)} async-done(((bf16[256,1024]{1,0:T(8,128)(2,1)}), bf16[1024,1024]{1,0:T(8,128)(2,1)}) %all-gather.10.cloned.1.call-update) | async-done | bytes 2097168 | tf_op jit(solution)/shard_map/all_gather | solution.py:698
  60.3 41.9 %all-gather.8.cloned.1.call-done.own.vo_own = bf16[1024,1024]{1,0:T(8,128)(2,1)} async-done(((bf16[256,1024]{1,0:T(8,128)(2,1)}), bf16[1024,1024]{1,0:T(8,128)(2,1)}) %all-gather.8.cloned.1.call-update) | async-done | bytes 2097168 | tf_op jit(solution)/shard_map/all_gather | solution.py:698
  103.8 3.3 fusion.1.refs_12_.refs_16_
  110.2 4.9 fusion.23
  115.1 4.0 fusion.27
  122.5 26.3 %all-gather.12.cloned.1.call-done.refs_7_ = bf16[1024,1024]{1,0:T(8,128)(2,1)} async-done(((bf16[256,1024]{1,0:T(8,128)(2,1)}), bf16[1024,1024]{1,0:T(8,128)(2,1)}) %all-gather.12.cloned.1.call-update) | async-done | bytes 2097168 | tf_op jit(solution)/shard_map/all_gather | solution.py:698
  149.4 3.1 fusion.16.refs_4_.refs_5_.refs_6_.refs_7_
  153.6 3.7 fusion.19
  159.5 12.5 %attend.1 = (bf16[1024,512]{1,0:T(8,128)(2,1)}, f32[1024,512]{1,0:T(8,128)}) custom-call(s32[1]{0:T(128)} %bitcast.1.turn, bf16[1024,512]{1,0:T(8,128)(2,1)} %fusion.18.refs_0_.refs_1_.refs_2_.refs_3_, bf16[1024,512]{1,0:T(8,128)(2,1)} %fusion.18.refs_0_.refs_1_.refs_2_.refs_3_, bf16[1024,512]{1,0:T(8,128)(2,1)} %fusion.18.refs_0_.refs_1_.refs_2_.refs_3_, ...), custom_call_target="tpu_custom_call" | custom-call | flops 100000000 | bytes 1000000 | tf_op jit(solution)/shard_map/attend/pallas_call | solution.py:306
  172.1 7.3 %out_rows.2 = (bf16[256,2048]{1,0:T(8,128)(2,1)}, bf16[256,2048]{1,0:T(8,128)(2,1)}) custom-call(bf16[1024,512]{1,0:T(8,128)(2,1)} %get-tuple-element.146.rows, bf16[16,512]{1,0:T(8,128)(2,1)} %bitcast.133, bf16[16,2048]{1,0:T(8,128)(2,1)} %copy-done.24, bf16[1024,1024]{1,0:T(8,128)(2,1)} %all-gather.8.cloned.1.call-done.own.vo_own, ...), custom_call_target="tpu_custom_call" | custom-call | flops 10000000 | bytes 100000 | tf_op jit(solution)/shard_map/out_rows/pallas_call | solution.py:391
  186.8 12.3 %collective-permute-done.7.refs_8_ = bf16[1024,1024]{1,0:T(8,128)(2,1)} collective-permute-done((bf16[1024,1024]{1,0:T(8,128)(2,1)}, bf16[1024,1024]{1,0:T(8,128)(2,1)}, u32[]{:S(2)}, u32[]{:S(2)}) %collective-permute-start.7) | collective-permute-done | bytes 2097184 | tf_op jit(solution)/shard_map/ppermute | solution.py:708
  199.1 7.2 %out_rows.3 = (bf16[256,2048]{1,0:T(8,128)(2,1)}, bf16[256,2048]{1,0:T(8,128)(2,1)}) custom-call(bf16[1024,512]{1,0:T(8,128)(2,1)} %get-tuple-element.146.rows, bf16[16,512]{1,0:T(8,128)(2,1)} %bitcast.134, bf16[16,2048]{1,0:T(8,128)(2,1)} %copy-done.24, bf16[1024,1024]{1,0:T(8,128)(2,1)} %all-gather.8.cloned.1.call-done.own.vo_own, ...), custom_call_target="tpu_custom_call" | custom-call | flops 10000000 | bytes 100000 | tf_op jit(solution)/shard_map/out_rows/pallas_call | solution.py:391
  222.8 11.8 %collective-permute-done.12.refs_8_ = bf16[512,1024]{1,0:T(8,128)(2,1)S(1)} collective-permute-done((bf16[512,1024]{1,0:T(8,128)(2,1)S(1)}, bf16[512,1024]{1,0:T(8,128)(2,1)S(1)}, u32[]{:S(2)}, u32[]{:S(2)}) %collective-permute-start.12) | collective-permute-done | bytes 1048608 | tf_op jit(solution)/shard_map/ppermute | solution.py:708
  235.5 21.4 %collective-permute-done.13.refs_9_ = bf16[512,1024]{1,0:T(8,128)(2,1)S(1)} collective-permute-done((bf16[512,1024]{1,0:T(8,128)(2,1)S(1)}, bf16[512,1024]{1,0:T(8,128)(2,1)S(1)}, u32[]{:S(2)}, u32[]{:S(2)}) %collective-permute-start.13) | collective-permute-done | bytes 1048608 | tf_op jit(solution)/shard_map/ppermute | solution.py:708
  265.1 5.7 %join_rows.1 = (bf16[1024,2048]{1,0:T(8,128)(2,1)}, bf16[1024,16]{1,0:T(8,128)(2,1)}) custom-call(bf16[256,2048]{1,0:T(8,128)(2,1)} %copy-done.18, bf16[256,2048]{1,0:T(8,128)(2,1)} %copy-done.38, bf16[256,2048]{1,0:T(8,128)(2,1)} %collective-permute-done.11.refs_2_, bf16[256,2048]{1,0:T(8,128)(2,1)} %collective-permute-done.17.refs_3_, ...), custom_call_target="tpu_custom_call" | custom-call | flops 1000000 | bytes 100000 | tf_op jit(solution)/shard_map/join_rows/pallas_call | solution.py:57
  270.8 16.0 %feed_forward.6 = (bf16[1024,2048]{1,0:T(8,128)(2,1)}, bf16[1024,2048]{1,0:T(8,128)(2,1)}, f32[1024,16]{1,0:T(8,128)}, f32[1024,16]{1,0:T(8,128)}, f32[16,512]{1,0:T(8,128)}, /*index=5*/f32[16,512]{1,0:T(8,128)}) custom-call(bf16[1024,2048]{1,0:T(8,128)(2,1)} %get-tuple-element.172.refs_0_, bf16[1024,2048]{1,0:T(8,128)(2,1)} %copy-done.2, ...), custom_call_target="tpu_custom_call" | custom-call | flops 1073741824 | bytes 41943040 | tf_op jit(solution)/shard_map/feed_forward/pallas_call | solution.py:188
  286.8 17.2 %feed_forward.7 = (bf16[1024,2048]{1,0:T(8,128)(2,1)}, bf16[1024,2048]{1,0:T(8,128)(2,1)}, f32[1024,16]{1,0:T(8,128)}, f32[1024,16]{1,0:T(8,128)}, f32[16,512]{1,0:T(8,128)}, /*index=5*/f32[16,512]{1,0:T(8,128)}) custom-call(bf16[1024,2048]{1,0:T(8,128)(2,1)} %get-tuple-element.172.refs_0_, bf16[1024,2048]{1,0:T(8,128)(2,1)} %copy-done.2, ...), custom_call_target="tpu_custom_call" | custom-call | flops 1073741824 | bytes 41943040 | tf_op jit(solution)/shard_map/feed_forward/pallas_call | solution.py:188
  304.1 17.4 %feed_forward.8 = (bf16[1024,2048]{1,0:T(8,128)(2,1)}, bf16[1024,2048]{1,0:T(8,128)(2,1)}, f32[1024,16]{1,0:T(8,128)}, f32[1024,16]{1,0:T(8,128)}, f32[16,512]{1,0:T(8,128)}, /*index=5*/f32[16,512]{1,0:T(8,128)}) custom-call(bf16[1024,2048]{1,0:T(8,128)(2,1)} %get-tuple-element.172.refs_0_, bf16[1024,2048]{1,0:T(8,128)(2,1)} %copy-done.2, ...), custom_call_target="tpu_custom_call" | custom-call | flops 1073741824 | bytes 41943040 | tf_op jit(solution)/shard_map/feed_forward/pallas_call | solution.py:188
  321.9 8.0 %feed_forward.9 = (bf16[256,2048]{1,0:T(8,128)(2,1)}, bf16[256,2048]{1,0:T(8,128)(2,1)}, f32[256,16]{1,0:T(8,128)}, f32[256,16]{1,0:T(8,128)}, f32[16,512]{1,0:T(8,128)}, /*index=5*/f32[16,512]{1,0:T(8,128)}) custom-call(bf16[1024,2048]{1,0:T(8,128)(2,1)} %get-tuple-element.172.refs_0_, bf16[1024,2048]{1,0:T(8,128)(2,1)} %copy-done.2, ...), custom_call_target="tpu_custom_call" | custom-call | flops 268435456 | bytes 10485760 | tf_op jit(solution)/shard_map/feed_forward/pallas_call | solution.py:188
  331.8 8.0 %feed_forward.10 = (bf16[256,2048]{1,0:T(8,128)(2,1)}, bf16[256,2048]{1,0:T(8,128)(2,1)}, f32[256,16]{1,0:T(8,128)}, f32[256,16]{1,0:T(8,128)}, f32[16,512]{1,0:T(8,128)}, /*index=5*/f32[16,512]{1,0:T(8,128)}) custom-call(bf16[1024,2048]{1,0:T(8,128)(2,1)} %get-tuple-element.172.refs_0_, bf16[1024,2048]{1,0:T(8,128)(2,1)} %copy-done.2, ...), custom_call_target="tpu_custom_call" | custom-call | flops 268435456 | bytes 10485760 | tf_op jit(solution)/shard_map/feed_forward/pallas_call | solution.py:188
  343.5 14.0 %feed_forward.11 = (bf16[256,2048]{1,0:T(8,128)(2,1)}, bf16[256,2048]{1,0:T(8,128)(2,1)}, bf16[256,2048]{1,0:T(8,128)(2,1)}, bf16[256,2048]{1,0:T(8,128)(2,1)}, ...) custom-call(bf16[1024,2048]{1,0:T(8,128)(2,1)} %get-tuple-element.172.refs_0_, ...), custom_call_target="tpu_custom_call" | custom-call | flops 536870912 | bytes 20971520 | tf_op jit(solution)/shard_map/feed_forward/pallas_call | solution.py:188
  357.6 9.7 %collective-permute-done.21.far = bf16[256,2048]{1,0:T(8,128)(2,1)S(1)} collective-permute-done((bf16[256,2048]{1,0:T(8,128)(2,1)}, bf16[256,2048]{1,0:T(8,128)(2,1)S(1)}, u32[]{:S(2)}, u32[]{:S(2)}) %collective-permute-start.21) | collective-permute-done | bytes 1048608 | tf_op jit(solution)/shard_map/ppermute | solution.py:661
  370.8 6.0 %branch_rows.1 = (f32[256,2048]{1,0:T(8,128)}, bf16[256,2048]{1,0:T(8,128)(2,1)}) custom-call(bf16[256,2048]{1,0:T(8,128)(2,1)} %get-tuple-element.176.zero, bf16[256,2048]{1,0:T(8,128)(2,1)} %collective-permute-done.22.one, bf16[256,2048]{1,0:T(8,128)(2,1)} %copy-done.31, bf16[256,2048]{1,0:T(8,128)(2,1)} %constant_dynamic-update-slice_fusion.30.base, ...), custom_call_target="tpu_custom_call" | custom-call | flops 10000000 | bytes 1000000 | tf_op jit(solution)/shard_map/branch_rows/pallas_call | solution.py:340
  380.1 3.7 fusion.142.refs_1_
  385.1 4.9 in_rows.2
  393.8 2.6 add_convert_fusion.1
  396.4 6.8 %collective-permute-done.25.refs_4_.first = bf16[256,2048]{1,0:T(8,128)(2,1)S(1)} collective-permute-done((bf16[256,2048]{1,0:T(8,128)(2,1)}, bf16[256,2048]{1,0:T(8,128)(2,1)S(1)}, u32[]{:S(2)}, u32[]{:S(2)}) %collective-permute-start.25) | collective-permute-done | bytes 1048608 | tf_op jit(solution)/shard_map/ppermute | solution.py:661
  406.9 2.9 pack.1
  413.4 4.9 in_rows.3
  423.5 6.6 %attend_back.3 = (bf16[1024,512]{1,0:T(8,128)(2,1)}, bf16[1024,512]{1,0:T(8,128)(2,1)}, bf16[1024,512]{1,0:T(8,128)(2,1)}) custom-call(s32[1]{0:T(128)} %bitcast.1.turn, bf16[1024,512]{1,0:T(8,128)(2,1)} %fusion.18.refs_0_.refs_1_.refs_2_.refs_3_, bf16[1024,512]{1,0:T(8,128)(2,1)} %fusion.18.refs_0_.refs_1_.refs_2_.refs_3_, ...), custom_call_target="tpu_custom_call" | custom-call | flops 100000000 | bytes 1000000 | tf_op jit(solution)/shard_map/attend_back/pallas_call | solution.py:306
  433.6 6.9 %attend_back.4 = (bf16[1024,512]{1,0:T(8,128)(2,1)}, bf16[1024,512]{1,0:T(8,128)(2,1)}, bf16[1024,512]{1,0:T(8,128)(2,1)}) custom-call(s32[1]{0:T(128)} %bitcast.1.turn, bf16[1024,512]{1,0:T(8,128)(2,1)} %fusion.18.refs_0_.refs_1_.refs_2_.refs_3_, ...), custom_call_target="tpu_custom_call", output_to_operand_aliasing={{0}: (19, {}), {1}: (20, {}), {2}: (21, {})} | custom-call | flops 100000000 | bytes 1000000 | tf_op jit(solution)/shard_map/attend_back/pallas_call | solution.py:306
  441.6 10.2 %attend_back.5 = (bf16[1024,512]{1,0:T(8,128)(2,1)}, bf16[1024,512]{1,0:T(8,128)(2,1)}, bf16[1024,512]{1,0:T(8,128)(2,1)}) custom-call(s32[1]{0:T(128)} %bitcast.1.turn, bf16[1024,512]{1,0:T(8,128)(2,1)} %fusion.18.refs_0_.refs_1_.refs_2_.refs_3_, ...), custom_call_target="tpu_custom_call", output_to_operand_aliasing={{0}: (19, {}), {1}: (20, {}), {2}: (21, {})} | custom-call | flops 100000000 | bytes 1000000 | tf_op jit(solution)/shard_map/attend_back/pallas_call | solution.py:306
  451.8 7.5 %late_deltas.1 = (bf16[1024,48]{1,0:T(8,128)(2,1)}, bf16[48,512]{1,0:T(8,128)(2,1)}, bf16[96,512]{1,0:T(8,128)(2,1)}, bf16[48,512]{1,0:T(8,128)(2,1)}, f32[16,51...) custom-call(s32[2]{0:T(128)} %pad_add_fusion.place, bf16[1024,512]{1,0:T(8,128)(2,1)} %get-tuple-element.224.refs_0_.query, ...), custom_call_target="tpu_custom_call" | custom-call | flops 1000000 | bytes 100000 | tf_op jit(solution)/shard_map/late_deltas/pallas_call | solution.py:544
  459.3 6.2 %collective-permute-done.28.far = bf16[256,2048]{1,0:T(8,128)(2,1)} collective-permute-done((bf16[256,2048]{1,0:T(8,128)(2,1)S(1)}, bf16[256,2048]{1,0:T(8,128)(2,1)}, u32[]{:S(2)}, u32[]{:S(2)}) %collective-permute-start.28) | collective-permute-done | bytes 1048608 | tf_op jit(solution)/shard_map/ppermute | solution.py:661
  469.3 3.1 collective-permute-done.32.refs_2_
  476.5 3.4 sum_slots.2
  480.8 6.2 %back_rows.4 = bf16[256,2048]{1,0:T(8,128)(2,1)} custom-call(bf16[1024,512]{1,0:T(8,128)(2,1)} %get-tuple-element.224.refs_0_.query, bf16[1024,512]{1,0:T(8,128)(2,1)} %get-tuple-element.225.refs_1_.key, bf16[1024,512]{1,0:T(8,128)(2,1)} %get-tuple-element.226.refs_2_.value, bf16[1024,48]{1,0:T(8,128)(2,1)} %get-tuple-element.245.rank, ...), custom_call_target="tpu_custom_call" | custom-call | flops 100000000 | bytes 1000000 | tf_op jit(solution)/shard_map/back_rows/pallas_call | solution.py:410
  489.1 6.1 %back_rows.5 = bf16[256,2048]{1,0:T(8,128)(2,1)} custom-call(bf16[1024,512]{1,0:T(8,128)(2,1)} %get-tuple-element.224.refs_0_.query, bf16[1024,512]{1,0:T(8,128)(2,1)} %get-tuple-element.225.refs_1_.key, bf16[1024,512]{1,0:T(8,128)(2,1)} %get-tuple-element.226.refs_2_.value, bf16[1024,48]{1,0:T(8,128)(2,1)} %get-tuple-element.245.rank, ...), custom_call_target="tpu_custom_call" | custom-call | flops 100000000 | bytes 1000000 | tf_op jit(solution)/shard_map/back_rows/pallas_call | solution.py:410
  495.2 2.9 add_convert_fusion
  504.1 4.5 output.1
  508.6 6.3 %back_rows.6 = bf16[256,2048]{1,0:T(8,128)(2,1)} custom-call(bf16[1024,512]{1,0:T(8,128)(2,1)} %get-tuple-element.224.refs_0_.query, bf16[1024,512]{1,0:T(8,128)(2,1)} %get-tuple-element.225.refs_1_.key, bf16[1024,512]{1,0:T(8,128)(2,1)} %get-tuple-element.226.refs_2_.value, bf16[1024,48]{1,0:T(8,128)(2,1)} %get-tuple-element.245.rank, ...), custom_call_target="tpu_custom_call" | custom-call | flops 100000000 | bytes 1000000 | tf_op jit(solution)/shard_map/back_rows/pallas_call | solution.py:410
  514.9 3.6 collective-permute-done.38.refs_3_
  518.4 6.2 %back_rows.7 = bf16[256,2048]{1,0:T(8,128)(2,1)} custom-call(bf16[1024,512]{1,0:T(8,128)(2,1)} %get-tuple-element.224.refs_0_.query, bf16[1024,512]{1,0:T(8,128)(2,1)} %get-tuple-element.225.refs_1_.key, bf16[1024,512]{1,0:T(8,128)(2,1)} %get-tuple-element.226.refs_2_.value, bf16[1024,48]{1,0:T(8,128)(2,1)} %get-tuple-element.245.rank, ...), custom_call_target="tpu_custom_call" | custom-call | flops 100000000 | bytes 1000000 | tf_op jit(solution)/shard_map/back_rows/pallas_call | solution.py:410
  524.7 2.8 sum_slots.3
  527.4 5.6 %collective-permute-start.40 = (bf16[256,2048]{1,0:T(8,128)(2,1)}, bf16[256,2048]{1,0:T(8,128)(2,1)}, u32[]{:S(2)}, u32[]{:S(2)}) collective-permute-start(bf16[256,2048]{1,0:T(8,128)(2,1)} %back_rows.6), channel_id=1, source_target_pairs={{0,1},{1,0},{2,3},{3,2},{4,5},{5,4},{6,7},{7,6},{8,9},{9,8},{10,11... | collective-permute-start | bytes 3145736 | tf_op jit(solution)/shard_map/ppermute | solution.py:658
  537.4 3.2 across.2
  543.3 2.7 fusion.13
  549.2 3.2 across.3
  (504 shorter events, 149.3 us)
Async XLA Ops:
  7.2 48.4 %all-gather.10.cloned.1.call-start = ((), (), s32[]{:S(2)}) async-start(), calls=%async_computation.1 | async-start | bytes 2621440 | tf_op jit(solution)/shard_map/all_gather | solution.py:698
  9.3 92.9 %all-gather.8.cloned.1.call-start = ((), (), s32[]{:S(2)}) async-start(), calls=%async_computation | async-start | bytes 2621440 | tf_op jit(solution)/shard_map/all_gather | solution.py:698
  12.1 24.5 %collective-permute-start.1 = (bf16[256,2048]{1,0:T(8,128)(2,1)S(1)}, bf16[256,2048]{1,0:T(8,128)(2,1)}, u32[]{:S(2)}, u32[]{:S(2)}) collective-permute-start(bf16[256,2048]{1,0:T(8,128)(2,1)S(1)} %fusion.8), channel_id=1, source_target_pairs={{0,2},{2,0},{1,3},{3,1},{4,6},{6,4},{5,7},{7,5},{8,10},{10,8},{9,1... | collective-permute-start | bytes 3145736 | tf_op jit(solution)/shard_map/ppermute | solution.py:661
  13.4 28.3 %collective-permute-start = (bf16[256,2048]{1,0:T(8,128)(2,1)S(1)}, bf16[256,2048]{1,0:T(8,128)(2,1)}, u32[]{:S(2)}, u32[]{:S(2)}) collective-permute-start(bf16[256,2048]{1,0:T(8,128)(2,1)S(1)} %fusion.8), channel_id=1, source_target_pairs={{0,1},{1,0},{2,3},{3,2},{4,5},{5,4},{6,7},{7,6},{8,9},{9,8},{10,11... | collective-permute-start | bytes 3145736 | tf_op jit(solution)/shard_map/ppermute | solution.py:658
  19.9 188.3 %collective-permute-start.15 = (bf16[256,2048]{1,0:T(8,128)(2,1)}, bf16[256,2048]{1,0:T(8,128)(2,1)}, u32[]{:S(2)}, u32[]{:S(2)}) collective-permute-start(bf16[256,2048]{1,0:T(8,128)(2,1)} %constant_dynamic-update-slice_fusion.30.base), channel_id=1, source_target_pairs={{0,2},{2,0},{1,3},{3,1},{4,6},{6,4},{5,7},{7,5},{8,10},{10,8},{9,1... | collective-permute-start | bytes 3145736 | tf_op jit(solution)/shard_map/ppermute | solution.py:661
  20.2 198.1 %collective-permute-start.14 = (bf16[256,2048]{1,0:T(8,128)(2,1)}, bf16[256,2048]{1,0:T(8,128)(2,1)}, u32[]{:S(2)}, u32[]{:S(2)}) collective-permute-start(bf16[256,2048]{1,0:T(8,128)(2,1)} %constant_dynamic-update-slice_fusion.30.base), channel_id=1, source_target_pairs={{0,1},{1,0},{2,3},{3,2},{4,5},{5,4},{6,7},{7,6},{8,9},{9,8},{10,11... | collective-permute-start | bytes 3145736 | tf_op jit(solution)/shard_map/ppermute | solution.py:658
  25.1 14.4 %collective-permute-start.4 = (bf16[256,1024]{1,0:T(8,128)(2,1)}, bf16[256,1024]{1,0:T(8,128)(2,1)}, u32[]{:S(2)}, u32[]{:S(2)}) collective-permute-start(bf16[256,1024]{1,0:T(8,128)(2,1)} %pad_maximum_fusion.6), channel_id=1, source_target_pairs={{0,4},{4,0},{8,12},{12,8},{16,20},{20,16},{24,28},{28,24},{1,5},{5... | collective-permute-start | bytes 1572872 | tf_op jit(solution)/shard_map/ppermute | solution.py:751
  29.3 119.6 %all-gather.12.cloned.1.call-start = ((), (), s32[]{:S(2)}) async-start(), calls=%async_computation.2 | async-start | bytes 2621440 | tf_op jit(solution)/shard_map/all_gather | solution.py:698
  36.7 5.1 collective-permute-start.2
  55.6 152.5 %all-gather.14.cloned.1.call-start = ((), (), s32[]{:S(2)}) async-start(), calls=%async_computation.3 | async-start | bytes 2621440 | tf_op jit(solution)/shard_map/all_gather | solution.py:698
  58.5 51.7 %collective-permute-start.3 = (bf16[1024,1024]{1,0:T(8,128)(2,1)}, bf16[1024,1024]{1,0:T(8,128)(2,1)}, u32[]{:S(2)}, u32[]{:S(2)}) collective-permute-start(bf16[1024,1024]{1,0:T(8,128)(2,1)} %all-gather.10.cloned.1.call-done.qk_own), channel_id=1, source_target_pairs={{0,4},{4,0},{8,12},{12,8},{16,20},{20,16},{24,28},{28,24},{1,5},{5... | collective-permute-start | bytes 6291464 | tf_op jit(solution)/shard_map/ppermute | solution.py:702
  102.2 155.7 %all-gather.18.cloned.1.call-start = ((), (), s32[]{:S(2)}) async-start(), calls=%async_computation.5 | async-start | bytes 2621440 | tf_op jit(solution)/shard_map/all_gather | solution.py:698
  107.1 46.5 %collective-permute-start.5 = (bf16[1024,1024]{1,0:T(8,128)(2,1)S(1)}, bf16[1024,1024]{1,0:T(8,128)(2,1)}, u32[]{:S(2)}, u32[]{:S(2)}) collective-permute-start(bf16[1024,1024]{1,0:T(8,128)(2,1)S(1)} %copy-done.5), channel_id=1, source_target_pairs={{0,4},{4,0},{8,12},{12,8},{16,20},{20,16},{24,28},{28,24},{1,5},{5... | collective-permute-start | bytes 6291464 | tf_op jit(solution)/shard_map/ppermute | solution.py:702
  148.9 173.0 %all-gather.16.cloned.1.call-start = ((), (), s32[]{:S(2)}) async-start(), calls=%async_computation.4 | async-start | bytes 5242880 | tf_op jit(solution)/shard_map/all_gather | solution.py:698
  152.4 46.7 %collective-permute-start.7 = (bf16[1024,1024]{1,0:T(8,128)(2,1)}, bf16[1024,1024]{1,0:T(8,128)(2,1)}, u32[]{:S(2)}, u32[]{:S(2)}) collective-permute-start(bf16[1024,1024]{1,0:T(8,128)(2,1)} %all-gather.12.cloned.1.call-done.refs_7_), channel_id=1, source_target_pairs={{0,4},{4,0},{8,12},{12,8},{16,20},{20,16},{24,28},{28,24},{1,5},{5... | collective-permute-start | bytes 6291464 | tf_op jit(solution)/shard_map/ppermute | solution.py:708
  179.4 3.6 collective-permute-start.6
  185.6 25.8 %collective-permute-start.9 = (bf16[256,2048]{1,0:T(8,128)(2,1)}, bf16[256,2048]{1,0:T(8,128)(2,1)S(1)}, u32[]{:S(2)}, u32[]{:S(2)}) collective-permute-start(bf16[256,2048]{1,0:T(8,128)(2,1)} %add_convert_fusion.4), channel_id=1, source_target_pairs={{0,2},{2,0},{1,3},{3,1},{4,6},{6,4},{5,7},{7,5},{8,10},{10,8},{9,1... | collective-permute-start | bytes 3145736 | tf_op jit(solution)/shard_map/ppermute | solution.py:661
  206.3 5.3 collective-permute-start.8
  208.1 268.4 %all-gather.20.cloned.1.call-start = ((), (), s32[]{:S(2)}) async-start(), calls=%async_computation.6 | async-start | bytes 2007040 | tf_op jit(solution)/shard_map/all_gather | solution.py:1029
  208.2 10.1 %collective-permute-start.16 = (bf16[256,2048]{1,0:T(8,128)(2,1)}, bf16[256,2048]{1,0:T(8,128)(2,1)S(1)}, u32[]{:S(2)}, u32[]{:S(2)}) collective-permute-start(bf16[256,2048]{1,0:T(8,128)(2,1)} %collective-permute-done.15), channel_id=1, source_target_pairs={{0,1},{1,0},{2,3},{3,2},{4,5},{5,4},{6,7},{7,6},{8,9},{9,8},{10,11... | collective-permute-start | bytes 3145736 | tf_op jit(solution)/shard_map/ppermute | solution.py:658
  210.1 24.5 %collective-permute-start.12 = (bf16[512,1024]{1,0:T(8,128)(2,1)S(1)}, bf16[512,1024]{1,0:T(8,128)(2,1)S(1)}, u32[]{:S(2)}, u32[]{:S(2)}) collective-permute-start(bf16[512,1024]{1,0:T(8,128)(2,1)S(1)} %get-tuple-element.271), channel_id=1, source_target_pairs={{0,4},{4,0},{8,12},{12,8},{16,20},{20,16},{24,28},{28,24},{1,5},{5... | collective-permute-start | bytes 3145736 | tf_op jit(solution)/shard_map/ppermute | solution.py:708
  211.3 45.6 %collective-permute-start.13 = (bf16[512,1024]{1,0:T(8,128)(2,1)S(1)}, bf16[512,1024]{1,0:T(8,128)(2,1)S(1)}, u32[]{:S(2)}, u32[]{:S(2)}) collective-permute-start(bf16[512,1024]{1,0:T(8,128)(2,1)S(1)} %get-tuple-element.270), channel_id=1, source_target_pairs={{0,4},{4,0},{8,12},{12,8},{16,20},{20,16},{24,28},{28,24},{1,5},{5... | collective-permute-start | bytes 3145736 | tf_op jit(solution)/shard_map/ppermute | solution.py:708
  217.1 40.8 %collective-permute-start.11 = (bf16[256,2048]{1,0:T(8,128)(2,1)S(1)}, bf16[256,2048]{1,0:T(8,128)(2,1)}, u32[]{:S(2)}, u32[]{:S(2)}) collective-permute-start(bf16[256,2048]{1,0:T(8,128)(2,1)S(1)} %get-tuple-element.266.refs_0_), channel_id=1, source_target_pairs={{0,2},{2,0},{1,3},{3,1},{4,6},{6,4},{5,7},{7,5},{8,10},{10,8},{9,1... | collective-permute-start | bytes 3145736 | tf_op jit(solution)/shard_map/ppermute | solution.py:661
  257.9 46.2 %collective-permute-start.18 = (bf16[1024,1024]{1,0:T(8,128)(2,1)}, bf16[1024,1024]{1,0:T(8,128)(2,1)}, u32[]{:S(2)}, u32[]{:S(2)}) collective-permute-start(bf16[1024,1024]{1,0:T(8,128)(2,1)} %all-gather.18.cloned.1.call-done.refs_7_), channel_id=1, source_target_pairs={{0,4},{4,0},{8,12},{12,8},{16,20},{20,16},{24,28},{28,24},{1,5},{5... | collective-permute-start | bytes 6291464 | tf_op jit(solution)/shard_map/ppermute | solution.py:714
  259.1 5.0 collective-permute-start.10
  260.8 4.4 collective-permute-start.17
  329.9 9.8 %collective-permute-start.19 = (bf16[256,2048]{1,0:T(8,128)(2,1)}, bf16[256,2048]{1,0:T(8,128)(2,1)S(1)}, u32[]{:S(2)}, u32[]{:S(2)}) collective-permute-start(bf16[256,2048]{1,0:T(8,128)(2,1)} %get-tuple-element.169), channel_id=1, source_target_pairs={{0,1},{1,0},{2,3},{3,2},{4,5},{5,4},{6,7},{7,6},{8,9},{9,8},{10,11... | collective-permute-start | bytes 3145736 | tf_op jit(solution)/shard_map/ppermute | solution.py:658
  342.4 24.9 %collective-permute-start.21 = (bf16[256,2048]{1,0:T(8,128)(2,1)}, bf16[256,2048]{1,0:T(8,128)(2,1)S(1)}, u32[]{:S(2)}, u32[]{:S(2)}) collective-permute-start(bf16[256,2048]{1,0:T(8,128)(2,1)} %add_convert_fusion.2), channel_id=1, source_target_pairs={{0,2},{2,0},{1,3},{3,1},{4,6},{6,4},{5,7},{7,5},{8,10},{10,8},{9,1... | collective-permute-start | bytes 3145736 | tf_op jit(solution)/shard_map/ppermute | solution.py:661
  367.3 3.5 collective-permute-start.22
  376.9 8.2 %collective-permute-start.24 = (bf16[256,2048]{1,0:T(8,128)(2,1)}, bf16[256,2048]{1,0:T(8,128)(2,1)}, u32[]{:S(2)}, u32[]{:S(2)}) collective-permute-start(bf16[256,2048]{1,0:T(8,128)(2,1)} %get-tuple-element.179.first), channel_id=1, source_target_pairs={{0,1},{1,0},{2,3},{3,2},{4,5},{5,4},{6,7},{7,6},{8,9},{9,8},{10,11... | collective-permute-start | bytes 3145736 | tf_op jit(solution)/shard_map/ppermute | solution.py:658
  378.4 24.9 %collective-permute-start.25 = (bf16[256,2048]{1,0:T(8,128)(2,1)}, bf16[256,2048]{1,0:T(8,128)(2,1)S(1)}, u32[]{:S(2)}, u32[]{:S(2)}) collective-permute-start(bf16[256,2048]{1,0:T(8,128)(2,1)} %get-tuple-element.179.first), channel_id=1, source_target_pairs={{0,2},{2,0},{1,3},{3,1},{4,6},{6,4},{5,7},{7,5},{8,10},{10,8},{9,1... | collective-permute-start | bytes 3145736 | tf_op jit(solution)/shard_map/ppermute | solution.py:661
  379.6 14.1 %collective-permute-start.23 = (bf16[256,2048]{1,0:T(8,128)(2,1)}, bf16[256,2048]{1,0:T(8,128)(2,1)}, u32[]{:S(2)}, u32[]{:S(2)}) collective-permute-start(bf16[256,2048]{1,0:T(8,128)(2,1)} %get-tuple-element.182), channel_id=1, source_target_pairs={{0,1},{1,0},{2,3},{3,2},{4,5},{5,4},{6,7},{7,6},{8,9},{9,8},{10,11... | collective-permute-start | bytes 3145736 | tf_op jit(solution)/shard_map/ppermute | solution.py:658
  403.2 3.7 collective-permute-start.26
  412.2 17.9 %collective-permute-start.29 = (bf16[48,512]{1,0:T(8,128)(2,1)S(1)}, bf16[48,512]{1,0:T(8,128)(2,1)S(1)}, u32[]{:S(2)}, u32[]{:S(2)}) collective-permute-start(bf16[48,512]{1,0:T(8,128)(2,1)S(1)} %add_convert_fusion.7), channel_id=1, source_target_pairs={{0,2},{2,0},{1,3},{3,1},{4,6},{6,4},{5,7},{7,5},{8,10},{10,8},{9,1... | collective-permute-start | bytes 147464 | tf_op jit(solution)/shard_map/ppermute | solution.py:661
  432.4 8.1 %collective-permute-start.30 = (bf16[16,6272]{1,0:T(8,128)(2,1)}, bf16[16,6272]{1,0:T(8,128)(2,1)S(1)}, u32[]{:S(2)}, u32[]{:S(2)}) collective-permute-start(bf16[16,6272]{1,0:T(8,128)(2,1)} %flatten.2), channel_id=1, source_target_pairs={{0,4},{4,0},{8,12},{12,8},{16,20},{20,16},{24,28},{28,24},{1,5},{5... | collective-permute-start | bytes 602120 | tf_op jit(solution)/shard_map/ppermute | solution.py:975
  441.3 24.2 %collective-permute-start.28 = (bf16[256,2048]{1,0:T(8,128)(2,1)S(1)}, bf16[256,2048]{1,0:T(8,128)(2,1)}, u32[]{:S(2)}, u32[]{:S(2)}) collective-permute-start(bf16[256,2048]{1,0:T(8,128)(2,1)S(1)} %copy-done.25), channel_id=1, source_target_pairs={{0,2},{2,0},{1,3},{3,1},{4,6},{6,4},{5,7},{7,5},{8,10},{10,8},{9,1... | collective-permute-start | bytes 3145736 | tf_op jit(solution)/shard_map/ppermute | solution.py:661
  474.6 5.3 collective-permute-start.33
  487.0 8.2 %collective-permute-start.34 = (bf16[256,2048]{1,0:T(8,128)(2,1)}, bf16[256,2048]{1,0:T(8,128)(2,1)}, u32[]{:S(2)}, u32[]{:S(2)}) collective-permute-start(bf16[256,2048]{1,0:T(8,128)(2,1)} %back_rows.4), channel_id=1, source_target_pairs={{0,1},{1,0},{2,3},{3,2},{4,5},{5,4},{6,7},{7,6},{8,9},{9,8},{10,11... | collective-permute-start | bytes 3145736 | tf_op jit(solution)/shard_map/ppermute | solution.py:658
  487.9 15.3 %collective-permute-start.20 = (bf16[256,2048]{1,0:T(8,128)(2,1)}, bf16[256,2048]{1,0:T(8,128)(2,1)S(1)}, u32[]{:S(2)}, u32[]{:S(2)}) collective-permute-start(bf16[256,2048]{1,0:T(8,128)(2,1)} %get-tuple-element.174), channel_id=1, source_target_pairs={{0,1},{1,0},{2,3},{3,2},{4,5},{5,4},{6,7},{7,6},{8,9},{9,8},{10,11... | collective-permute-start | bytes 3145736 | tf_op jit(solution)/shard_map/ppermute | solution.py:658
  487.9 10.2 %collective-permute-start.35 = (bf16[8,16,1536]{2,1,0:T(8,128)(2,1)S(1)}, bf16[8,16,1536]{2,1,0:T(8,128)(2,1)S(1)}, u32[]{:S(2)}, u32[]{:S(2)}) collective-permute-start(bf16[8,16,1536]{2,1,0:T(8,128)(2,1)S(1)} %bitcast.162), channel_id=1, source_target_pairs={{0,2},{2,0},{1,3},{3,1},{4,6},{6,4},{5,7},{7,5},{8,10},{10,8},{9,1... | collective-permute-start | bytes 1179656 | tf_op jit(solution)/shard_map/ppermute | solution.py:661
  498.1 29.3 %collective-permute-start.39 = (bf16[256,2048]{1,0:T(8,128)(2,1)}, bf16[256,2048]{1,0:T(8,128)(2,1)}, u32[]{:S(2)}, u32[]{:S(2)}) collective-permute-start(bf16[256,2048]{1,0:T(8,128)(2,1)} %add_convert_fusion), channel_id=1, source_target_pairs={{0,2},{2,0},{1,3},{3,1},{4,6},{6,4},{5,7},{7,5},{8,10},{10,8},{9,1... | collective-permute-start | bytes 3145736 | tf_op jit(solution)/shard_map/ppermute | solution.py:661
  499.2 9.4 %collective-permute-start.36 = (bf16[32,3200]{1,0:T(8,128)(2,1)S(1)}, bf16[32,3200]{1,0:T(8,128)(2,1)S(1)}, u32[]{:S(2)}, u32[]{:S(2)}) collective-permute-start(bf16[32,3200]{1,0:T(8,128)(2,1)S(1)} %pad_maximum_fusion.10.refs_0_), channel_id=1, source_target_pairs={{0,8},{4,12},{8,16},{12,20},{16,24},{20,28},{24,0},{28,4},{1,9},{5... | collective-permute-start | bytes 614408 | tf_op jit(solution)/shard_map/ppermute | solution.py:979
  499.7 15.2 %collective-permute-start.37 = (bf16[32,3200]{1,0:T(8,128)(2,1)S(1)}, bf16[32,3200]{1,0:T(8,128)(2,1)}, u32[]{:S(2)}, u32[]{:S(2)}) collective-permute-start(bf16[32,3200]{1,0:T(8,128)(2,1)S(1)} %pad_maximum_fusion.10.refs_0_), channel_id=1, source_target_pairs={{0,16},{4,20},{8,24},{12,28},{16,0},{20,4},{24,8},{28,12},{1,17},{... | collective-permute-start | bytes 614408 | tf_op jit(solution)/shard_map/ppermute | solution.py:979
  501.1 17.4 %collective-permute-start.38 = (bf16[32,3200]{1,0:T(8,128)(2,1)S(1)}, bf16[32,3200]{1,0:T(8,128)(2,1)}, u32[]{:S(2)}, u32[]{:S(2)}) collective-permute-start(bf16[32,3200]{1,0:T(8,128)(2,1)S(1)} %pad_maximum_fusion.10.refs_0_), channel_id=1, source_target_pairs={{0,24},{4,28},{8,0},{12,4},{16,8},{20,12},{24,16},{28,20},{1,25},{... | collective-permute-start | bytes 614408 | tf_op jit(solution)/shard_map/ppermute | solution.py:979
  527.4 13.2 %collective-permute-start.40 = (bf16[256,2048]{1,0:T(8,128)(2,1)}, bf16[256,2048]{1,0:T(8,128)(2,1)}, u32[]{:S(2)}, u32[]{:S(2)}) collective-permute-start(bf16[256,2048]{1,0:T(8,128)(2,1)} %back_rows.6), channel_id=1, source_target_pairs={{0,1},{1,0},{2,3},{3,2},{4,5},{5,4},{6,7},{7,6},{8,9},{9,8},{10,11... | collective-permute-start | bytes 3145736 | tf_op jit(solution)/shard_map/ppermute | solution.py:658
  533.1 3.5 collective-permute-start.44
  533.6 13.3 %collective-permute-start.41 = (bf16[8,16,1536]{2,1,0:T(8,128)(2,1)}, bf16[8,16,1536]{2,1,0:T(8,128)(2,1)}, u32[]{:S(2)}, u32[]{:S(2)}) collective-permute-start(bf16[8,16,1536]{2,1,0:T(8,128)(2,1)} %bitcast.164), channel_id=1, source_target_pairs={{0,1},{1,0},{2,3},{3,2},{4,5},{5,4},{6,7},{7,6},{8,9},{9,8},{10,11... | collective-permute-start | bytes 1179656 | tf_op jit(solution)/shard_map/ppermute | solution.py:658
  533.6 12.8 %collective-permute-start.42 = (bf16[8,16,1536]{2,1,0:T(8,128)(2,1)}, bf16[8,16,1536]{2,1,0:T(8,128)(2,1)}, u32[]{:S(2)}, u32[]{:S(2)}) collective-permute-start(bf16[8,16,1536]{2,1,0:T(8,128)(2,1)} %bitcast.165), channel_id=1, source_target_pairs={{0,2},{2,0},{1,3},{3,1},{4,6},{6,4},{5,7},{7,5},{8,10},{10,8},{9,1... | collective-permute-start | bytes 1179656 | tf_op jit(solution)/shard_map/ppermute | solution.py:661
  (101 other events, 1264.2 us)
Sparse Core Ops, SparseCore 0:
  10.2 45.3 all-gather.9
  57.7 44.4 all-gather.7
  104.3 44.4 all-gather.11
  150.3 44.4 all-gather.13
  196.2 44.4 all-gather.17
  242.7 79.2 all-gather.15
  441.4 35.0 all-gather.19

commit v5 on v4

--- a/solution.py
+++ b/solution.py
@@ -1040,10 +1040,6 @@
         + packed(3)
         + [((rank_width, width_local), F32)] * 3,
     )
-    late_parts[1] = after(late_parts[1], main_arrived)
-    late_base, late_near, late_far = settle_near(*late_parts)
-    late_chip = to_chip(late_far)
-
     def rows_back(first, count, *held):
         rank = after(grad_rank_one, *held) if held else grad_rank_one
         return back_rows(
@@ -1056,6 +1052,11 @@
             count,
         )
 
+    (back_third,) = rows_back(3, 1)
+    late_parts[1] = after(late_parts[1], main_arrived, back_third)
+    late_base, late_near, late_far = settle_near(*late_parts)
+    late_chip = to_chip(late_far)
+
     late_flat = settle_flat(
         late_base, late_near, late_chip, [delta_query_up, delta_key_up, delta_value_up]
     )
@@ -1069,9 +1070,8 @@
     )
     late_pair = jnp.concatenate([late_flat, after(late_other, early_own)], axis=0)
     late_trees = settle_line(late_pair)
-    (back_third,) = rows_back(3, 1, late_pair)
     back_core = to_core(back_third)
-    (back_second,) = rows_back(2, 1, back_third)
+    (back_second,) = rows_back(2, 1, late_pair)
     early_away = to_chip(early_own)
     back_far = (back_second.astype(F32) + back_core.astype(F32)).astype(BF)
     back_far = after(back_far, early_away)

time: 568 us -> 560 us (0.986)
  waiting for transfers between devices: 165 us -> 156 us
    ppermute x12, waiting for transfers between devices: 25.7 us -> 18.7 us  [to_chip(): return lax.ppermute(v, 'tensor', chip_pairs)]
    unnamed x195 -> x199, local copies, waits for them, and re-layouts: 15 us -> 15.1 us
  transfers between devices with their start and end apart: 53 -> 53, of which waited for: 21 -> 19; matrix products, arithmetic and copies ran while one was open for 18% -> 19% of each run, Pallas kernels for 32% -> 34%
where the time goes in v5:
time: 560 us; the launch traced here: 552 us
  Pallas kernels  208 us (37%)
  waiting for transfers between devices  156 us (28%)
  other arithmetic  49.7 us (9%)
  starting transfers between devices  48.3 us (9%)
  matrix products  46.6 us (8%)
  local copies, waits for them, and re-layouts  25.9 us (5%)
  between operations  17 us (3%)
    pallas_call x6, Pallas kernels, feed_forward(): pl.pallas_call(functools.partial(feed_kernel, first, last, len(weight)),...  80.7 us
    all_gather x6, waiting for transfers between devices, line_gather(): lax.all_gather(shard, 'dp', axis=0, tiled=True, axis_index_groups=line_gr...  77.2 us
    ppermute x3, waiting for transfers between devices, fetch_pieces(): lax.ppermute(own[k * size:(k + 1) * size], 'dp', dp_pairs)  45.5 us
    pallas_call x4, Pallas kernels, by_head(): pl.pallas_call(functools.partial(kernel, HEAD_DIM ** (-0.5)), grid_spec=p...  36.2 us
    pallas_call x4, Pallas kernels, back_rows(): pl.pallas_call(back_kernel, grid=(count,), in_specs=[pl.BlockSpec((tile,...  24.8 us
    ppermute x22, starting transfers between devices, to_core(): return lax.ppermute(v, 'tensor', core_pairs)  22.9 us
    pallas_call x5, Pallas kernels, local_call(): pl.pallas_call(kernel, in_specs=specs, out_specs=out_specs, out_shape=[ja...  21.2 us
    dot_general x7, matrix products, product(): return jnp.dot(left, right, preferred_element_type=F32)  21.1 us
  transfers between devices with their start and end apart: 53, of which 19 were waited for; matrix products, arithmetic and copies ran while one was open for 19% of the time, Pallas kernels for 34%

profile of v5, /device:TPU:17, one launch (start us, length us, event | category | flops | bytes accessed | tf_op | source)
XLA Modules:
  0.0 551.6 jit_solution(3559054562119085902)
XLA Ops:
  46.9 8.6 %all-gather.10.cloned.1.call-done.qk_own = bf16[1024,1024]{1,0:T(8,128)(2,1)} async-done(((bf16[256,1024]{1,0:T(8,128)(2,1)}), bf16[1024,1024]{1,0:T(8,128)(2,1)}) %all-gather.10.cloned.1.call-update) | async-done | bytes 2097168 | tf_op jit(solution)/shard_map/all_gather | solution.py:698
  60.3 41.9 %all-gather.8.cloned.1.call-done.own.vo_own = bf16[1024,1024]{1,0:T(8,128)(2,1)} async-done(((bf16[256,1024]{1,0:T(8,128)(2,1)}), bf16[1024,1024]{1,0:T(8,128)(2,1)}) %all-gather.8.cloned.1.call-update) | async-done | bytes 2097168 | tf_op jit(solution)/shard_map/all_gather | solution.py:698
  103.8 3.4 fusion.1.refs_12_.refs_16_
  110.2 4.9 fusion.23
  115.2 4.0 fusion.27
  122.6 26.2 %all-gather.12.cloned.1.call-done.refs_7_ = bf16[1024,1024]{1,0:T(8,128)(2,1)} async-done(((bf16[256,1024]{1,0:T(8,128)(2,1)}), bf16[1024,1024]{1,0:T(8,128)(2,1)}) %all-gather.12.cloned.1.call-update) | async-done | bytes 2097168 | tf_op jit(solution)/shard_map/all_gather | solution.py:698
  149.3 3.1 fusion.16.refs_4_.refs_5_.refs_6_.refs_7_
  153.6 3.7 fusion.19
  159.6 12.5 %attend.1 = (bf16[1024,512]{1,0:T(8,128)(2,1)}, f32[1024,512]{1,0:T(8,128)}) custom-call(s32[1]{0:T(128)} %bitcast.1.turn, bf16[1024,512]{1,0:T(8,128)(2,1)} %fusion.18.refs_0_.refs_1_.refs_2_.refs_3_, bf16[1024,512]{1,0:T(8,128)(2,1)} %fusion.18.refs_0_.refs_1_.refs_2_.refs_3_, bf16[1024,512]{1,0:T(8,128)(2,1)} %fusion.18.refs_0_.refs_1_.refs_2_.refs_3_, ...), custom_call_target="tpu_custom_call" | custom-call | flops 100000000 | bytes 1000000 | tf_op jit(solution)/shard_map/attend/pallas_call | solution.py:306
  172.1 7.3 %out_rows.2 = (bf16[256,2048]{1,0:T(8,128)(2,1)}, bf16[256,2048]{1,0:T(8,128)(2,1)}) custom-call(bf16[1024,512]{1,0:T(8,128)(2,1)} %get-tuple-element.145.rows, bf16[16,512]{1,0:T(8,128)(2,1)} %bitcast.133, bf16[16,2048]{1,0:T(8,128)(2,1)} %copy-done.24, bf16[1024,1024]{1,0:T(8,128)(2,1)} %all-gather.8.cloned.1.call-done.own.vo_own, ...), custom_call_target="tpu_custom_call" | custom-call | flops 10000000 | bytes 100000 | tf_op jit(solution)/shard_map/out_rows/pallas_call | solution.py:391
  186.7 12.3 %collective-permute-done.7.refs_8_ = bf16[1024,1024]{1,0:T(8,128)(2,1)} collective-permute-done((bf16[1024,1024]{1,0:T(8,128)(2,1)}, bf16[1024,1024]{1,0:T(8,128)(2,1)}, u32[]{:S(2)}, u32[]{:S(2)}) %collective-permute-start.7) | collective-permute-done | bytes 2097184 | tf_op jit(solution)/shard_map/ppermute | solution.py:708
  199.1 7.2 %out_rows.3 = (bf16[256,2048]{1,0:T(8,128)(2,1)}, bf16[256,2048]{1,0:T(8,128)(2,1)}) custom-call(bf16[1024,512]{1,0:T(8,128)(2,1)} %get-tuple-element.145.rows, bf16[16,512]{1,0:T(8,128)(2,1)} %bitcast.134, bf16[16,2048]{1,0:T(8,128)(2,1)} %copy-done.24, bf16[1024,1024]{1,0:T(8,128)(2,1)} %all-gather.8.cloned.1.call-done.own.vo_own, ...), custom_call_target="tpu_custom_call" | custom-call | flops 10000000 | bytes 100000 | tf_op jit(solution)/shard_map/out_rows/pallas_call | solution.py:391
  222.8 11.7 %collective-permute-done.12.refs_8_ = bf16[512,1024]{1,0:T(8,128)(2,1)S(1)} collective-permute-done((bf16[512,1024]{1,0:T(8,128)(2,1)S(1)}, bf16[512,1024]{1,0:T(8,128)(2,1)S(1)}, u32[]{:S(2)}, u32[]{:S(2)}) %collective-permute-start.12) | collective-permute-done | bytes 1048608 | tf_op jit(solution)/shard_map/ppermute | solution.py:708
  235.5 21.4 %collective-permute-done.13.refs_9_ = bf16[512,1024]{1,0:T(8,128)(2,1)S(1)} collective-permute-done((bf16[512,1024]{1,0:T(8,128)(2,1)S(1)}, bf16[512,1024]{1,0:T(8,128)(2,1)S(1)}, u32[]{:S(2)}, u32[]{:S(2)}) %collective-permute-start.13) | collective-permute-done | bytes 1048608 | tf_op jit(solution)/shard_map/ppermute | solution.py:708
  265.1 5.7 %join_rows.1 = (bf16[1024,2048]{1,0:T(8,128)(2,1)}, bf16[1024,16]{1,0:T(8,128)(2,1)}) custom-call(bf16[256,2048]{1,0:T(8,128)(2,1)} %copy-done.18, bf16[256,2048]{1,0:T(8,128)(2,1)} %copy-done.38, bf16[256,2048]{1,0:T(8,128)(2,1)} %collective-permute-done.11.refs_2_, bf16[256,2048]{1,0:T(8,128)(2,1)} %collective-permute-done.17.refs_3_, ...), custom_call_target="tpu_custom_call" | custom-call | flops 1000000 | bytes 100000 | tf_op jit(solution)/shard_map/join_rows/pallas_call | solution.py:57
  270.9 16.0 %feed_forward.6 = (bf16[1024,2048]{1,0:T(8,128)(2,1)}, bf16[1024,2048]{1,0:T(8,128)(2,1)}, f32[1024,16]{1,0:T(8,128)}, f32[1024,16]{1,0:T(8,128)}, f32[16,512]{1,0:T(8,128)}, /*index=5*/f32[16,512]{1,0:T(8,128)}) custom-call(bf16[1024,2048]{1,0:T(8,128)(2,1)} %get-tuple-element.171.refs_0_, bf16[1024,2048]{1,0:T(8,128)(2,1)} %copy-done.2, ...), custom_call_target="tpu_custom_call" | custom-call | flops 1073741824 | bytes 41943040 | tf_op jit(solution)/shard_map/feed_forward/pallas_call | solution.py:188
  286.8 17.2 %feed_forward.7 = (bf16[1024,2048]{1,0:T(8,128)(2,1)}, bf16[1024,2048]{1,0:T(8,128)(2,1)}, f32[1024,16]{1,0:T(8,128)}, f32[1024,16]{1,0:T(8,128)}, f32[16,512]{1,0:T(8,128)}, /*index=5*/f32[16,512]{1,0:T(8,128)}) custom-call(bf16[1024,2048]{1,0:T(8,128)(2,1)} %get-tuple-element.171.refs_0_, bf16[1024,2048]{1,0:T(8,128)(2,1)} %copy-done.2, ...), custom_call_target="tpu_custom_call" | custom-call | flops 1073741824 | bytes 41943040 | tf_op jit(solution)/shard_map/feed_forward/pallas_call | solution.py:188
  304.1 17.4 %feed_forward.8 = (bf16[1024,2048]{1,0:T(8,128)(2,1)}, bf16[1024,2048]{1,0:T(8,128)(2,1)}, f32[1024,16]{1,0:T(8,128)}, f32[1024,16]{1,0:T(8,128)}, f32[16,512]{1,0:T(8,128)}, /*index=5*/f32[16,512]{1,0:T(8,128)}) custom-call(bf16[1024,2048]{1,0:T(8,128)(2,1)} %get-tuple-element.171.refs_0_, bf16[1024,2048]{1,0:T(8,128)(2,1)} %copy-done.2, ...), custom_call_target="tpu_custom_call" | custom-call | flops 1073741824 | bytes 41943040 | tf_op jit(solution)/shard_map/feed_forward/pallas_call | solution.py:188
  321.9 8.0 %feed_forward.9 = (bf16[256,2048]{1,0:T(8,128)(2,1)}, bf16[256,2048]{1,0:T(8,128)(2,1)}, f32[256,16]{1,0:T(8,128)}, f32[256,16]{1,0:T(8,128)}, f32[16,512]{1,0:T(8,128)}, /*index=5*/f32[16,512]{1,0:T(8,128)}) custom-call(bf16[1024,2048]{1,0:T(8,128)(2,1)} %get-tuple-element.171.refs_0_, bf16[1024,2048]{1,0:T(8,128)(2,1)} %copy-done.2, ...), custom_call_target="tpu_custom_call" | custom-call | flops 268435456 | bytes 10485760 | tf_op jit(solution)/shard_map/feed_forward/pallas_call | solution.py:188
  331.8 8.0 %feed_forward.10 = (bf16[256,2048]{1,0:T(8,128)(2,1)}, bf16[256,2048]{1,0:T(8,128)(2,1)}, f32[256,16]{1,0:T(8,128)}, f32[256,16]{1,0:T(8,128)}, f32[16,512]{1,0:T(8,128)}, /*index=5*/f32[16,512]{1,0:T(8,128)}) custom-call(bf16[1024,2048]{1,0:T(8,128)(2,1)} %get-tuple-element.171.refs_0_, bf16[1024,2048]{1,0:T(8,128)(2,1)} %copy-done.2, ...), custom_call_target="tpu_custom_call" | custom-call | flops 268435456 | bytes 10485760 | tf_op jit(solution)/shard_map/feed_forward/pallas_call | solution.py:188
  339.8 2.6 add_convert_fusion.2
  343.6 14.0 %feed_forward.11 = (bf16[256,2048]{1,0:T(8,128)(2,1)}, bf16[256,2048]{1,0:T(8,128)(2,1)}, bf16[256,2048]{1,0:T(8,128)(2,1)}, bf16[256,2048]{1,0:T(8,128)(2,1)}, ...) custom-call(bf16[1024,2048]{1,0:T(8,128)(2,1)} %get-tuple-element.171.refs_0_, ...), custom_call_target="tpu_custom_call" | custom-call | flops 536870912 | bytes 20971520 | tf_op jit(solution)/shard_map/feed_forward/pallas_call | solution.py:188
  357.6 9.7 %collective-permute-done.21.far = bf16[256,2048]{1,0:T(8,128)(2,1)S(1)} collective-permute-done((bf16[256,2048]{1,0:T(8,128)(2,1)}, bf16[256,2048]{1,0:T(8,128)(2,1)S(1)}, u32[]{:S(2)}, u32[]{:S(2)}) %collective-permute-start.21) | collective-permute-done | bytes 1048608 | tf_op jit(solution)/shard_map/ppermute | solution.py:661
  370.9 6.0 %branch_rows.1 = (f32[256,2048]{1,0:T(8,128)}, bf16[256,2048]{1,0:T(8,128)(2,1)}) custom-call(bf16[256,2048]{1,0:T(8,128)(2,1)} %get-tuple-element.175.zero, bf16[256,2048]{1,0:T(8,128)(2,1)} %collective-permute-done.22.one, bf16[256,2048]{1,0:T(8,128)(2,1)} %copy-done.32, bf16[256,2048]{1,0:T(8,128)(2,1)} %constant_dynamic-update-slice_fusion.30.base, ...), custom_call_target="tpu_custom_call" | custom-call | flops 10000000 | bytes 1000000 | tf_op jit(solution)/shard_map/branch_rows/pallas_call | solution.py:340
  380.1 3.7 fusion.142.refs_1_
  385.1 4.9 in_rows.2
  393.8 2.6 add_convert_fusion.1
  396.5 6.8 %collective-permute-done.25.refs_4_.first = bf16[256,2048]{1,0:T(8,128)(2,1)S(1)} collective-permute-done((bf16[256,2048]{1,0:T(8,128)(2,1)}, bf16[256,2048]{1,0:T(8,128)(2,1)S(1)}, u32[]{:S(2)}, u32[]{:S(2)}) %collective-permute-start.25) | collective-permute-done | bytes 1048608 | tf_op jit(solution)/shard_map/ppermute | solution.py:661
  406.9 2.9 pack.1
  413.4 4.9 in_rows.3
  423.4 6.6 %attend_back.3 = (bf16[1024,512]{1,0:T(8,128)(2,1)}, bf16[1024,512]{1,0:T(8,128)(2,1)}, bf16[1024,512]{1,0:T(8,128)(2,1)}) custom-call(s32[1]{0:T(128)} %bitcast.1.turn, bf16[1024,512]{1,0:T(8,128)(2,1)} %fusion.18.refs_0_.refs_1_.refs_2_.refs_3_, bf16[1024,512]{1,0:T(8,128)(2,1)} %fusion.18.refs_0_.refs_1_.refs_2_.refs_3_, ...), custom_call_target="tpu_custom_call" | custom-call | flops 100000000 | bytes 1000000 | tf_op jit(solution)/shard_map/attend_back/pallas_call | solution.py:306
  433.5 6.9 %attend_back.4 = (bf16[1024,512]{1,0:T(8,128)(2,1)}, bf16[1024,512]{1,0:T(8,128)(2,1)}, bf16[1024,512]{1,0:T(8,128)(2,1)}) custom-call(s32[1]{0:T(128)} %bitcast.1.turn, bf16[1024,512]{1,0:T(8,128)(2,1)} %fusion.18.refs_0_.refs_1_.refs_2_.refs_3_, ...), custom_call_target="tpu_custom_call", output_to_operand_aliasing={{0}: (19, {}), {1}: (20, {}), {2}: (21, {})} | custom-call | flops 100000000 | bytes 1000000 | tf_op jit(solution)/shard_map/attend_back/pallas_call | solution.py:306
  441.6 10.2 %attend_back.5 = (bf16[1024,512]{1,0:T(8,128)(2,1)}, bf16[1024,512]{1,0:T(8,128)(2,1)}, bf16[1024,512]{1,0:T(8,128)(2,1)}) custom-call(s32[1]{0:T(128)} %bitcast.1.turn, bf16[1024,512]{1,0:T(8,128)(2,1)} %fusion.18.refs_0_.refs_1_.refs_2_.refs_3_, ...), custom_call_target="tpu_custom_call", output_to_operand_aliasing={{0}: (19, {}), {1}: (20, {}), {2}: (21, {})} | custom-call | flops 100000000 | bytes 1000000 | tf_op jit(solution)/shard_map/attend_back/pallas_call | solution.py:306
  451.8 7.5 %late_deltas.1 = (bf16[1024,48]{1,0:T(8,128)(2,1)}, bf16[48,512]{1,0:T(8,128)(2,1)}, bf16[96,512]{1,0:T(8,128)(2,1)}, bf16[48,512]{1,0:T(8,128)(2,1)}, f32[16,51...) custom-call(s32[2]{0:T(128)} %pad_add_fusion.place, bf16[1024,512]{1,0:T(8,128)(2,1)} %get-tuple-element.223.refs_0_.query, ...), custom_call_target="tpu_custom_call" | custom-call | flops 1000000 | bytes 100000 | tf_op jit(solution)/shard_map/late_deltas/pallas_call | solution.py:544
  459.3 6.2 %back_rows.4 = bf16[256,2048]{1,0:T(8,128)(2,1)} custom-call(bf16[1024,512]{1,0:T(8,128)(2,1)} %get-tuple-element.223.refs_0_.query, bf16[1024,512]{1,0:T(8,128)(2,1)} %get-tuple-element.224.refs_1_.key, bf16[1024,512]{1,0:T(8,128)(2,1)} %get-tuple-element.225.refs_2_.value, bf16[1024,48]{1,0:T(8,128)(2,1)} %get-tuple-element.243.rank, ...), custom_call_target="tpu_custom_call" | custom-call | flops 100000000 | bytes 1000000 | tf_op jit(solution)/shard_map/back_rows/pallas_call | solution.py:410
  476.5 3.4 sum_slots.2
  482.0 6.2 %back_rows.5 = bf16[256,2048]{1,0:T(8,128)(2,1)} custom-call(bf16[1024,512]{1,0:T(8,128)(2,1)} %get-tuple-element.223.refs_0_.query, bf16[1024,512]{1,0:T(8,128)(2,1)} %get-tuple-element.224.refs_1_.key, bf16[1024,512]{1,0:T(8,128)(2,1)} %get-tuple-element.225.refs_2_.value, bf16[1024,48]{1,0:T(8,128)(2,1)} %get-tuple-element.243.rank, ...), custom_call_target="tpu_custom_call" | custom-call | flops 100000000 | bytes 1000000 | tf_op jit(solution)/shard_map/back_rows/pallas_call | solution.py:410
  488.2 2.9 add_convert_fusion
  496.4 4.4 output.1
  500.8 6.2 %back_rows.6 = bf16[256,2048]{1,0:T(8,128)(2,1)} custom-call(bf16[1024,512]{1,0:T(8,128)(2,1)} %get-tuple-element.223.refs_0_.query, bf16[1024,512]{1,0:T(8,128)(2,1)} %get-tuple-element.224.refs_1_.key, bf16[1024,512]{1,0:T(8,128)(2,1)} %get-tuple-element.225.refs_2_.value, bf16[1024,48]{1,0:T(8,128)(2,1)} %get-tuple-element.243.rank, ...), custom_call_target="tpu_custom_call" | custom-call | flops 100000000 | bytes 1000000 | tf_op jit(solution)/shard_map/back_rows/pallas_call | solution.py:410
  507.1 3.2 collective-permute-done.38.refs_3_
  510.3 6.2 %back_rows.7 = bf16[256,2048]{1,0:T(8,128)(2,1)} custom-call(bf16[1024,512]{1,0:T(8,128)(2,1)} %get-tuple-element.223.refs_0_.query, bf16[1024,512]{1,0:T(8,128)(2,1)} %get-tuple-element.224.refs_1_.key, bf16[1024,512]{1,0:T(8,128)(2,1)} %get-tuple-element.225.refs_2_.value, bf16[1024,48]{1,0:T(8,128)(2,1)} %get-tuple-element.243.rank, ...), custom_call_target="tpu_custom_call" | custom-call | flops 100000000 | bytes 1000000 | tf_op jit(solution)/shard_map/back_rows/pallas_call | solution.py:410
  516.5 2.7 sum_slots.3
  519.3 5.8 %collective-permute-start.40 = (bf16[256,2048]{1,0:T(8,128)(2,1)}, bf16[256,2048]{1,0:T(8,128)(2,1)}, u32[]{:S(2)}, u32[]{:S(2)}) collective-permute-start(bf16[256,2048]{1,0:T(8,128)(2,1)} %back_rows.6), channel_id=1, source_target_pairs={{0,1},{1,0},{2,3},{3,2},{4,5},{5,4},{6,7},{7,6},{8,9},{9,8},{10,11... | collective-permute-start | bytes 3145736 | tf_op jit(solution)/shard_map/ppermute | solution.py:658
  529.5 3.2 across.2
  532.7 2.6 fusion.50
  535.3 2.7 fusion.13
  541.3 3.2 across.3
  (508 shorter events, 145.6 us)
Async XLA Ops:
  7.2 48.4 %all-gather.10.cloned.1.call-start = ((), (), s32[]{:S(2)}) async-start(), calls=%async_computation.1 | async-start | bytes 2621440 | tf_op jit(solution)/shard_map/all_gather | solution.py:698
  9.3 92.9 %all-gather.8.cloned.1.call-start = ((), (), s32[]{:S(2)}) async-start(), calls=%async_computation | async-start | bytes 2621440 | tf_op jit(solution)/shard_map/all_gather | solution.py:698
  12.1 24.5 %collective-permute-start.1 = (bf16[256,2048]{1,0:T(8,128)(2,1)S(1)}, bf16[256,2048]{1,0:T(8,128)(2,1)}, u32[]{:S(2)}, u32[]{:S(2)}) collective-permute-start(bf16[256,2048]{1,0:T(8,128)(2,1)S(1)} %fusion.8), channel_id=1, source_target_pairs={{0,2},{2,0},{1,3},{3,1},{4,6},{6,4},{5,7},{7,5},{8,10},{10,8},{9,1... | collective-permute-start | bytes 3145736 | tf_op jit(solution)/shard_map/ppermute | solution.py:661
  13.4 28.3 %collective-permute-start = (bf16[256,2048]{1,0:T(8,128)(2,1)S(1)}, bf16[256,2048]{1,0:T(8,128)(2,1)}, u32[]{:S(2)}, u32[]{:S(2)}) collective-permute-start(bf16[256,2048]{1,0:T(8,128)(2,1)S(1)} %fusion.8), channel_id=1, source_target_pairs={{0,1},{1,0},{2,3},{3,2},{4,5},{5,4},{6,7},{7,6},{8,9},{9,8},{10,11... | collective-permute-start | bytes 3145736 | tf_op jit(solution)/shard_map/ppermute | solution.py:658
  19.9 188.3 %collective-permute-start.15 = (bf16[256,2048]{1,0:T(8,128)(2,1)}, bf16[256,2048]{1,0:T(8,128)(2,1)}, u32[]{:S(2)}, u32[]{:S(2)}) collective-permute-start(bf16[256,2048]{1,0:T(8,128)(2,1)} %constant_dynamic-update-slice_fusion.30.base), channel_id=1, source_target_pairs={{0,2},{2,0},{1,3},{3,1},{4,6},{6,4},{5,7},{7,5},{8,10},{10,8},{9,1... | collective-permute-start | bytes 3145736 | tf_op jit(solution)/shard_map/ppermute | solution.py:661
  20.2 198.2 %collective-permute-start.14 = (bf16[256,2048]{1,0:T(8,128)(2,1)}, bf16[256,2048]{1,0:T(8,128)(2,1)}, u32[]{:S(2)}, u32[]{:S(2)}) collective-permute-start(bf16[256,2048]{1,0:T(8,128)(2,1)} %constant_dynamic-update-slice_fusion.30.base), channel_id=1, source_target_pairs={{0,1},{1,0},{2,3},{3,2},{4,5},{5,4},{6,7},{7,6},{8,9},{9,8},{10,11... | collective-permute-start | bytes 3145736 | tf_op jit(solution)/shard_map/ppermute | solution.py:658
  25.1 14.4 %collective-permute-start.4 = (bf16[256,1024]{1,0:T(8,128)(2,1)}, bf16[256,1024]{1,0:T(8,128)(2,1)}, u32[]{:S(2)}, u32[]{:S(2)}) collective-permute-start(bf16[256,1024]{1,0:T(8,128)(2,1)} %pad_maximum_fusion.6), channel_id=1, source_target_pairs={{0,4},{4,0},{8,12},{12,8},{16,20},{20,16},{24,28},{28,24},{1,5},{5... | collective-permute-start | bytes 1572872 | tf_op jit(solution)/shard_map/ppermute | solution.py:751
  29.3 119.5 %all-gather.12.cloned.1.call-start = ((), (), s32[]{:S(2)}) async-start(), calls=%async_computation.2 | async-start | bytes 2621440 | tf_op jit(solution)/shard_map/all_gather | solution.py:698
  36.7 5.1 collective-permute-start.2
  55.6 152.5 %all-gather.14.cloned.1.call-start = ((), (), s32[]{:S(2)}) async-start(), calls=%async_computation.3 | async-start | bytes 2621440 | tf_op jit(solution)/shard_map/all_gather | solution.py:698
  58.4 51.8 %collective-permute-start.3 = (bf16[1024,1024]{1,0:T(8,128)(2,1)}, bf16[1024,1024]{1,0:T(8,128)(2,1)}, u32[]{:S(2)}, u32[]{:S(2)}) collective-permute-start(bf16[1024,1024]{1,0:T(8,128)(2,1)} %all-gather.10.cloned.1.call-done.qk_own), channel_id=1, source_target_pairs={{0,4},{4,0},{8,12},{12,8},{16,20},{20,16},{24,28},{28,24},{1,5},{5... | collective-permute-start | bytes 6291464 | tf_op jit(solution)/shard_map/ppermute | solution.py:702
  102.2 155.6 %all-gather.18.cloned.1.call-start = ((), (), s32[]{:S(2)}) async-start(), calls=%async_computation.5 | async-start | bytes 2621440 | tf_op jit(solution)/shard_map/all_gather | solution.py:698
  107.2 46.5 %collective-permute-start.5 = (bf16[1024,1024]{1,0:T(8,128)(2,1)S(1)}, bf16[1024,1024]{1,0:T(8,128)(2,1)}, u32[]{:S(2)}, u32[]{:S(2)}) collective-permute-start(bf16[1024,1024]{1,0:T(8,128)(2,1)S(1)} %copy-done.5), channel_id=1, source_target_pairs={{0,4},{4,0},{8,12},{12,8},{16,20},{20,16},{24,28},{28,24},{1,5},{5... | collective-permute-start | bytes 6291464 | tf_op jit(solution)/shard_map/ppermute | solution.py:702
  148.9 173.1 %all-gather.16.cloned.1.call-start = ((), (), s32[]{:S(2)}) async-start(), calls=%async_computation.4 | async-start | bytes 5242880 | tf_op jit(solution)/shard_map/all_gather | solution.py:698
  152.4 46.7 %collective-permute-start.7 = (bf16[1024,1024]{1,0:T(8,128)(2,1)}, bf16[1024,1024]{1,0:T(8,128)(2,1)}, u32[]{:S(2)}, u32[]{:S(2)}) collective-permute-start(bf16[1024,1024]{1,0:T(8,128)(2,1)} %all-gather.12.cloned.1.call-done.refs_7_), channel_id=1, source_target_pairs={{0,4},{4,0},{8,12},{12,8},{16,20},{20,16},{24,28},{28,24},{1,5},{5... | collective-permute-start | bytes 6291464 | tf_op jit(solution)/shard_map/ppermute | solution.py:708
  179.4 3.6 collective-permute-start.6
  185.6 25.8 %collective-permute-start.9 = (bf16[256,2048]{1,0:T(8,128)(2,1)}, bf16[256,2048]{1,0:T(8,128)(2,1)S(1)}, u32[]{:S(2)}, u32[]{:S(2)}) collective-permute-start(bf16[256,2048]{1,0:T(8,128)(2,1)} %add_convert_fusion.4), channel_id=1, source_target_pairs={{0,2},{2,0},{1,3},{3,1},{4,6},{6,4},{5,7},{7,5},{8,10},{10,8},{9,1... | collective-permute-start | bytes 3145736 | tf_op jit(solution)/shard_map/ppermute | solution.py:661
  206.3 5.3 collective-permute-start.8
  208.1 268.4 %all-gather.20.cloned.1.call-start = ((), (), s32[]{:S(2)}) async-start(), calls=%async_computation.6 | async-start | bytes 2007040 | tf_op jit(solution)/shard_map/all_gather | solution.py:1029
  208.2 10.1 %collective-permute-start.16 = (bf16[256,2048]{1,0:T(8,128)(2,1)}, bf16[256,2048]{1,0:T(8,128)(2,1)S(1)}, u32[]{:S(2)}, u32[]{:S(2)}) collective-permute-start(bf16[256,2048]{1,0:T(8,128)(2,1)} %collective-permute-done.15), channel_id=1, source_target_pairs={{0,1},{1,0},{2,3},{3,2},{4,5},{5,4},{6,7},{7,6},{8,9},{9,8},{10,11... | collective-permute-start | bytes 3145736 | tf_op jit(solution)/shard_map/ppermute | solution.py:658
  210.1 24.5 %collective-permute-start.12 = (bf16[512,1024]{1,0:T(8,128)(2,1)S(1)}, bf16[512,1024]{1,0:T(8,128)(2,1)S(1)}, u32[]{:S(2)}, u32[]{:S(2)}) collective-permute-start(bf16[512,1024]{1,0:T(8,128)(2,1)S(1)} %get-tuple-element.269), channel_id=1, source_target_pairs={{0,4},{4,0},{8,12},{12,8},{16,20},{20,16},{24,28},{28,24},{1,5},{5... | collective-permute-start | bytes 3145736 | tf_op jit(solution)/shard_map/ppermute | solution.py:708
  211.3 45.6 %collective-permute-start.13 = (bf16[512,1024]{1,0:T(8,128)(2,1)S(1)}, bf16[512,1024]{1,0:T(8,128)(2,1)S(1)}, u32[]{:S(2)}, u32[]{:S(2)}) collective-permute-start(bf16[512,1024]{1,0:T(8,128)(2,1)S(1)} %get-tuple-element.268), channel_id=1, source_target_pairs={{0,4},{4,0},{8,12},{12,8},{16,20},{20,16},{24,28},{28,24},{1,5},{5... | collective-permute-start | bytes 3145736 | tf_op jit(solution)/shard_map/ppermute | solution.py:708
  217.1 40.8 %collective-permute-start.11 = (bf16[256,2048]{1,0:T(8,128)(2,1)S(1)}, bf16[256,2048]{1,0:T(8,128)(2,1)}, u32[]{:S(2)}, u32[]{:S(2)}) collective-permute-start(bf16[256,2048]{1,0:T(8,128)(2,1)S(1)} %get-tuple-element.264.refs_0_), channel_id=1, source_target_pairs={{0,2},{2,0},{1,3},{3,1},{4,6},{6,4},{5,7},{7,5},{8,10},{10,8},{9,1... | collective-permute-start | bytes 3145736 | tf_op jit(solution)/shard_map/ppermute | solution.py:661
  257.9 46.2 %collective-permute-start.18 = (bf16[1024,1024]{1,0:T(8,128)(2,1)}, bf16[1024,1024]{1,0:T(8,128)(2,1)}, u32[]{:S(2)}, u32[]{:S(2)}) collective-permute-start(bf16[1024,1024]{1,0:T(8,128)(2,1)} %all-gather.18.cloned.1.call-done.refs_7_), channel_id=1, source_target_pairs={{0,4},{4,0},{8,12},{12,8},{16,20},{20,16},{24,28},{28,24},{1,5},{5... | collective-permute-start | bytes 6291464 | tf_op jit(solution)/shard_map/ppermute | solution.py:714
  259.1 5.0 collective-permute-start.10
  260.8 4.4 collective-permute-start.17
  329.9 9.8 %collective-permute-start.19 = (bf16[256,2048]{1,0:T(8,128)(2,1)}, bf16[256,2048]{1,0:T(8,128)(2,1)S(1)}, u32[]{:S(2)}, u32[]{:S(2)}) collective-permute-start(bf16[256,2048]{1,0:T(8,128)(2,1)} %get-tuple-element.168), channel_id=1, source_target_pairs={{0,1},{1,0},{2,3},{3,2},{4,5},{5,4},{6,7},{7,6},{8,9},{9,8},{10,11... | collective-permute-start | bytes 3145736 | tf_op jit(solution)/shard_map/ppermute | solution.py:658
  342.4 24.9 %collective-permute-start.21 = (bf16[256,2048]{1,0:T(8,128)(2,1)}, bf16[256,2048]{1,0:T(8,128)(2,1)S(1)}, u32[]{:S(2)}, u32[]{:S(2)}) collective-permute-start(bf16[256,2048]{1,0:T(8,128)(2,1)} %add_convert_fusion.2), channel_id=1, source_target_pairs={{0,2},{2,0},{1,3},{3,1},{4,6},{6,4},{5,7},{7,5},{8,10},{10,8},{9,1... | collective-permute-start | bytes 3145736 | tf_op jit(solution)/shard_map/ppermute | solution.py:661
  367.3 3.5 collective-permute-start.22
  376.9 8.2 %collective-permute-start.24 = (bf16[256,2048]{1,0:T(8,128)(2,1)}, bf16[256,2048]{1,0:T(8,128)(2,1)}, u32[]{:S(2)}, u32[]{:S(2)}) collective-permute-start(bf16[256,2048]{1,0:T(8,128)(2,1)} %get-tuple-element.178.first), channel_id=1, source_target_pairs={{0,1},{1,0},{2,3},{3,2},{4,5},{5,4},{6,7},{7,6},{8,9},{9,8},{10,11... | collective-permute-start | bytes 3145736 | tf_op jit(solution)/shard_map/ppermute | solution.py:658
  378.4 24.9 %collective-permute-start.25 = (bf16[256,2048]{1,0:T(8,128)(2,1)}, bf16[256,2048]{1,0:T(8,128)(2,1)S(1)}, u32[]{:S(2)}, u32[]{:S(2)}) collective-permute-start(bf16[256,2048]{1,0:T(8,128)(2,1)} %get-tuple-element.178.first), channel_id=1, source_target_pairs={{0,2},{2,0},{1,3},{3,1},{4,6},{6,4},{5,7},{7,5},{8,10},{10,8},{9,1... | collective-permute-start | bytes 3145736 | tf_op jit(solution)/shard_map/ppermute | solution.py:661
  379.7 14.1 %collective-permute-start.23 = (bf16[256,2048]{1,0:T(8,128)(2,1)}, bf16[256,2048]{1,0:T(8,128)(2,1)}, u32[]{:S(2)}, u32[]{:S(2)}) collective-permute-start(bf16[256,2048]{1,0:T(8,128)(2,1)} %get-tuple-element.181), channel_id=1, source_target_pairs={{0,1},{1,0},{2,3},{3,2},{4,5},{5,4},{6,7},{7,6},{8,9},{9,8},{10,11... | collective-permute-start | bytes 3145736 | tf_op jit(solution)/shard_map/ppermute | solution.py:658
  403.3 3.6 collective-permute-start.26
  412.1 17.9 %collective-permute-start.29 = (bf16[48,512]{1,0:T(8,128)(2,1)S(1)}, bf16[48,512]{1,0:T(8,128)(2,1)S(1)}, u32[]{:S(2)}, u32[]{:S(2)}) collective-permute-start(bf16[48,512]{1,0:T(8,128)(2,1)S(1)} %add_convert_fusion.7), channel_id=1, source_target_pairs={{0,2},{2,0},{1,3},{3,1},{4,6},{6,4},{5,7},{7,5},{8,10},{10,8},{9,1... | collective-permute-start | bytes 147464 | tf_op jit(solution)/shard_map/ppermute | solution.py:661
  432.3 8.1 %collective-permute-start.30 = (bf16[16,6272]{1,0:T(8,128)(2,1)}, bf16[16,6272]{1,0:T(8,128)(2,1)S(1)}, u32[]{:S(2)}, u32[]{:S(2)}) collective-permute-start(bf16[16,6272]{1,0:T(8,128)(2,1)} %flatten.2), channel_id=1, source_target_pairs={{0,4},{4,0},{8,12},{12,8},{16,20},{20,16},{24,28},{28,24},{1,5},{5... | collective-permute-start | bytes 602120 | tf_op jit(solution)/shard_map/ppermute | solution.py:975
  441.2 25.3 %collective-permute-start.28 = (bf16[256,2048]{1,0:T(8,128)(2,1)S(1)}, bf16[256,2048]{1,0:T(8,128)(2,1)}, u32[]{:S(2)}, u32[]{:S(2)}) collective-permute-start(bf16[256,2048]{1,0:T(8,128)(2,1)S(1)} %copy-done.25), channel_id=1, source_target_pairs={{0,2},{2,0},{1,3},{3,1},{4,6},{6,4},{5,7},{7,5},{8,10},{10,8},{9,1... | collective-permute-start | bytes 3145736 | tf_op jit(solution)/shard_map/ppermute | solution.py:661
  465.5 22.7 %collective-permute-start.34 = (bf16[256,2048]{1,0:T(8,128)(2,1)}, bf16[256,2048]{1,0:T(8,128)(2,1)}, u32[]{:S(2)}, u32[]{:S(2)}) collective-permute-start(bf16[256,2048]{1,0:T(8,128)(2,1)} %back_rows.4), channel_id=1, source_target_pairs={{0,1},{1,0},{2,3},{3,2},{4,5},{5,4},{6,7},{7,6},{8,9},{9,8},{10,11... | collective-permute-start | bytes 3145736 | tf_op jit(solution)/shard_map/ppermute | solution.py:658
  474.7 6.3 %collective-permute-start.33 = (bf16[16,3200]{1,0:T(8,128)(2,1)}, bf16[16,3200]{1,0:T(8,128)(2,1)S(1)}, u32[]{:S(2)}, u32[]{:S(2)}) collective-permute-start(bf16[16,3200]{1,0:T(8,128)(2,1)} %flatten.3), channel_id=1, source_target_pairs={{0,4},{4,0},{8,12},{12,8},{16,20},{20,16},{24,28},{28,24},{1,5},{5... | collective-permute-start | bytes 307208 | tf_op jit(solution)/shard_map/ppermute | solution.py:1063
  474.7 20.7 %collective-permute-start.20 = (bf16[256,2048]{1,0:T(8,128)(2,1)}, bf16[256,2048]{1,0:T(8,128)(2,1)S(1)}, u32[]{:S(2)}, u32[]{:S(2)}) collective-permute-start(bf16[256,2048]{1,0:T(8,128)(2,1)} %get-tuple-element.173), channel_id=1, source_target_pairs={{0,1},{1,0},{2,3},{3,2},{4,5},{5,4},{6,7},{7,6},{8,9},{9,8},{10,11... | collective-permute-start | bytes 3145736 | tf_op jit(solution)/shard_map/ppermute | solution.py:658
  479.9 11.2 %collective-permute-start.35 = (bf16[8,16,1536]{2,1,0:T(8,128)(2,1)}, bf16[8,16,1536]{2,1,0:T(8,128)(2,1)S(1)}, u32[]{:S(2)}, u32[]{:S(2)}) collective-permute-start(bf16[8,16,1536]{2,1,0:T(8,128)(2,1)} %bitcast.162), channel_id=1, source_target_pairs={{0,2},{2,0},{1,3},{3,1},{4,6},{6,4},{5,7},{7,5},{8,10},{10,8},{9,1... | collective-permute-start | bytes 1179656 | tf_op jit(solution)/shard_map/ppermute | solution.py:661
  491.1 28.2 %collective-permute-start.39 = (bf16[256,2048]{1,0:T(8,128)(2,1)}, bf16[256,2048]{1,0:T(8,128)(2,1)}, u32[]{:S(2)}, u32[]{:S(2)}) collective-permute-start(bf16[256,2048]{1,0:T(8,128)(2,1)} %add_convert_fusion), channel_id=1, source_target_pairs={{0,2},{2,0},{1,3},{3,1},{4,6},{6,4},{5,7},{7,5},{8,10},{10,8},{9,1... | collective-permute-start | bytes 3145736 | tf_op jit(solution)/shard_map/ppermute | solution.py:661
  491.4 9.4 %collective-permute-start.36 = (bf16[32,3200]{1,0:T(8,128)(2,1)S(1)}, bf16[32,3200]{1,0:T(8,128)(2,1)S(1)}, u32[]{:S(2)}, u32[]{:S(2)}) collective-permute-start(bf16[32,3200]{1,0:T(8,128)(2,1)S(1)} %pad_maximum_fusion.10.refs_0_), channel_id=1, source_target_pairs={{0,8},{4,12},{8,16},{12,20},{16,24},{20,28},{24,0},{28,4},{1,9},{5... | collective-permute-start | bytes 614408 | tf_op jit(solution)/shard_map/ppermute | solution.py:979
  492.4 14.7 %collective-permute-start.37 = (bf16[32,3200]{1,0:T(8,128)(2,1)S(1)}, bf16[32,3200]{1,0:T(8,128)(2,1)}, u32[]{:S(2)}, u32[]{:S(2)}) collective-permute-start(bf16[32,3200]{1,0:T(8,128)(2,1)S(1)} %pad_maximum_fusion.10.refs_0_), channel_id=1, source_target_pairs={{0,16},{4,20},{8,24},{12,28},{16,0},{20,4},{24,8},{28,12},{1,17},{... | collective-permute-start | bytes 614408 | tf_op jit(solution)/shard_map/ppermute | solution.py:979
  493.1 17.2 %collective-permute-start.38 = (bf16[32,3200]{1,0:T(8,128)(2,1)S(1)}, bf16[32,3200]{1,0:T(8,128)(2,1)}, u32[]{:S(2)}, u32[]{:S(2)}) collective-permute-start(bf16[32,3200]{1,0:T(8,128)(2,1)S(1)} %pad_maximum_fusion.10.refs_0_), channel_id=1, source_target_pairs={{0,24},{4,28},{8,0},{12,4},{16,8},{20,12},{24,16},{28,20},{1,25},{... | collective-permute-start | bytes 614408 | tf_op jit(solution)/shard_map/ppermute | solution.py:979
  519.3 13.4 %collective-permute-start.40 = (bf16[256,2048]{1,0:T(8,128)(2,1)}, bf16[256,2048]{1,0:T(8,128)(2,1)}, u32[]{:S(2)}, u32[]{:S(2)}) collective-permute-start(bf16[256,2048]{1,0:T(8,128)(2,1)} %back_rows.6), channel_id=1, source_target_pairs={{0,1},{1,0},{2,3},{3,2},{4,5},{5,4},{6,7},{7,6},{8,9},{9,8},{10,11... | collective-permute-start | bytes 3145736 | tf_op jit(solution)/shard_map/ppermute | solution.py:658
  525.2 3.5 collective-permute-start.44
  525.6 13.3 %collective-permute-start.41 = (bf16[8,16,1536]{2,1,0:T(8,128)(2,1)}, bf16[8,16,1536]{2,1,0:T(8,128)(2,1)}, u32[]{:S(2)}, u32[]{:S(2)}) collective-permute-start(bf16[8,16,1536]{2,1,0:T(8,128)(2,1)} %bitcast.165), channel_id=1, source_target_pairs={{0,1},{1,0},{2,3},{3,2},{4,5},{5,4},{6,7},{7,6},{8,9},{9,8},{10,11... | collective-permute-start | bytes 1179656 | tf_op jit(solution)/shard_map/ppermute | solution.py:658
  525.7 12.8 %collective-permute-start.42 = (bf16[8,16,1536]{2,1,0:T(8,128)(2,1)}, bf16[8,16,1536]{2,1,0:T(8,128)(2,1)}, u32[]{:S(2)}, u32[]{:S(2)}) collective-permute-start(bf16[8,16,1536]{2,1,0:T(8,128)(2,1)} %bitcast.166), channel_id=1, source_target_pairs={{0,2},{2,0},{1,3},{3,1},{4,6},{6,4},{5,7},{7,5},{8,10},{10,8},{9,1... | collective-permute-start | bytes 1179656 | tf_op jit(solution)/shard_map/ppermute | solution.py:661
  (103 other events, 1281.7 us)
Sparse Core Ops, SparseCore 0:
  10.2 45.3 all-gather.9
  57.7 44.4 all-gather.7
  104.3 44.4 all-gather.11
  150.3 44.4 all-gather.13
  196.2 44.4 all-gather.17
  242.7 79.2 all-gather.15
  441.3 35.1 all-gather.19
